TPU v7x, 32 devices: a whole 2x2x4 slice. The times are simulated.
32 devices in a mesh: dp: 4 (over x, core), expert: 8 (over z, y).
Axes of the slice: x: 2, y: 2, z: 4, core: 2. Of those that a mesh axis runs over, the one named last changes fastest.
Arguments:
- hidden_in: bfloat16 [8192, 2, 768], P(('dp', 'expert')), may hold values from -6 to 6
- cotangent: bfloat16 [8192, 2, 768], P(('dp', 'expert')), may hold values from -6 to 6
- gate_residual: float32 [8192, 2, 12], P(('dp', 'expert')), may hold values from -6 to 6
- routes: int32 [8192, 2, 2], P(('dp', 'expert')), may hold values from 0 to 11, all different within a row; in each aligned block of 512 rows (0 to 511, 512 to 1023, ..., all dimensions but the last counted through in order) at most 128 rows name the same one
- groups: int32 [32], P('dp'), may hold values from 0 to 0, as said below
- lengths: int32 [32], P('dp'), may hold values from 1 to 256, 6144 in all
- attn_gain: bfloat16 [768], P(('dp', 'expert')), may hold values from 0.5 to 1.5
- qkv_weight: bfloat16 [768, 2304], P(('dp', 'expert')), may hold values from -0.21875 to 0.21875
- out_weight: bfloat16 [768, 768], P(('dp', 'expert')), may hold values from -1.75 to 1.75
- ffn_gain: bfloat16 [768], P(('dp', 'expert')), may hold values from 0.5 to 1.5
- router_weight: bfloat16 [768, 12], P(('dp', 'expert')), may hold values from -0.21875 to 0.21875
- const_proj: bfloat16 [768, 4], P(('dp', 'expert')), may hold values from -0.21875 to 0.21875
- const_vec: bfloat16 [768, 2], P(('dp', 'expert')), may hold values from -6 to 6
- gate_weight: bfloat16 [768, 16384], P('dp', 'expert'), may hold values from -0.21875 to 0.21875
- up_weight: bfloat16 [768, 16384], P('dp', 'expert'), may hold values from -0.21875 to 0.21875
- down_weight: bfloat16 [768, 16384], P('dp', 'expert'), may hold values from -0.375 to 0.375
Outputs:
- output: bfloat16 [8192, 2, 768], P(('dp', 'expert'))
- grad_input: float32 [8192, 2, 768], P(('dp', 'expert'))
- grad_gate_residual: float32 [8192, 2, 12], P(('dp', 'expert'))
- grad_attn_gain: float32 [768], P(('dp', 'expert'))
- grad_qkv_weight: float32 [768, 2304], P(('dp', 'expert'))
- grad_out_weight: float32 [768, 768], P(('dp', 'expert'))
- grad_ffn_gain: float32 [768], P(('dp', 'expert'))
- grad_router_weight: float32 [768, 12], P(('dp', 'expert'))
- grad_const_proj: float32 [768, 4], P(('dp', 'expert'))
- grad_const_vec: float32 [768, 2], P(('dp', 'expert'))
- grad_gate_weight: float32 [768, 16384], P('dp', 'expert')
- grad_up_weight: float32 [768, 16384], P('dp', 'expert')
- grad_down_weight: float32 [768, 16384], P('dp', 'expert')
Inputs may be any that keep to these rules, and one draw needn't show every extreme that they name: `routes`: among the 512 rows of one device (aligned blocks of 256 first-dimension indices), no number is named by more than 128 rows; each row names two different numbers; number 8 is the zero expert, 9 the copy expert, 10 and 11 the constant experts. `groups`: in each aligned block of 8 continuations (one index of dp) every prompt number is named by exactly 8 of them.
All inputs are finite; a program needn't handle non-finite values. No bound on the sum of `lengths` on one device may be relied on, other than what follows from the above.
Results may differ from a plain program's by a relative error of at most 0.022.
Values may be sent and summed in bfloat16 or wider, within the bound.
No kernel may reach another device: no remote copies, remote signals or barrier semaphores. Data moves between devices by JAX's collectives and lax.ppermute only.
A program may use at most 256 MiB of HBM per device.

v0:
```python
import functools

import jax
import jax.numpy as jnp
from jax import lax
from jax.experimental import pallas as pl
from jax.experimental.pallas import tpu as pltpu
from jax.sharding import PartitionSpec as P


D = 768
HEAD_DIM = 64
PAIRS = 6
EXPERTS = 8
CONT_LEN = 256
PROMPT = 2048
LANES = 128
ROW_TILE = 512
EPS = 1e-06
NEG = -1e30
LOG2E = 1.4426950408889634
SCALE = float(HEAD_DIM) ** (-0.5)
LC = SCALE * LOG2E
F32 = jnp.float32
BF16 = jnp.bfloat16
ALL_AXES = ("dp", "expert")
VMEM_LIMIT = 60 * 1024 * 1024


def dot(a, b):
    return jnp.dot(a, b, preferred_element_type=F32)


def dot_nt(a, b):
    return lax.dot_general(a, b, (((1,), (1,)), ((), ())), preferred_element_type=F32)


def split_hi_lo(v):
    hi = v.astype(BF16)
    return hi, (v - hi.astype(F32)).astype(BF16)


def params(cost=None):
    return dict(
        compiler_params=pltpu.CompilerParams(vmem_limit_bytes=VMEM_LIMIT),
        cost_estimate=None if cost is None else pl.CostEstimate(
            flops=int(cost[0]), bytes_accessed=int(cost[1]), transcendentals=0
        ),
    )


def shape(dims, dtype):
    return jax.ShapeDtypeStruct(tuple(dims), dtype)


def spec(block, index):
    return pl.BlockSpec(tuple(block), index)


def whole(dims):
    return pl.BlockSpec(tuple(dims), lambda *_: (0,) * len(dims))


SMEM_SPEC = pl.BlockSpec(memory_space=pltpu.SMEM)


def partner(v):
    lane = lax.broadcasted_iota(jnp.int32, v.shape, 1)
    return jnp.where((lane & 63) < 32, pltpu.roll(v, 96, 1), pltpu.roll(v, 32, 1))


def qkv_body(x_ref, gain_ref, wq_ref, wk_ref, wv_ref, c_ref, s_ref, n_ref, q_ref, qt_ref, kvp_ref, kvc_ref):
    @pl.when(pl.program_id(0) == 0)
    def _():
        x = x_ref[...].astype(F32)
        scale = lax.rsqrt(jnp.mean(x * x, axis=-1, keepdims=True) + EPS)
        n_ref[...] = (x * scale * gain_ref[...]).astype(BF16)

    n = n_ref[...]
    cosine = c_ref[...]
    sine = s_ref[...]
    kv = dot(n, jnp.concatenate([wk_ref[...], wv_ref[...]], axis=1))
    k = kv[:, :LANES]
    k = (k * cosine + partner(k) * sine).astype(BF16)
    v = kv[:, LANES:].astype(BF16)
    r = k.shape[0] // 2
    kvp_ref[:, :LANES] = k[:r]
    kvp_ref[:, LANES:] = v[:r]
    kvc_ref[:, :LANES] = k[r:]
    kvc_ref[:, LANES:] = v[r:]
    q = dot(n, wq_ref[...])
    q = q * cosine + partner(q) * sine
    q_ref[...] = q.astype(BF16)
    qt_ref[...] = q.T.astype(BF16)


def qkv_call(x, gain, pack, cosine, sine):
    t = x.shape[0]
    return pl.pallas_call(
        qkv_body,
        grid=(PAIRS,),
        in_specs=[
            whole((t, D)),
            whole((1, D)),
            spec((D, LANES), lambda i: (0, i)),
            spec((D, LANES), lambda i: (0, PAIRS + i)),
            spec((D, LANES), lambda i: (0, 2 * PAIRS + i)),
            whole((t, LANES)),
            whole((t, LANES)),
        ],
        out_specs=[
            whole((t, D)),
            spec((t, LANES), lambda i: (0, i)),
            spec((LANES, t), lambda i: (i, 0)),
            spec((t // 2, 2 * LANES), lambda i: (0, i)),
            spec((t // 2, 2 * LANES), lambda i: (0, i)),
        ],
        out_shape=[
            shape((t, D), BF16),
            shape((t, D), BF16),
            shape((D, t), BF16),
            shape((t // 2, 2 * D), BF16),
            shape((t // 2, 2 * D), BF16),
        ],
        name="qkv_rope",
        **params((2 * t * D * 3 * D, 6 * D * D)),
    )(x, gain, pack, pack, pack, cosine, sine)


def head_rows(v, h):
    row = lax.broadcasted_iota(jnp.int32, v.shape, 0)
    return jnp.where(row // HEAD_DIM == h, v, jnp.zeros_like(v))


def head_lanes(v, h):
    lane = lax.broadcasted_iota(jnp.int32, v.shape, 1)
    return jnp.where(lane // HEAD_DIM == h, v, jnp.zeros_like(v))


def attend_update(qz, kb, vt, lo, hi, mask, st_ref, a_ref, first):
    for h in range(2):
        s = dot(kb, qz[h][:, lo:hi])
        if mask is not None:
            s = jnp.where(mask, s, NEG)
        top = jnp.max(s, axis=0, keepdims=True)
        rows = slice(h * HEAD_DIM, (h + 1) * HEAD_DIM)
        if first:
            p = jnp.exp2((s - top) * LC)
            st_ref[h : h + 1, lo:hi] = top
            st_ref[2 + h : 3 + h, lo:hi] = jnp.sum(p, axis=0, keepdims=True)
            a_ref[rows, lo:hi] = dot(vt[rows], p.astype(BF16))
        else:
            old = st_ref[h : h + 1, lo:hi]
            new = jnp.maximum(old, top)
            alpha = jnp.exp2((old - new) * LC)
            p = jnp.exp2((s - new) * LC)
            st_ref[h : h + 1, lo:hi] = new
            st_ref[2 + h : 3 + h, lo:hi] = st_ref[2 + h : 3 + h, lo:hi] * alpha + jnp.sum(
                p, axis=0, keepdims=True
            )
            a_ref[rows, lo:hi] = a_ref[rows, lo:hi] * alpha + dot(vt[rows], p.astype(BF16))


def local_masks(sc_ref, r, keys, lo, hi):
    cpos = sc_ref[1]
    length = sc_ref[2]
    col = lo + lax.broadcasted_iota(jnp.int32, (r, hi - lo), 1)
    row = lax.broadcasted_iota(jnp.int32, (r, hi - lo), 0)
    own = (row <= col) | (col >= r)
    col = lo + lax.broadcasted_iota(jnp.int32, (keys, hi - lo), 1)
    row = lax.broadcasted_iota(jnp.int32, (keys, hi - lo), 0)
    cont = (col >= r) & (row <= cpos + col - r) & (row < length)
    return own, cont


def fwd_local_body(sc_ref, qt_ref, kv_ref, kvo_ref, st_ref, a_ref):
    t = qt_ref.shape[1]
    r = t // 2
    keys = kvo_ref.shape[0]
    qt = qt_ref[...]
    qz = [head_rows(qt, h) for h in range(2)]
    kb = kv_ref[:, :LANES]
    vt = kv_ref[:, LANES:].T
    kbo = kvo_ref[:, :LANES]
    vto = kvo_ref[:, LANES:].T
    st_ref[...] = jnp.zeros_like(st_ref)
    own, cont = local_masks(sc_ref, r, keys, 0, t)
    if r % LANES == 0:
        attend_update(qz, kb, vt, 0, r, own[:, :r], st_ref, a_ref, True)
        attend_update(qz, kb, vt, r, t, None, st_ref, a_ref, True)
        attend_update(qz, kbo, vto, r, t, cont[:, r:], st_ref, a_ref, False)
    else:
        attend_update(qz, kb, vt, 0, t, own, st_ref, a_ref, True)
        attend_update(qz, kbo, vto, 0, t, cont, st_ref, a_ref, False)


def halves_value(a_ref, b_ref):
    return jnp.where(pl.program_id(0) < PAIRS // 2, a_ref[...], b_ref[...])


def fwd_remote_body(offsets, count, halves, final, sc_ref, qt_ref, *refs):
    kv_refs, refs = refs[:count], refs[count:]
    st_in, a_in, st_ref, a_ref = refs[:4]
    t = qt_ref.shape[1]
    r = t // 2
    me = sc_ref[0]
    qt = qt_ref[...]
    qz = [head_rows(qt, h) for h in range(2)]
    st_ref[...] = st_in[...]
    a_ref[...] = a_in[...]
    for j, offset in enumerate(offsets):
        block = sc_ref[3 + offset]

        def go(lo, hi, mask):
            if halves:
                kv = halves_value(*kv_refs)
            elif len(kv_refs) == len(offsets):
                kv = kv_refs[j][...]
            else:
                kv = kv_refs[0][j * r : (j + 1) * r, :]
            attend_update(qz, kv[:, :LANES], kv[:, LANES:].T, lo, hi, mask, st_ref, a_ref, False)

        if r % LANES == 0:
            if count != len(offsets) and not halves:
                pl.when(block != me)(lambda: go(r, t, None))
            else:
                go(r, t, None)

            @pl.when(block < me)
            def _():
                go(0, r, None)

        else:

            @pl.when(block != me)
            def _():
                col = lax.broadcasted_iota(jnp.int32, (r, t), 1)
                go(0, t, (col >= r) | (block < me))

    if final:
        low_ref = refs[4]
        for h in range(2):
            rows = slice(h * HEAD_DIM, (h + 1) * HEAD_DIM)
            total = st_ref[2 + h : 3 + h, :]
            a_ref[rows, :] = a_ref[rows, :] / total
            st_ref[h : h + 1, :] = st_ref[h : h + 1, :] * LC + jnp.log2(total)
        low_ref[...] = a_ref[...].T.astype(BF16)


def kv_specs(kvs, halves):
    if halves:
        r = kvs[0].shape[0]
        return [
            spec((r, 2 * LANES), lambda i: (0, jnp.minimum(i, PAIRS // 2 - 1))),
            spec((r, 2 * LANES), lambda i: (0, jnp.maximum(i - PAIRS // 2, 0))),
        ]
    return [spec((kv.shape[0], 2 * LANES), lambda i: (0, i)) for kv in kvs]


def fwd_local(sc, qt, kv_prompt, kv_own):
    t = qt.shape[1]
    keys = kv_own.shape[0]
    return pl.pallas_call(
        fwd_local_body,
        grid=(PAIRS,),
        in_specs=[
            SMEM_SPEC,
            spec((LANES, t), lambda i: (i, 0)),
            spec((t // 2, 2 * LANES), lambda i: (0, i)),
            spec((keys, 2 * LANES), lambda i: (0, i)),
        ],
        out_specs=[spec((8, t), lambda i: (i, 0)), spec((LANES, t), lambda i: (i, 0))],
        out_shape=[shape((8 * PAIRS, t), F32), shape((D, t), F32)],
        name="attend_local",
        **params((4 * 4 * t * keys * D, 4 * D * t)),
    )(sc, qt, kv_prompt, kv_own)


def fwd_remote(sc, qt, kvs, offsets, st, acc, halves=False, final=False):
    t = qt.shape[1]
    rows = len(offsets) * (t // 2)
    out_specs = [spec((8, t), lambda i: (i, 0)), spec((LANES, t), lambda i: (i, 0))]
    out_shape = [shape((8 * PAIRS, t), F32), shape((D, t), F32)]
    if final:
        out_specs.append(spec((t, LANES), lambda i: (0, i)))
        out_shape.append(shape((t, D), BF16))
    return pl.pallas_call(
        functools.partial(fwd_remote_body, tuple(offsets), len(kvs), halves, final),
        grid=(PAIRS,),
        in_specs=[SMEM_SPEC, spec((LANES, t), lambda i: (i, 0))]
        + kv_specs(kvs, halves)
        + [spec((8, t), lambda i: (i, 0)), spec((LANES, t), lambda i: (i, 0))],
        out_specs=out_specs,
        out_shape=out_shape,
        name="attend_remote",
        **params((4 * 4 * t * rows * D, 8 * D * t + 4 * D * rows)),
    )(sc, qt, *kvs, st, acc)


def back_block(ops, kb, vb, kt, lo, hi, mask, dq_ref):
    qz, qn, doz, don, lse, delta = ops
    dk = None
    dv = None
    for h in range(2):
        s = dot(kb, qz[h][:, lo:hi])
        dp = dot(vb, doz[h][:, lo:hi])
        p = jnp.exp2(s * LC - lse[h][:, lo:hi])
        if mask is not None:
            p = jnp.where(mask, p, 0.0)
        ds = (p * (dp - delta[h][:, lo:hi])).astype(BF16)
        dv_h = dot(p.astype(BF16), don[h][lo:hi])
        dk_h = dot(ds, qn[h][lo:hi])
        rows = slice(h * HEAD_DIM, (h + 1) * HEAD_DIM)
        dq_ref[rows, lo:hi] += dot(kt[rows], ds)
        dv = dv_h if dv is None else dv + dv_h
        dk = dk_h if dk is None else dk + dk_h
    return dk, dv


def back_operands(qt_ref, q_ref, dot_ref, do_ref, st_ref):
    qt, q, do_t, do = qt_ref[...], q_ref[...], dot_ref[...], do_ref[...]
    return (
        [head_rows(qt, h) for h in range(2)],
        [head_lanes(q, h) for h in range(2)],
        [head_rows(do_t, h) for h in range(2)],
        [head_lanes(do, h) for h in range(2)],
        [st_ref[h : h + 1, :] for h in range(2)],
        [st_ref[4 + h : 5 + h, :] for h in range(2)],
    )


def bwd_local_body(
    sc_ref, qt_ref, q_ref, dot_ref, do_ref, st_ref, dq_in, kv_ref, kvo_ref,
    out_ref, dkv_ref, dkvo_ref, dq_ref,
):
    t = qt_ref.shape[1]
    r = t // 2
    keys = kvo_ref.shape[0]
    ops = back_operands(qt_ref, q_ref, dot_ref, do_ref, st_ref)
    dq_ref[...] = dq_in[...]
    kb, vb = kv_ref[:, :LANES], kv_ref[:, LANES:]
    kbo, vbo = kvo_ref[:, :LANES], kvo_ref[:, LANES:]
    kt, kto = kb.T, kbo.T
    own, cont = local_masks(sc_ref, r, keys, 0, t)
    if r % LANES == 0:
        dk, dv = back_block(ops, kb, vb, kt, 0, r, own[:, :r], dq_ref)
        dk2, dv2 = back_block(ops, kb, vb, kt, r, t, None, dq_ref)
        dk, dv = dk + dk2, dv + dv2
        dko, dvo = back_block(ops, kbo, vbo, kto, r, t, cont[:, r:], dq_ref)
    else:
        dk, dv = back_block(ops, kb, vb, kt, 0, t, own, dq_ref)
        dko, dvo = back_block(ops, kbo, vbo, kto, 0, t, cont, dq_ref)
    dkv_ref[:, :LANES] = dk * SCALE
    dkv_ref[:, LANES:] = dv
    dkvo_ref[:, :LANES] = dko * SCALE
    dkvo_ref[:, LANES:] = dvo
    out_ref[...] = dq_ref[...].T * SCALE


def bwd_remote_body(
    offsets, count, halves, first, dtype, sc_ref, qt_ref, q_ref, dot_ref, do_ref, st_in, *refs
):
    t = qt_ref.shape[1]
    r = t // 2
    me = sc_ref[0]
    kv_refs, refs = refs[:count], refs[count:]
    src, refs = refs[0], refs[1:]
    dq_ref, refs = refs[0], refs[1:]
    out_refs, refs = refs[:count], refs[count:]
    sum_ref = refs[-1]
    if first:
        st_ref, refs = refs[0], refs[1:]
        st_ref[...] = st_in[...]
        prod = src[...] * dot_ref[...].astype(F32)
        for h in range(2):
            st_ref[4 + h : 5 + h, :] = jnp.sum(
                prod[h * HEAD_DIM : (h + 1) * HEAD_DIM], axis=0, keepdims=True
            )
        dq_ref[...] = jnp.zeros_like(dq_ref)
    else:
        st_ref = st_in
        dq_ref[...] = src[...]
    ops = back_operands(qt_ref, q_ref, dot_ref, do_ref, st_ref)
    split = len(offsets) != count and not halves

    def store(j, dk, dv):
        if halves:
            for part in range(2):

                @pl.when((pl.program_id(0) < PAIRS // 2) == (part == 0))
                def _():
                    out_refs[part][:, :LANES] = dk
                    out_refs[part][:, LANES:] = dv

        elif split:
            out_refs[0][j * r : (j + 1) * r, :LANES] = dk
            out_refs[0][j * r : (j + 1) * r, LANES:] = dv
        else:
            out_refs[j][:, :LANES] = dk
            out_refs[j][:, LANES:] = dv

    for j, offset in enumerate(offsets):
        block = sc_ref[3 + offset]

        def go(lo, hi, mask, add):
            if halves:
                kv = halves_value(*kv_refs)
            elif split:
                kv = kv_refs[0][j * r : (j + 1) * r, :]
            else:
                kv = kv_refs[j][...]
            kb = kv[:, :LANES]
            dk, dv = back_block(ops, kb, kv[:, LANES:], kb.T, lo, hi, mask, dq_ref)
            if add:
                dk, dv = dk + sum_ref[:, :LANES], dv + sum_ref[:, LANES:]
            sum_ref[:, :LANES] = dk
            sum_ref[:, LANES:] = dv

        if split:

            @pl.when(block == me)
            def _():
                sum_ref[...] = jnp.zeros_like(sum_ref)

        if r % LANES == 0:
            if split:
                pl.when(block != me)(lambda: go(r, t, None, False))
            else:
                go(r, t, None, False)

            @pl.when(block < me)
            def _():
                go(0, r, None, True)

        else:

            @pl.when(block != me)
            def _():
                col = lax.broadcasted_iota(jnp.int32, (r, t), 1)
                go(0, t, (col >= r) | (block < me), False)

        store(j, (sum_ref[:, :LANES] * SCALE).astype(dtype), sum_ref[:, LANES:].astype(dtype))


def q_specs(t):
    return [
        spec((LANES, t), lambda i: (i, 0)),
        spec((t, LANES), lambda i: (0, i)),
        spec((LANES, t), lambda i: (i, 0)),
        spec((t, LANES), lambda i: (0, i)),
        spec((8, t), lambda i: (i, 0)),
    ]


def bwd_local(sc, qt, q, do_t, do, st, dq, kv_prompt, kv_own):
    t = qt.shape[1]
    keys = kv_own.shape[0]
    return pl.pallas_call(
        bwd_local_body,
        grid=(PAIRS,),
        in_specs=[SMEM_SPEC]
        + q_specs(t)
        + [spec((LANES, t), lambda i: (i, 0))]
        + kv_specs((kv_prompt, kv_own), False),
        out_specs=[spec((t, LANES), lambda i: (0, i))] + kv_specs((kv_prompt, kv_own), False),
        out_shape=[
            shape((t, D), F32),
            shape((t // 2, 2 * D), F32),
            shape((keys, 2 * D), F32),
        ],
        scratch_shapes=[pltpu.VMEM((LANES, t), F32)],
        name="attend_back_local",
        **params((10 * 4 * t * keys * D, 16 * D * t)),
    )(sc, qt, q, do_t, do, st, dq, kv_prompt, kv_own)


def bwd_remote(
    sc, qt, q, do_t, do, st, src, kvs, offsets, halves=False, first=False, dtype=F32
):
    t = qt.shape[1]
    rows = len(offsets) * (t // 2)
    out_specs = [spec((LANES, t), lambda i: (i, 0))] + kv_specs(kvs, halves)
    out_shape = [shape((D, t), F32)] + [shape(kv.shape, dtype) for kv in kvs]
    if first:
        out_specs.append(spec((8, t), lambda i: (i, 0)))
        out_shape.append(shape((8 * PAIRS, t), F32))
    return pl.pallas_call(
        functools.partial(bwd_remote_body, tuple(offsets), len(kvs), halves, first, dtype),
        grid=(PAIRS,),
        in_specs=[SMEM_SPEC]
        + q_specs(t)
        + kv_specs(kvs, halves)
        + [spec((LANES, t), lambda i: (i, 0))],
        out_specs=out_specs,
        out_shape=out_shape,
        scratch_shapes=[pltpu.VMEM((t // 2, 2 * LANES), F32)],
        name="attend_back_remote",
        **params((10 * 4 * t * rows * D, 16 * D * t + 8 * D * rows)),
    )(sc, qt, q, do_t, do, st, *kvs, src)


def route_body(
    x_ref, att_ref, ow_ref, sw_ref, gain_ref, res_ref, rt_ref, tr_ref,
    h_ref, n_ref, pr_ref, xs_ref,
):
    t = x_ref.shape[0]
    step = pl.program_id(0)

    @pl.when(step == 0)
    def _():
        hidden = x_ref[...].astype(F32) + dot(att_ref[...], ow_ref[...])
        h_ref[...] = hidden
        scale = lax.rsqrt(jnp.mean(hidden * hidden, axis=-1, keepdims=True) + EPS)
        low = (hidden * scale * gain_ref[...]).astype(BF16)
        n_ref[...] = low
        z = dot(low, sw_ref[...])
        lane = lax.broadcasted_iota(jnp.int32, (t, LANES), 1)
        is_route = lane < EXPERTS + 4
        logits = jnp.where(is_route, z + res_ref[...], NEG)
        ex = jnp.exp(logits - jnp.max(logits, axis=-1, keepdims=True))
        probs = ex / jnp.sum(ex, axis=-1, keepdims=True)
        out = probs
        first = EXPERTS + 4
        for k in range(2):
            l0 = z[:, first + 2 * k : first + 2 * k + 1]
            l1 = z[:, first + 2 * k + 1 : first + 2 * k + 2]
            top = jnp.maximum(l0, l1)
            e0 = jnp.exp(l0 - top)
            e1 = jnp.exp(l1 - top)
            den = e0 + e1
            out = jnp.where(lane == first + 2 * k, e0 / den, out)
            out = jnp.where(lane == first + 2 * k + 1, e1 / den, out)
        for j in range(2):
            mix = jnp.sum(jnp.where(lane == rt_ref[:, j : j + 1], probs, 0.0), axis=-1, keepdims=True)
            out = jnp.where(lane == 16 + j, mix, out)
        pr_ref[...] = out

    slots = xs_ref.shape[0]
    base = step * slots
    slot = base + lax.broadcasted_iota(jnp.int32, (slots, t), 0)
    pick = (slot == tr_ref[0:1, :]) | (slot == tr_ref[1:2, :])
    xs_ref[...] = dot(pick.astype(BF16), n_ref[...]).astype(BF16)


def out_w_spec():
    return spec((D, D), lambda *_: (0, 3))


def small_w_spec():
    return spec((D, LANES), lambda *_: (0, 4 * D // LANES))


def grad_rows_body(g_ref, pr_ref, tr_ref, gs_ref, mg_ref):
    t = g_ref.shape[0]
    step = pl.program_id(0)

    @pl.when(step == 0)
    def _():
        g = g_ref[...].astype(F32)
        for j in range(2):
            mg_ref[j * t : (j + 1) * t, :] = (g * pr_ref[:, 16 + j : 17 + j]).astype(BF16)

    slots = gs_ref.shape[0]
    slot = step * slots + lax.broadcasted_iota(jnp.int32, (slots, t), 0)
    picks = [(slot == tr_ref[j : j + 1, :]).astype(BF16) for j in range(2)]
    gs_ref[...] = dot(jnp.concatenate(picks, axis=1), mg_ref[...]).astype(BF16)


def grad_rows_call(g, pr, tr, slots):
    t = g.shape[0]
    part = min(slots, 256)
    return pl.pallas_call(
        grad_rows_body,
        grid=(slots // part,),
        in_specs=[whole((t, D)), whole((t, LANES)), whole((2, t))],
        out_specs=spec((part, D), lambda i: (i, 0)),
        out_shape=shape((slots, D), BF16),
        scratch_shapes=[pltpu.VMEM((2 * t, D), BF16)],
        name="grad_rows",
        **params((4 * slots * t * D, 4 * t * D)),
    )(g, pr, tr)


def route_call(x, att, pack, gain, res, rt, tr, slots):
    t = x.shape[0]
    part = min(slots, 256)
    return pl.pallas_call(
        route_body,
        grid=(slots // part,),
        in_specs=[
            whole((t, D)), whole((t, D)), out_w_spec(), small_w_spec(), whole((1, D)),
            whole((t, LANES)), whole((t, 2)), whole((2, t)),
        ],
        out_specs=[
            whole((t, D)), whole((t, D)), whole((t, LANES)),
            spec((part, D), lambda i: (i, 0)),
        ],
        out_shape=[
            shape((t, D), F32), shape((t, D), BF16), shape((t, LANES), F32),
            shape((slots, D), BF16),
        ],
        name="route_dispatch",
        **params((2 * t * D * D + 2 * slots * t * D, 8 * t * D)),
    )(x, att, pack, pack, gain, res, rt, tr)


def expert_fwd_body(x_ref, w_ref, o_ref, acc_ref):
    step = pl.program_id(0)
    x = x_ref[...]
    wide = w_ref.shape[-1]
    wg = w_ref[:, 0].reshape(D, wide)
    wu = w_ref[:, 1].reshape(D, wide)
    wd = w_ref[:, 2].reshape(D, wide)
    gate = dot(x, wg)
    up = dot(x, wu)
    act = (gate / (1.0 + jnp.exp(-gate)) * up).astype(BF16)
    out = dot_nt(act, wd)

    @pl.when(step == 0)
    def _():
        acc_ref[...] = out

    @pl.when(step > 0)
    def _():
        acc_ref[...] += out

    @pl.when(step == pl.num_programs(0) - 1)
    def _():
        o_ref[...] = acc_ref[...].astype(BF16)


def expert_fwd(xr, w):
    rows = xr.shape[0]
    shards, _, per, wide = w.shape
    part = min(wide, 256)
    return pl.pallas_call(
        expert_fwd_body,
        grid=(wide // part,),
        in_specs=[whole((rows, D)), spec((shards, 3, per, part), lambda i: (0, 0, 0, i))],
        out_specs=whole((rows, D)),
        out_shape=shape((rows, D), BF16),
        scratch_shapes=[pltpu.VMEM((rows, D), F32)],
        name="expert_forward",
        **params((6 * rows * D * wide, 6 * D * wide)),
    )(xr, w)


def expert_in_body(x_ref, g_ref, w_ref, gi_ref, act_ref, dg_ref, du_ref, acc_ref):
    step = pl.program_id(0)
    wide = w_ref.shape[-1]
    wg = w_ref[:, 0].reshape(D, wide)
    wu = w_ref[:, 1].reshape(D, wide)
    wd = w_ref[:, 2].reshape(D, wide)

    @pl.loop(0, x_ref.shape[0] // ROW_TILE)
    def _(i):
        rows = pl.ds(pl.multiple_of(i * ROW_TILE, ROW_TILE), ROW_TILE)
        gate = dot(x_ref[rows, :], wg)
        up = dot(x_ref[rows, :], wu)
        ga = dot(g_ref[rows, :], wd)
        sig = 1.0 / (1.0 + jnp.exp(-gate))
        silu = gate * sig
        act_ref[rows, :] = (silu * up).astype(BF16)
        d_gate = (ga * up * sig * (1.0 + gate * (1.0 - sig))).astype(BF16)
        d_up = (ga * silu).astype(BF16)
        dg_ref[rows, :] = d_gate
        du_ref[rows, :] = d_up
        gi = dot_nt(d_gate, wg) + dot_nt(d_up, wu)

        @pl.when(step == 0)
        def _():
            acc_ref[rows, :] = gi

        @pl.when(step > 0)
        def _():
            acc_ref[rows, :] += gi

    @pl.when(step == pl.num_programs(0) - 1)
    def _():
        gi_ref[...] = acc_ref[...].astype(BF16)


def expert_in(xr, gr, w):
    rows = xr.shape[0]
    shards, _, per, wide = w.shape
    part = min(wide, 256)
    tile = spec((rows, part), lambda i: (0, i))
    return pl.pallas_call(
        expert_in_body,
        grid=(wide // part,),
        in_specs=[
            whole((rows, D)), whole((rows, D)),
            spec((shards, 3, per, part), lambda i: (0, 0, 0, i)),
        ],
        out_specs=[whole((rows, D)), tile, tile, tile],
        out_shape=[shape((rows, D), BF16)] + [shape((rows, wide), BF16)] * 3,
        scratch_shapes=[pltpu.VMEM((rows, D), F32)],
        name="expert_back_in",
        **params((10 * rows * D * wide, 12 * D * wide)),
    )(xr, gr, w)


def expert_weights_body(x_ref, gl_ref, act_ref, dg_ref, du_ref, dw_ref, xt_ref, gt_ref):
    @pl.when(pl.program_id(0) == 0)
    def _():
        gt_ref[...] = gl_ref[...].T
        xt_ref[...] = x_ref[...].T

    shards, _, per, wide = dw_ref.shape
    xt = xt_ref[...]
    dw_ref[:, 0] = dot(xt, dg_ref[...]).astype(BF16).reshape(shards, per, wide)
    dw_ref[:, 1] = dot(xt, du_ref[...]).astype(BF16).reshape(shards, per, wide)
    dw_ref[:, 2] = dot(gt_ref[...], act_ref[...]).astype(BF16).reshape(shards, per, wide)


def expert_weights(xr, low, act, d_gate, d_up, dims):
    rows = xr.shape[0]
    shards, _, per, wide = dims
    part = min(wide, 256)
    tile = spec((rows, part), lambda i: (0, i))
    return pl.pallas_call(
        expert_weights_body,
        grid=(wide // part,),
        in_specs=[whole((rows, D)), whole((rows, D)), tile, tile, tile],
        out_specs=spec((shards, 3, per, part), lambda i: (0, 0, 0, i)),
        out_shape=shape(dims, BF16),
        scratch_shapes=[pltpu.VMEM((D, rows), BF16), pltpu.VMEM((D, rows), BF16)],
        name="expert_weight_grads",
        **params((6 * rows * D * wide, 12 * D * wide)),
    )(xr, low, act, d_gate, d_up)


def mix_body(
    h_ref, g_ref, pr_ref, rt_ref, tc_ref, ret_ref, n_ref, sw_ref, rows_ref,
    out_ref, gn_ref, gl_ref, gs_ref,
):
    t = h_ref.shape[0]
    slots = ret_ref.shape[0]
    hidden = h_ref[...]
    g16 = g_ref[...]
    g = g16.astype(F32)
    pr = pr_ref[...]
    scale = lax.rsqrt(jnp.mean(hidden * hidden, axis=-1, keepdims=True) + EPS)
    normed = hidden * scale * rows_ref[2:3, :]
    lane = lax.broadcasted_iota(jnp.int32, (t, LANES), 1)
    slot = lax.broadcasted_iota(jnp.int32, (t, slots), 1)
    first = EXPERTS + 4
    ret = ret_ref[...]
    c0 = [pr[:, first + 2 * k : first + 2 * k + 1] for k in range(2)]
    c1 = [pr[:, first + 2 * k + 1 : first + 2 * k + 2] for k in range(2)]
    total = hidden
    s = jnp.zeros((t, LANES), F32)
    coef = jnp.zeros((t, 1), F32)
    weight = [jnp.zeros((t, 1), F32) for _ in range(2)]
    for j in range(2):
        route = rt_ref[:, j : j + 1]
        mix = pr[:, 16 + j : 17 + j]
        branch = dot((slot == tc_ref[:, j : j + 1]).astype(BF16), ret)
        keep = jnp.where(route == EXPERTS + 1, 1.0, 0.0)
        for k in range(2):
            here = jnp.where(route == EXPERTS + 2 + k, 1.0, 0.0)
            keep = keep + here * c0[k]
            weight[k] = weight[k] + here * mix
            branch = branch + (here * c1[k]) * rows_ref[k : k + 1, :]
        branch = branch + keep * normed
        coef = coef + mix * keep
        total = total + mix * branch
        gp = jnp.sum(g * branch, axis=-1, keepdims=True)
        s = s + jnp.where(lane == route, gp, 0.0)
    out_ref[...] = total.astype(BF16)
    probs = jnp.where(lane < first, pr, 0.0)
    d_logits = probs * (s - jnp.sum(probs * s, axis=-1, keepdims=True))
    gl_ref[...] = d_logits
    dz = d_logits
    dvec = jnp.zeros((t, LANES), F32)
    g_dot_n = jnp.sum(g * normed, axis=-1, keepdims=True)
    for k in range(2):
        d0 = weight[k] * g_dot_n
        d1 = weight[k] * jnp.sum(g * rows_ref[k : k + 1, :], axis=-1, keepdims=True)
        mean = c0[k] * d0 + c1[k] * d1
        dz = jnp.where(lane == first + 2 * k, c0[k] * (d0 - mean), dz)
        dz = jnp.where(lane == first + 2 * k + 1, c1[k] * (d1 - mean), dz)
        dvec = jnp.where(lane == 16 + k, weight[k] * c1[k], dvec)
    hi, lo = split_hi_lo(dz)
    sw = sw_ref[...]
    gn_ref[...] = coef * g + (dot_nt(hi, sw) + dot_nt(lo, sw))
    nt = n_ref[...].T
    gt = g16.T
    vhi, vlo = split_hi_lo(dvec)
    gs = dot(nt, hi) + dot(nt, lo) + dot(gt, vhi) + dot(gt, vlo)

    @pl.when(pl.program_id(0) == 0)
    def _():
        gs_ref[...] = gs

    @pl.when(pl.program_id(0) > 0)
    def _():
        gs_ref[...] += gs


def mix_call(hidden, g, pr, rt, tc, ret, low, pack, rows):
    t = hidden.shape[0]
    half = min(t, LANES)
    slots = ret.shape[0]
    tile = spec((half, D), lambda i: (i, 0))
    lane_tile = spec((half, LANES), lambda i: (i, 0))
    pair = spec((half, 2), lambda i: (i, 0))
    return pl.pallas_call(
        mix_body,
        grid=(t // half,),
        in_specs=[
            tile, tile, lane_tile, pair, pair, whole((slots, D)), tile, small_w_spec(),
            whole((8, D)),
        ],
        out_specs=[tile, tile, lane_tile, whole((D, LANES))],
        out_shape=[
            shape((t, D), BF16), shape((t, D), F32), shape((t, LANES), F32), shape((D, LANES), F32),
        ],
        name="mixture",
        **params((4 * t * slots * D, 12 * t * D)),
    )(hidden, g, pr, rt, tc, ret, low, pack, rows)


def norm_back_body(
    h_ref, g_ref, gn_ref, tc_ref, ret_ref, rows_ref, ow_ref, att_ref,
    gh_ref, do_ref, dot_ref, gow_ref, gg_ref,
):
    t = h_ref.shape[0]
    slots = ret_ref.shape[0]
    hidden = h_ref[...]
    slot = lax.broadcasted_iota(jnp.int32, (t, slots), 1)
    pick = (slot == tc_ref[:, 0:1]) | (slot == tc_ref[:, 1:2])
    gn = gn_ref[...] + dot(pick.astype(BF16), ret_ref[...])
    q = lax.rsqrt(jnp.mean(hidden * hidden, axis=-1, keepdims=True) + EPS)
    u = gn * rows_ref[2:3, :]
    mean = jnp.mean(u * hidden, axis=-1, keepdims=True)
    gh = g_ref[...].astype(F32) + q * u - hidden * (q * q * q * mean)
    gh_ref[...] = gh
    gb = gh.astype(BF16)
    d_out = dot_nt(gb, ow_ref[...])
    do_ref[...] = d_out.astype(BF16)
    dot_ref[...] = d_out.T.astype(BF16)
    gow = dot(att_ref[...].T, gb)
    gain = jnp.sum(gn * hidden * q, axis=0, keepdims=True)

    @pl.when(pl.program_id(0) == 0)
    def _():
        gow_ref[...] = gow
        gg_ref[...] = jnp.broadcast_to(gain, gg_ref.shape)

    @pl.when(pl.program_id(0) > 0)
    def _():
        gow_ref[...] += gow
        gg_ref[...] += jnp.broadcast_to(gain, gg_ref.shape)


def norm_back_call(hidden, g, gn, tc, ret, rows, pack, att):
    t = hidden.shape[0]
    half = t // 2 if (t // 2) % LANES == 0 else t
    slots = ret.shape[0]
    tile = spec((half, D), lambda i: (i, 0))
    return pl.pallas_call(
        norm_back_body,
        grid=(t // half,),
        in_specs=[
            tile, tile, tile, spec((half, 2), lambda i: (i, 0)), whole((slots, D)), whole((8, D)),
            out_w_spec(), tile,
        ],
        out_specs=[tile, tile, spec((D, half), lambda i: (0, i)), whole((D, D)), whole((8, D))],
        out_shape=[
            shape((t, D), F32), shape((t, D), BF16), shape((D, t), BF16), shape((D, D), F32),
            shape((8, D), F32),
        ],
        name="norm_two_back",
        **params((2 * t * slots * D + 4 * t * D * D, 16 * t * D)),
    )(hidden, g, gn, tc, ret, rows, pack, att)


def store_grad(sc_ref, split, value, refs):
    if not split:
        refs[0][...] = value
        return
    send_ref, keep_ref = refs
    per = value.shape[0] // 4
    for core in range(2):

        @pl.when(sc_ref[11] == core)
        def _():
            for part in range(2):
                mine = (2 * part + core) * per
                other = (2 * part + 1 - core) * per
                send_ref[part] = value[other : other + per].astype(BF16)
                keep_ref[part] = value[mine : mine + per]


def grad_outs(split, width):
    block = 2 * LANES
    if not split:
        return [spec((D, block), lambda i: (0, i))], [shape((D, width), F32)]
    dims = (2, D // 4, width)
    tile = spec((2, D // 4, block), lambda i: (0, 0, i))
    return [tile, tile], [shape(dims, BF16), shape(dims, F32)]


def q_back_body(split, sc_ref, n_ref, dq_ref, c_ref, s_ref, w_ref, gn_ref, *refs):
    nt_ref = refs[-1]
    step = pl.program_id(0)

    @pl.when(step == 0)
    def _():
        nt_ref[...] = n_ref[...].T

    cosine = c_ref[...]
    sine = s_ref[...]
    v0 = dq_ref[:, :LANES]
    v1 = dq_ref[:, LANES:]
    gq = jnp.concatenate(
        [
            (v0 * cosine - partner(v0) * sine).astype(BF16),
            (v1 * cosine - partner(v1) * sine).astype(BF16),
        ],
        axis=1,
    )
    store_grad(sc_ref, split, dot(nt_ref[...], gq), refs[:-1])
    gn = dot_nt(gq, w_ref[...])

    @pl.when(step == 0)
    def _():
        gn_ref[...] = gn

    @pl.when(step > 0)
    def _():
        gn_ref[...] += gn


def q_back_call(sc, low, dq, cosine, sine, pack, split):
    t = low.shape[0]
    specs, shapes = grad_outs(split, D)
    return pl.pallas_call(
        functools.partial(q_back_body, split),
        grid=(PAIRS // 2,),
        in_specs=[
            SMEM_SPEC, whole((t, D)), spec((t, 2 * LANES), lambda i: (0, i)), whole((t, LANES)),
            whole((t, LANES)), spec((D, 2 * LANES), lambda i: (0, i)),
        ],
        out_specs=[whole((t, D))] + specs,
        out_shape=[shape((t, D), F32)] + shapes,
        scratch_shapes=[pltpu.VMEM((D, t), BF16)],
        name="q_back",
        **params((4 * t * D * D, 12 * t * D)),
    )(sc, low, dq, cosine, sine, pack)


def kv_back_body(
    split, count, sc_ref, x_ref, n_ref, gnq_ref, gh_ref, gain_ref, c_ref, s_ref, wk_ref, wv_ref,
    own_ref, cont_ref, *refs
):
    got_refs, refs = refs[:count], refs[count:]
    gi_ref, grads, (nt_ref, gn_ref) = refs[0], refs[1:-2], refs[-2:]
    step = pl.program_id(0)

    @pl.when(step == 0)
    def _():
        nt_ref[...] = n_ref[...].T
        gn_ref[...] = gnq_ref[...]

    own = own_ref[...]
    for got in got_refs:
        own = own + got[...].astype(F32)
    total = jnp.concatenate([own, cont_ref[...]], axis=0)
    k = total[:, :LANES]
    gk = (k * c_ref[...] - partner(k) * s_ref[...]).astype(BF16)
    gkv = jnp.concatenate([gk, total[:, LANES:].astype(BF16)], axis=1)
    store_grad(sc_ref, split, dot(nt_ref[...], gkv), grads)
    gn_ref[...] += dot_nt(gkv, jnp.concatenate([wk_ref[...], wv_ref[...]], axis=1))

    @pl.when(step == pl.num_programs(0) - 1)
    def _():
        gn = gn_ref[...]
        x = x_ref[...].astype(F32)
        q = lax.rsqrt(jnp.mean(x * x, axis=-1, keepdims=True) + EPS)
        u = gn * gain_ref[...]
        mean = jnp.mean(u * x, axis=-1, keepdims=True)
        gi_ref[...] = gh_ref[...] + q * u - x * (q * q * q * mean)


def kv_back_call(sc, x, low, gn, gh, gain, cosine, sine, pack, own, cont, got, split):
    t = x.shape[0]
    r = t // 2
    specs, shapes = grad_outs(split, 2 * D)
    wide = spec((r, 2 * LANES), lambda i: (0, i))
    return pl.pallas_call(
        functools.partial(kv_back_body, split, len(got)),
        grid=(PAIRS,),
        in_specs=[
            SMEM_SPEC, whole((t, D)), whole((t, D)), whole((t, D)), whole((t, D)), whole((1, D)),
            whole((t, LANES)), whole((t, LANES)),
            spec((D, LANES), lambda i: (0, PAIRS + i)),
            spec((D, LANES), lambda i: (0, 2 * PAIRS + i)),
            wide, wide,
        ]
        + [wide] * len(got),
        out_specs=[whole((t, D))] + specs,
        out_shape=[shape((t, D), F32)] + shapes,
        scratch_shapes=[pltpu.VMEM((D, t), BF16), pltpu.VMEM((t, D), F32)],
        name="kv_back",
        **params((8 * t * D * D, 24 * t * D)),
    )(sc, x, low, gn, gh, gain, cosine, sine, pack, pack, own, cont, *got)


def rotation_tables(position):
    half = HEAD_DIM // 2
    frequency = 10000.0 ** (-jnp.arange(half, dtype=F32) / half)
    angles = position[:, None] * frequency[None, :]
    cosine, sine = jnp.cos(angles), jnp.sin(angles)
    return (
        jnp.concatenate([cosine] * 4, axis=1),
        jnp.concatenate([-sine, sine, -sine, sine], axis=1),
    )


def to_rows(array):
    return jnp.transpose(array, (1, 0, 2)).reshape(2 * array.shape[0], array.shape[2])


def from_rows(array):
    r = array.shape[0] // 2
    return jnp.transpose(array.reshape(2, r, array.shape[1]), (1, 0, 2))


RING = (0, 2, 4, 6, 7, 5, 3, 1)


def ring_offsets():
    place = {e: i for i, e in enumerate(RING)}
    return [[RING[(place[e] + k) % 8] for k in range(8)] for e in range(8)]


def along_ring(array, step):
    pairs = [(RING[i], RING[(i + step) % 8]) for i in range(8)]
    return lax.ppermute(array, "expert", pairs)


def tie(*values):
    return lax.optimization_barrier(values)


def swap_core(array):
    return lax.ppermute(array, "dp", [(0, 1), (1, 0), (2, 3), (3, 2)])


def add_and_cross(keep, got):
    across = lax.axis_index("dp") // 2
    keep = keep + got.astype(F32)
    send = lax.dynamic_index_in_dim(keep, 1 - across, 0, keepdims=False).astype(BF16)
    mine = lax.dynamic_index_in_dim(keep, across, 0, keepdims=False)
    return mine, lax.ppermute(send, "dp", [(0, 2), (2, 0), (1, 3), (3, 1)])


def add_and_scatter(keep, got):
    keep = (keep + got.astype(F32)).astype(BF16)
    rows, w = keep.shape
    return lax.all_to_all(
        keep.reshape(8, rows // 8, w), "expert", split_axis=0, concat_axis=0, tiled=True
    )


def add_up(got):
    return jnp.sum(got.astype(F32), axis=0)


def scatter_all(array):
    return lax.psum_scatter(
        array.astype(BF16), ALL_AXES, scatter_dimension=0, tiled=True
    ).astype(F32)


def per_device(
    hidden_in, cotangent, gate_residual, routes, groups, lengths, attn_gain, qkv_weight, out_weight,
    ffn_gain, router_weight, const_proj, const_vec, gate_weight, up_weight, down_weight,
):
    del groups
    r = hidden_in.shape[0]
    t = 2 * r
    capacity = r // 2
    owners = lax.axis_size("expert")
    copies = owners // EXPERTS
    slots = EXPERTS * capacity
    me = lax.axis_index("expert")
    per_cont = max(CONT_LEN // r, 1)

    small = jnp.concatenate(
        [
            router_weight, const_proj, const_vec, attn_gain[:, None], ffn_gain[:, None],
            jnp.zeros((attn_gain.shape[0], LANES - 20), BF16),
        ],
        axis=1,
    )
    pack = lax.all_gather(
        jnp.concatenate([qkv_weight, out_weight, small], axis=1), ALL_AXES, axis=0, tiled=True
    )
    index = jnp.arange(r, dtype=jnp.int32)
    row_ids = me * r + index
    position = jnp.concatenate([row_ids, PROMPT + row_ids % CONT_LEN]).astype(F32)
    cosine, sine = rotation_tables(position)
    cont = (me * r) // CONT_LEN
    length = lax.dynamic_slice(lengths, (cont,), (1,))
    header = jnp.stack([me, (me * r) % CONT_LEN]).astype(jnp.int32)
    header = jnp.concatenate([header, length.astype(jnp.int32)])
    ring = owners == 8
    if ring:
        ids = lax.dynamic_index_in_dim(jnp.asarray(ring_offsets(), jnp.int32), me, 0, keepdims=False)
    else:
        ids = jnp.arange(owners, dtype=jnp.int32)
    sc = jnp.concatenate([header, ids, (lax.axis_index("dp") % 2).astype(jnp.int32)[None]])

    picked = to_rows(routes)
    flat = jnp.transpose(picked).reshape(2 * t)
    hot = flat[:, None] == jnp.arange(EXPERTS, dtype=jnp.int32)[None, :]
    earlier = jnp.arange(2 * t)[:, None] > jnp.arange(2 * t)[None, :]
    before = jnp.dot(earlier.astype(BF16), hot.astype(BF16), preferred_element_type=F32)
    slot_index = jnp.sum(jnp.where(hot, before, 0.0), axis=1).astype(jnp.int32)
    target = jnp.where(flat < EXPERTS, flat * capacity + slot_index, -1)
    target_rows = target.reshape(2, t)
    target_cols = jnp.transpose(target_rows)

    def to_owners(rows):
        w = rows.shape[-1]
        shaped = rows.reshape(EXPERTS, 1, capacity, w)
        return jnp.broadcast_to(shaped, (EXPERTS, copies, capacity, w)).reshape(owners, capacity, w)

    def exchange(rows):
        got = lax.all_to_all(rows, "expert", split_axis=0, concat_axis=0, tiled=True)
        return got.reshape(owners * got.shape[1], got.shape[2])

    def from_owners(rows):
        got = exchange(rows.reshape(owners, capacity, D))
        if copies == 1:
            return got
        got = got.reshape(EXPERTS, copies, capacity, D).astype(F32)
        return jnp.sum(got, axis=1).reshape(slots, D).astype(BF16)

    x = to_rows(hidden_in)
    g = to_rows(cotangent)
    small_w = pack[:, 4 * D :]
    small_rows = jnp.transpose(small_w[:, 16:24]).astype(F32)
    gain_one = small_rows[2:3]
    rows_two = jnp.concatenate([small_rows[0:2], small_rows[3:4], small_rows[3:8]], axis=0)
    gain_two = small_rows[3:4]

    low_one, q, q_t, kv_prompt, kv_cont = qkv_call(x, gain_one, pack, cosine, sine)
    if not ring:
        kv_all = lax.all_gather(kv_prompt, "expert", axis=0, tiled=True)
    if per_cont == 1:
        kv_own = kv_cont
    else:
        cont_groups = [
            [c * per_cont + i for i in range(per_cont)] for c in range(owners // per_cont)
        ]
        kv_own = lax.all_gather(
            kv_cont, "expert", axis=0, tiled=True, axis_index_groups=cont_groups
        )
    weights = lax.all_gather(
        jnp.stack([gate_weight, up_weight, down_weight]), "dp", axis=0, tiled=False
    )
    if ring:
        right, left = [kv_prompt], [kv_prompt]
        for i in range(3):
            right.append(along_ring(right[i], 1))
            left.append(along_ring(left[i], -1))
            if i == 0:
                st, acc = fwd_local(sc, q_t, kv_prompt, kv_own)
            else:
                st, acc = fwd_remote(sc, q_t, (right[i], left[i]), (8 - i, i), st, acc)
            right[i + 1], left[i + 1], st = tie(right[i + 1], left[i + 1], st)
        far = [along_ring(right[3][:, :D], 1), along_ring(left[3][:, D:], -1)]
        st, acc = fwd_remote(sc, q_t, (right[3], left[3]), (5, 3), st, acc)
        st, att_t, att = fwd_remote(sc, q_t, far, (4,), st, acc, halves=True, final=True)
    else:
        st, acc = fwd_local(sc, q_t, kv_prompt, kv_own)
        st, att_t, att = fwd_remote(sc, q_t, (kv_all,), range(owners), st, acc, final=True)

    res = jnp.pad(to_rows(gate_residual), ((0, 0), (0, LANES - EXPERTS - 4)))
    hidden, low_two, pr, x_send = route_call(
        x, att, pack, gain_two, res, picked, target_rows, slots
    )
    x_got = exchange(to_owners(x_send))
    g_send = grad_rows_call(g, pr, target_rows, slots)
    x_got, g_send = tie(x_got, g_send)
    g_got = exchange(to_owners(g_send))
    expert_rows = expert_fwd(x_got, weights)
    out_back = from_owners(expert_rows)
    grad_in, act, d_gate, d_up = expert_in(x_got, g_got, weights)
    in_back = from_owners(grad_in)
    output, gn, grad_logits, grad_small = mix_call(
        hidden, g, pr, picked, target_cols, out_back, low_two, pack, rows_two
    )
    act, gn = tie(act, gn)
    grad_w = expert_weights(x_got, g_got, act, d_gate, d_up, weights.shape)
    grad_expert = lax.psum_scatter(
        grad_w.reshape(-1, grad_w.shape[-1]), "dp", scatter_dimension=0, tiled=True
    ).astype(F32)
    gh, d_att, d_att_t, grad_ow, gg_two = norm_back_call(
        hidden, g, gn, target_cols, in_back, rows_two, pack, att
    )

    early = jnp.concatenate(
        [grad_ow, grad_small[:, :19], jnp.transpose(gg_two[0:1]), jnp.zeros((D, LANES - 20), F32)],
        axis=1,
    )
    back = (sc, q_t, q, d_att_t, d_att)
    if ring:
        parts = early.reshape(2, 2, D // 4, D + LANES)
        core = lax.axis_index("dp") % 2
        early_keep = lax.dynamic_index_in_dim(parts, core, 1, keepdims=False)
        early_got = swap_core(
            lax.dynamic_index_in_dim(parts, 1 - core, 1, keepdims=False).astype(BF16)
        )
        dq_t, send_r, send_l, st = bwd_remote(
            *back, st, att_t, far, (4,), halves=True, first=True, dtype=BF16
        )
        for i in range(3, 0, -1):
            got_r, got_l = along_ring(send_r, 1), along_ring(send_l, -1)
            dq_t, part_r, part_l = bwd_remote(
                *back, st, dq_t, (left[i], right[i]), (i, 8 - i)
            )
            got_r, got_l, part_r, part_l, dq_t, early_got = tie(
                got_r, got_l, part_r, part_l, dq_t, early_got
            )
            if i == 3:
                send_r = jnp.concatenate([part_r[:, :D] + got_r.astype(F32), part_r[:, D:]], axis=1)
                send_l = jnp.concatenate([part_l[:, :D], part_l[:, D:] + got_l.astype(F32)], axis=1)
                early_keep, early_got = add_and_cross(early_keep, early_got)
            else:
                send_r, send_l = part_r + got_r.astype(F32), part_l + got_l.astype(F32)
            send_r, send_l = send_r.astype(BF16), send_l.astype(BF16)
        send_r, send_l, dq_t = tie(send_r, send_l, dq_t)
        got_r = along_ring(send_r, 1)
        got_l = along_ring(send_l, -1)
        got = (got_r, got_l)
        dq, dkv_own, dkv_cont = bwd_local(*back, st, dq_t, kv_prompt, kv_own)
    else:
        dq_t, dkv_all, st = bwd_remote(
            *back, st, att_t, (kv_all,), range(owners), first=True, dtype=BF16
        )
        dq, dkv_own, dkv_cont = bwd_local(*back, st, dq_t, kv_prompt, kv_own)
        got = (lax.psum_scatter(dkv_all, "expert", scatter_dimension=0, tiled=True),)
        early = scatter_all(early)
    if per_cont > 1:
        dkv_cont = lax.psum_scatter(
            dkv_cont, "expert", scatter_dimension=0, tiled=True, axis_index_groups=cont_groups
        )
    gn_q, *grad_q = q_back_call(sc, low_one, dq, cosine, sine, pack, ring)
    if ring:
        keep_q, got_q = add_and_cross(grad_q[1], swap_core(grad_q[0]))
        keep_q, got_q, got_0, got_1 = tie(keep_q, got_q, *got)
        got = (got_0, got_1)
    grad_input, *grad_kv = kv_back_call(
        sc, x, low_one, gn_q, gh, gain_one, cosine, sine, pack, dkv_own, dkv_cont, got, ring
    )
    output, grad_input = from_rows(output), from_rows(grad_input)
    if ring:
        got_kv = swap_core(grad_kv[0])
        got_q = add_and_scatter(
            jnp.concatenate([early_keep, keep_q], axis=1), jnp.concatenate([early_got, got_q], axis=1)
        )
        keep_kv, got_kv = add_and_cross(grad_kv[1], got_kv)
        got_kv, grad_expert, output, grad_input = tie(got_kv, grad_expert, output, grad_input)
        summed = add_up(got_q)
        early, late_q = summed[:, : D + LANES], summed[:, D + LANES :]
        late_kv = add_up(add_and_scatter(keep_kv, got_kv))
    else:
        late_q, late_kv = scatter_all(grad_q[0]), scatter_all(grad_kv[0])
    per = late_kv.shape[0]
    late_kv = jnp.transpose(late_kv.reshape(per, PAIRS, 2, LANES), (0, 2, 1, 3))
    late = jnp.concatenate([late_q, late_kv.reshape(per, 2 * D)], axis=1)
    grad_gain = jnp.sum(late * qkv_weight.astype(F32), axis=1) / attn_gain.astype(F32)
    tail = early[:, D:]
    per = grad_expert.shape[0] // 3
    return (
        output,
        grad_input,
        from_rows(grad_logits)[:, :, : EXPERTS + 4],
        grad_gain,
        late,
        early[:, :D],
        tail[:, 19],
        tail[:, :12],
        tail[:, 12:16],
        tail[:, 16:18],
        grad_expert[:per],
        grad_expert[per : 2 * per],
        grad_expert[2 * per :],
    )


def solution(mesh):
    rows = P(ALL_AXES, None, None)
    flat = P(ALL_AXES)
    mat = P(ALL_AXES, None)
    expert = P("dp", "expert")
    in_specs = (
        rows, rows, rows, rows, P("dp"), P("dp"), flat, mat, mat, flat, mat, mat, mat,
        expert, expert, expert,
    )
    out_specs = (
        rows, rows, rows, flat, mat, mat, flat, mat, mat, mat, expert, expert, expert,
    )

    return jax.shard_map(
        per_device, mesh=mesh, in_specs=in_specs, out_specs=out_specs, check_vma=False
    )
```

profile of v0, /device:TPU:0, one launch (start us, length us, event | category | flops | bytes accessed | tf_op | source)
XLA Modules:
  0.0 609.4 jit_solution(18032637407509878702)
XLA Ops:
  21.0 58.9 %all-gather.4.cloned.1.call-done.wq_ref.wk_ref.wv_ref.ow_ref.sw_ref.w_ref = bf16[768,3200]{1,0:T(8,128)(2,1)} async-done(((bf16[24,3200]{1,0:T(8,128)(2,1)}), bf16[768,3200]{1,0:T(8,128)(2,1)}) %all-gather.4.cloned.1.call-update) | async-done | bytes 4915216 | tf_op jit(solution)/shard_map/all_gather | solution.py:1099
  82.0 9.1 %qkv_rope.1 = (bf16[512,768]{1,0:T(8,128)(2,1)}, bf16[512,768]{1,0:T(8,128)(2,1)}, bf16[768,512]{1,0:T(8,128)(2,1)}, bf16[256,1536]{1,0:T(8,128)(2,1)}, bf16[256,1536]{1,0:T(8,128)(2,1)}) custom-call(bf16[512,768]{1,0:T(8,128)(2,1)} %bitcast.72, f32[1,768]{1,0:T(1,128)} %copy.137.gain_ref, ...), custom_call_target="tpu_custom_call" | custom-call | flops 1811939328 | bytes 3538944 | tf_op jit(solution)/shard_map/qkv_rope/pallas_call | solution.py:99
  95.7 12.4 %attend_local.1 = (f32[48,512]{1,0:T(8,128)}, f32[768,512]{1,0:T(8,128)}) custom-call(s32[12]{0:T(128)} %concatenate.59.sc_ref, bf16[768,512]{1,0:T(8,128)(2,1)} %get-tuple-element.111.qt_ref, bf16[256,1536]{1,0:T(8,128)(2,1)} %get-tuple-element.113.kv_ref, bf16[256,1536]{1,0:T(8,128)(2,1)} %get-tuple-element.114.kvo_ref), custom_call_target="tpu_custom_call" | custom-call | flops 1610612736 | bytes 1572864 | tf_op jit(solution)/shard_map/attend_local/pallas_call | solution.py:263
  114.2 10.0 %attend_remote.4 = (f32[48,512]{1,0:T(8,128)}, f32[768,512]{1,0:T(8,128)}) custom-call(s32[12]{0:T(128)} %concatenate.59.sc_ref, bf16[768,512]{1,0:T(8,128)(2,1)} %get-tuple-element.111.qt_ref, bf16[256,1536]{1,0:T(8,128)(2,1)} %copy-done.26, bf16[256,1536]{1,0:T(8,128)(2,1)} %copy-done.25, f32[48,512]{1,0:T(8,128)} %get-tuple-element.118.refs_2_, ...), custom_call_target="tpu_custom_call" | custom-call | flops 3221225472 | bytes 4718592 | tf_op jit(solution)/shard_map/attend_remote/pallas_call | solution.py:287
  124.2 6.7 %collective-permute-done.2.refs_0_.refs_1_ = bf16[256,1536]{1,0:T(8,128)(2,1)S(1)} collective-permute-done((bf16[256,1536]{1,0:T(8,128)(2,1)S(1)}, bf16[256,1536]{1,0:T(8,128)(2,1)S(1)}, u32[]{:S(2)}, u32[]{:S(2)}) %collective-permute-start.2) | collective-permute-done | bytes 786464 | tf_op jit(solution)/shard_map/ppermute | solution.py:1041
  134.7 10.0 %attend_remote.5 = (f32[48,512]{1,0:T(8,128)}, f32[768,512]{1,0:T(8,128)}) custom-call(s32[12]{0:T(128)} %concatenate.59.sc_ref, bf16[768,512]{1,0:T(8,128)(2,1)} %get-tuple-element.111.qt_ref, bf16[256,1536]{1,0:T(8,128)(2,1)} %copy-done.27, bf16[256,1536]{1,0:T(8,128)(2,1)} %collective-permute-done.3.refs_1_.refs_0_, ...), custom_call_target="tpu_custom_call" | custom-call | flops 3221225472 | bytes 4718592 | tf_op jit(solution)/shard_map/attend_remote/pallas_call | solution.py:287
  156.7 10.0 %attend_remote.6 = (f32[48,512]{1,0:T(8,128)}, f32[768,512]{1,0:T(8,128)}) custom-call(s32[12]{0:T(128)} %concatenate.59.sc_ref, bf16[768,512]{1,0:T(8,128)(2,1)} %get-tuple-element.111.qt_ref, bf16[256,1536]{1,0:T(8,128)(2,1)} %copy-done.19, bf16[256,1536]{1,0:T(8,128)(2,1)} %copy-done.20, f32[48,512]{1,0:T(8,128)} %get-tuple-element.128.refs_2_, ...), custom_call_target="tpu_custom_call" | custom-call | flops 3221225472 | bytes 4718592 | tf_op jit(solution)/shard_map/attend_remote/pallas_call | solution.py:287
  166.7 7.4 %attend_remote.7 = (f32[48,512]{1,0:T(8,128)}, f32[768,512]{1,0:T(8,128)}, bf16[512,768]{1,0:T(8,128)(2,1)}) custom-call(s32[12]{0:T(128)} %concatenate.59.sc_ref, bf16[768,512]{1,0:T(8,128)(2,1)} %get-tuple-element.111.qt_ref, bf16[256,768]{1,0:T(8,128)(2,1)} %collective-permute-done.6.refs_0_, bf16[256,768]{1,0:T(8,128)(2,1)} %collective-permute-done.7.refs_1_, ...), custom_call_target="tpu_custom_call" | custom-call | flops 1610612736 | bytes 3932160 | tf_op jit(solution)/shard_map/attend_remote/pallas_call | solution.py:287
  174.1 9.4 %route_dispatch.1 = (f32[512,768]{1,0:T(8,128)}, bf16[512,768]{1,0:T(8,128)(2,1)}, f32[512,128]{1,0:T(8,128)}, bf16[1024,768]{1,0:T(8,128)(2,1)}) custom-call(bf16[512,768]{1,0:T(8,128)(2,1)} %bitcast.73, bf16[512,768]{1,0:T(8,128)(2,1)} %get-tuple-element.132.att_ref, ...), custom_call_target="tpu_custom_call" | custom-call | flops 1409286144 | bytes 3145728 | tf_op jit(solution)/shard_map/route_dispatch/pallas_call | solution.py:587
  183.5 17.4 %all-to-all-start = ((bf16[8,128,768]{2,1,0:T(8,128)(2,1)}), bf16[8,128,768]{2,1,0:T(8,128)(2,1)S(1)}, u32[]{:S(2)}, u32[]{:S(2)}) async-start(bf16[8,128,768]{2,1,0:T(8,128)(2,1)} %bitcast.100), calls=%async_computation | async-start | bytes 3145728 | tf_op jit(solution)/shard_map/all_to_all | solution.py:1133
  206.7 29.1 %all-to-all-done = bf16[8,128,768]{2,1,0:T(8,128)(2,1)S(1)} async-done(((bf16[8,128,768]{2,1,0:T(8,128)(2,1)}), bf16[8,128,768]{2,1,0:T(8,128)(2,1)S(1)}, u32[]{:S(2)}, u32[]{:S(2)}) %all-to-all-start) | async-done | bytes 1572896 | tf_op jit(solution)/shard_map/all_to_all | solution.py:1133
  240.6 17.6 %expert_forward.1 = bf16[1024,768]{1,0:T(8,128)(2,1)} custom-call(bf16[1024,768]{1,0:T(8,128)(2,1)} %bitcast.92, bf16[4,3,192,2048]{3,2,1,0:T(8,128)(2,1)} %bitcast.120), custom_call_target="tpu_custom_call" | custom-call | flops 9663676416 | bytes 9437184 | tf_op jit(solution)/shard_map/expert_forward/pallas_call | solution.py:636
  258.2 19.3 %all-to-all-done.1 = bf16[8,128,768]{2,1,0:T(8,128)(2,1)S(1)} async-done(((bf16[8,128,768]{2,1,0:T(8,128)(2,1)}), bf16[8,128,768]{2,1,0:T(8,128)(2,1)S(1)}, u32[]{:S(2)}, u32[]{:S(2)}) %all-to-all-start.1) | async-done | bytes 1572896 | tf_op jit(solution)/shard_map/all_to_all | solution.py:1133
  283.7 39.3 %expert_back_in.1 = (bf16[1024,768]{1,0:T(8,128)(2,1)}, bf16[1024,2048]{1,0:T(8,128)(2,1)}, bf16[1024,2048]{1,0:T(8,128)(2,1)}, bf16[1024,2048]{1,0:T(8,128)(2,1)}) custom-call(bf16[1024,768]{1,0:T(8,128)(2,1)} %bitcast.93, bf16[1024,768]{1,0:T(8,128)(2,1)} %bitcast.95, bf16[4,3,192,2048]{3,2,1,0:T(8,128)(2,1)} %bitcast.121), custom_call_target="tpu_custom_call" | custom-call | flops 16106127360 | bytes 18874368 | tf_op jit(solution)/shard_map/expert_back_in/pallas_call | solution.py:688
  324.1 12.4 %mixture.1 = (bf16[512,768]{1,0:T(8,128)(2,1)}, f32[512,768]{1,0:T(8,128)}, f32[512,128]{1,0:T(8,128)}, f32[768,128]{1,0:T(8,128)}) custom-call(f32[512,768]{1,0:T(8,128)} %get-tuple-element.133.h_ref, bf16[512,768]{1,0:T(8,128)(2,1)} %bitcast.78, f32[512,128]{1,0:T(8,128)} %get-tuple-element.135.pr_ref, s32[512,2]{1,0:T(8,128)} %bitcast.82, ...), custom_call_target="tpu_custom_call" | custom-call | flops 1610612736 | bytes 4718592 | tf_op jit(solution)/shard_map/mixture/pallas_call | solution.py:808
  336.5 17.3 %expert_weight_grads.1 = bf16[4,3,192,2048]{3,2,1,0:T(8,128)(2,1)} custom-call(bf16[1024,768]{1,0:T(8,128)(2,1)} %bitcast.94, bf16[1024,768]{1,0:T(8,128)(2,1)} %bitcast.96, bf16[1024,2048]{1,0:T(8,128)(2,1)} %get-tuple-element.194.act_ref, bf16[1024,2048]{1,0:T(8,128)(2,1)} %get-tuple-element.195.dg_ref, bf16[1024,2048]{1,0:T(8,128)(2,1)} %get-tuple-element.196.du_ref), custom_call_target="tpu_custom_call" | custom-call | flops 9663676416 | bytes 18874368 | tf_op jit(solution)/shard_map/expert_weight_grads/pallas_call | solution.py:721
  353.9 6.0 all-to-all-start.3
  359.9 36.5 %all-to-all-done.3 = bf16[8,128,768]{2,1,0:T(8,128)(2,1)S(1)} async-done(((bf16[8,128,768]{2,1,0:T(8,128)(2,1)}), bf16[8,128,768]{2,1,0:T(8,128)(2,1)S(1)}, u32[]{:S(2)}, u32[]{:S(2)}) %all-to-all-start.3) | async-done | bytes 1572896 | tf_op jit(solution)/shard_map/all_to_all | solution.py:1133
  397.6 8.9 %norm_two_back.1 = (f32[512,768]{1,0:T(8,128)}, bf16[512,768]{1,0:T(8,128)(2,1)}, bf16[768,512]{1,0:T(8,128)(2,1)}, f32[768,768]{1,0:T(8,128)}, f32[8,768]{1,0:T(8,128)}) custom-call(f32[512,768]{1,0:T(8,128)} %get-tuple-element.133.h_ref, bf16[512,768]{1,0:T(8,128)(2,1)} %bitcast.79, f32[512,768]{1,0:T(8,128)} %get-tuple-element.141.gn_ref, ...), custom_call_target="tpu_custom_call" | custom-call | flops 2013265920 | bytes 6291456 | tf_op jit(solution)/shard_map/norm_two_back/pallas_call | solution.py:862
  407.6 8.3 %attend_back_remote.4 = (f32[768,512]{1,0:T(8,128)}, bf16[256,768]{1,0:T(8,128)(2,1)}, bf16[256,768]{1,0:T(8,128)(2,1)}, f32[48,512]{1,0:T(8,128)}) custom-call(s32[12]{0:T(128)} %concatenate.59.sc_ref, bf16[768,512]{1,0:T(8,128)(2,1)} %get-tuple-element.111.qt_ref, bf16[512,768]{1,0:T(8,128)(2,1)} %get-tuple-element.112.q_ref, ...), custom_call_target="tpu_custom_call" | custom-call | flops 4026531840 | bytes 7864320 | tf_op jit(solution)/shard_map/attend_back_remote/pallas_call | solution.py:487
  420.4 11.0 %attend_back_remote.5 = (f32[768,512]{1,0:T(8,128)}, f32[256,1536]{1,0:T(8,128)}, f32[256,1536]{1,0:T(8,128)}) custom-call(s32[12]{0:T(128)} %concatenate.59.sc_ref, bf16[768,512]{1,0:T(8,128)(2,1)} %get-tuple-element.111.qt_ref, bf16[512,768]{1,0:T(8,128)(2,1)} %get-tuple-element.112.q_ref, bf16[768,512]{1,0:T(8,128)(2,1)} %get-tuple-element.143.dot_ref, ...), custom_call_target="tpu_custom_call" | custom-call | flops 8053063680 | bytes 9437184 | tf_op jit(solution)/shard_map/attend_back_remote/pallas_call | solution.py:487
  441.9 10.9 %attend_back_remote.6 = (f32[768,512]{1,0:T(8,128)}, f32[256,1536]{1,0:T(8,128)}, f32[256,1536]{1,0:T(8,128)}) custom-call(s32[12]{0:T(128)} %concatenate.59.sc_ref, bf16[768,512]{1,0:T(8,128)(2,1)} %get-tuple-element.111.qt_ref, bf16[512,768]{1,0:T(8,128)(2,1)} %get-tuple-element.112.q_ref, bf16[768,512]{1,0:T(8,128)(2,1)} %get-tuple-element.143.dot_ref, ...), custom_call_target="tpu_custom_call" | custom-call | flops 8053063680 | bytes 9437184 | tf_op jit(solution)/shard_map/attend_back_remote/pallas_call | solution.py:487
  456.5 6.1 collective-permute-done.11
  464.5 6.1 collective-permute-start.15
  472.0 10.9 %attend_back_remote.7 = (f32[768,512]{1,0:T(8,128)}, f32[256,1536]{1,0:T(8,128)}, f32[256,1536]{1,0:T(8,128)}) custom-call(s32[12]{0:T(128)} %concatenate.59.sc_ref, bf16[768,512]{1,0:T(8,128)(2,1)} %get-tuple-element.111.qt_ref, bf16[512,768]{1,0:T(8,128)(2,1)} %get-tuple-element.112.q_ref, bf16[768,512]{1,0:T(8,128)(2,1)} %get-tuple-element.143.dot_ref, ...), custom_call_target="tpu_custom_call" | custom-call | flops 8053063680 | bytes 9437184 | tf_op jit(solution)/shard_map/attend_back_remote/pallas_call | solution.py:487
  494.9 12.2 %attend_back_local.1 = (f32[512,768]{1,0:T(8,128)}, f32[256,1536]{1,0:T(8,128)}, f32[256,1536]{1,0:T(8,128)}) custom-call(s32[12]{0:T(128)} %concatenate.59.sc_ref, bf16[768,512]{1,0:T(8,128)(2,1)} %get-tuple-element.111.qt_ref, bf16[512,768]{1,0:T(8,128)(2,1)} %get-tuple-element.112.q_ref, bf16[768,512]{1,0:T(8,128)(2,1)} %get-tuple-element.143.dot_ref, ...), custom_call_target="tpu_custom_call" | custom-call | flops 4026531840 | bytes 6291456 | tf_op jit(solution)/shard_map/attend_back_local/pallas_call | solution.py:458
  507.2 7.8 %q_back.1 = (f32[512,768]{1,0:T(8,128)}, bf16[2,192,768]{2,1,0:T(8,128)(2,1)}, f32[2,192,768]{2,1,0:T(8,128)}) custom-call(s32[12]{0:T(128)} %concatenate.59.sc_ref, bf16[512,768]{1,0:T(8,128)(2,1)} %get-tuple-element.110.n_ref, f32[512,768]{1,0:T(8,128)} %get-tuple-element.181.dq_ref, f32[512,128]{1,0:T(8,128)} %pad_maximum_fusion.3.c_ref, ...), custom_call_target="tpu_custom_call" | custom-call | flops 1207959552 | bytes 4718592 | tf_op jit(solution)/shard_map/q_back/pallas_call | solution.py:939
  520.9 14.5 %collective-permute-done.18.refs_0_ = bf16[256,1536]{1,0:T(8,128)(2,1)} collective-permute-done((bf16[256,1536]{1,0:T(8,128)(2,1)}, bf16[256,1536]{1,0:T(8,128)(2,1)}, u32[]{:S(2)}, u32[]{:S(2)}) %collective-permute-start.18) | collective-permute-done | bytes 786464 | tf_op jit(solution)/shard_map/ppermute | solution.py:1041
  535.5 13.7 %kv_back.1 = (f32[512,768]{1,0:T(8,128)}, bf16[2,192,1536]{2,1,0:T(8,128)(2,1)}, f32[2,192,1536]{2,1,0:T(8,128)}) custom-call(s32[12]{0:T(128)} %concatenate.59.sc_ref, bf16[512,768]{1,0:T(8,128)(2,1)} %bitcast.74, bf16[512,768]{1,0:T(8,128)(2,1)} %get-tuple-element.110.n_ref, f32[512,768]{1,0:T(8,128)} %get-tuple-element.182.gnq_ref, ...), custom_call_target="tpu_custom_call" | custom-call | flops 2415919104 | bytes 9437184 | tf_op jit(solution)/shard_map/kv_back/pallas_call | solution.py:992
  551.3 6.9 %all-to-all-start.4 = ((bf16[8,24,1664]{2,1,0:T(8,128)(2,1)}), bf16[8,24,1664]{2,1,0:T(8,128)(2,1)S(1)}, u32[]{:S(2)}, u32[]{:S(2)}) async-start(bf16[8,24,1664]{2,1,0:T(8,128)(2,1)} %fusion.1), calls=%async_computation.5 | async-start | bytes 1277952 | tf_op jit(solution)/shard_map/all_to_all | solution.py:1063
  580.2 5.7 all-to-all-start.5
  594.1 6.9 %all-to-all-done.5 = bf16[8,24,1536]{2,1,0:T(8,128)(2,1)S(1)} async-done(((bf16[8,24,1536]{2,1,0:T(8,128)(2,1)}), bf16[8,24,1536]{2,1,0:T(8,128)(2,1)S(1)}, u32[]{:S(2)}, u32[]{:S(2)}) %all-to-all-start.5) | async-done | bytes 589856 | tf_op jit(solution)/shard_map/all_to_all | solution.py:1063
  (198 shorter events, 136.3 us)
Async XLA Ops:
  7.2 72.7 %all-gather.4.cloned.1.call-start = ((), (), s32[]{:S(2)}) async-start(), calls=%async_computation.7 | async-start | bytes 5068800 | tf_op jit(solution)/shard_map/all_gather | solution.py:1099
  12.7 227.9 %all-gather.6.cloned.1.call-start = ((), (), s32[]{:S(2)}) async-start(), calls=%async_computation.9 | async-start | bytes 11796480 | tf_op jit(solution)/shard_map/all_gather | solution.py:1163
  91.1 20.0 %collective-permute-start.1 = (bf16[256,1536]{1,0:T(8,128)(2,1)}, bf16[256,1536]{1,0:T(8,128)(2,1)S(1)}, u32[]{:S(2)}, u32[]{:S(2)}) collective-permute-start(bf16[256,1536]{1,0:T(8,128)(2,1)} %get-tuple-element.113.kv_ref), channel_id=1, source_target_pairs={{0,1},{2,0},{4,2},{6,4},{7,6},{5,7},{3,5},{1,3},{8,9},{10,8},{12,1... | collective-permute-start | bytes 2359304 | tf_op jit(solution)/shard_map/ppermute | solution.py:1041
  92.5 19.7 %collective-permute-start = (bf16[256,1536]{1,0:T(8,128)(2,1)}, bf16[256,1536]{1,0:T(8,128)(2,1)S(1)}, u32[]{:S(2)}, u32[]{:S(2)}) collective-permute-start(bf16[256,1536]{1,0:T(8,128)(2,1)} %get-tuple-element.113.kv_ref), channel_id=1, source_target_pairs={{0,2},{2,4},{4,6},{6,7},{7,5},{5,3},{3,1},{1,0},{8,10},{10,12},{12... | collective-permute-start | bytes 2359304 | tf_op jit(solution)/shard_map/ppermute | solution.py:1041
  112.2 18.7 %collective-permute-start.2 = (bf16[256,1536]{1,0:T(8,128)(2,1)S(1)}, bf16[256,1536]{1,0:T(8,128)(2,1)S(1)}, u32[]{:S(2)}, u32[]{:S(2)}) collective-permute-start(bf16[256,1536]{1,0:T(8,128)(2,1)S(1)} %collective-permute-done.refs_0_.refs_1_), channel_id=1, source_target_pairs={{0,2},{2,4},{4,6},{6,7},{7,5},{5,3},{3,1},{1,0},{8,10},{10,12},{12... | collective-permute-start | bytes 2359304 | tf_op jit(solution)/shard_map/ppermute | solution.py:1041
  112.8 18.5 %collective-permute-start.3 = (bf16[256,1536]{1,0:T(8,128)(2,1)S(1)}, bf16[256,1536]{1,0:T(8,128)(2,1)}, u32[]{:S(2)}, u32[]{:S(2)}) collective-permute-start(bf16[256,1536]{1,0:T(8,128)(2,1)S(1)} %collective-permute-done.1.refs_1_.refs_0_), channel_id=1, source_target_pairs={{0,1},{2,0},{4,2},{6,4},{7,6},{5,7},{3,5},{1,3},{8,9},{10,8},{12,1... | collective-permute-start | bytes 2359304 | tf_op jit(solution)/shard_map/ppermute | solution.py:1041
  131.7 18.2 %collective-permute-start.4 = (bf16[256,1536]{1,0:T(8,128)(2,1)}, bf16[256,1536]{1,0:T(8,128)(2,1)S(1)}, u32[]{:S(2)}, u32[]{:S(2)}) collective-permute-start(bf16[256,1536]{1,0:T(8,128)(2,1)} %copy-done.27), channel_id=1, source_target_pairs={{0,2},{2,4},{4,6},{6,7},{7,5},{5,3},{3,1},{1,0},{8,10},{10,12},{12... | collective-permute-start | bytes 2359304 | tf_op jit(solution)/shard_map/ppermute | solution.py:1041
  132.6 17.5 %collective-permute-start.5 = (bf16[256,1536]{1,0:T(8,128)(2,1)}, bf16[256,1536]{1,0:T(8,128)(2,1)S(1)}, u32[]{:S(2)}, u32[]{:S(2)}) collective-permute-start(bf16[256,1536]{1,0:T(8,128)(2,1)} %collective-permute-done.3.refs_1_.refs_0_), channel_id=1, source_target_pairs={{0,1},{2,0},{4,2},{6,4},{7,6},{5,7},{3,5},{1,3},{8,9},{10,8},{12,1... | collective-permute-start | bytes 2359304 | tf_op jit(solution)/shard_map/ppermute | solution.py:1041
  133.9 20.4 %copy-start = (s32[2,256,2]{2,1,0:T(8,128)}, s32[2,256,2]{2,1,0:T(8,128)S(1)}, u32[]{:S(2)}) copy-start(s32[2,256,2]{2,1,0:T(8,128)S(1)} %copy.139) | copy-start | bytes 12292
  152.1 14.6 %collective-permute-start.7 = (bf16[256,768]{1,0:T(8,128)(2,1)S(1)}, bf16[256,768]{1,0:T(8,128)(2,1)}, u32[]{:S(2)}, u32[]{:S(2)}) collective-permute-start(bf16[256,768]{1,0:T(8,128)(2,1)S(1)} %slice.85), channel_id=1, source_target_pairs={{0,1},{2,0},{4,2},{6,4},{7,6},{5,7},{3,5},{1,3},{8,9},{10,8},{12,1... | collective-permute-start | bytes 1179656 | tf_op jit(solution)/shard_map/ppermute | solution.py:1041
  153.6 13.0 %collective-permute-start.6 = (bf16[256,768]{1,0:T(8,128)(2,1)S(1)}, bf16[256,768]{1,0:T(8,128)(2,1)}, u32[]{:S(2)}, u32[]{:S(2)}) collective-permute-start(bf16[256,768]{1,0:T(8,128)(2,1)S(1)} %slice.84), channel_id=1, source_target_pairs={{0,2},{2,4},{4,6},{6,7},{7,5},{5,3},{3,1},{1,0},{8,10},{10,12},{12... | collective-permute-start | bytes 1179656 | tf_op jit(solution)/shard_map/ppermute | solution.py:1041
  183.5 52.4 %all-to-all-start = ((bf16[8,128,768]{2,1,0:T(8,128)(2,1)}), bf16[8,128,768]{2,1,0:T(8,128)(2,1)S(1)}, u32[]{:S(2)}, u32[]{:S(2)}) async-start(bf16[8,128,768]{2,1,0:T(8,128)(2,1)} %bitcast.100), calls=%async_computation | async-start | bytes 3145728 | tf_op jit(solution)/shard_map/all_to_all | solution.py:1133
  237.0 40.6 %all-to-all-start.1 = ((bf16[8,128,768]{2,1,0:T(8,128)(2,1)}), bf16[8,128,768]{2,1,0:T(8,128)(2,1)S(1)}, u32[]{:S(2)}, u32[]{:S(2)}) async-start(bf16[8,128,768]{2,1,0:T(8,128)(2,1)} %bitcast.99), calls=%async_computation.1 | async-start | bytes 3145728 | tf_op jit(solution)/shard_map/all_to_all | solution.py:1133
  278.7 44.3 %all-to-all-start.2 = ((bf16[8,128,768]{2,1,0:T(8,128)(2,1)}), bf16[8,128,768]{2,1,0:T(8,128)(2,1)S(1)}, u32[]{:S(2)}, u32[]{:S(2)}) async-start(bf16[8,128,768]{2,1,0:T(8,128)(2,1)} %bitcast.98), calls=%async_computation.2 | async-start | bytes 3145728 | tf_op jit(solution)/shard_map/all_to_all | solution.py:1133
  282.4 286.6 %reduce-scatter.2.cloned.1.call-start = ((), (), s32[]{:S(2)}) async-start(), calls=%async_computation.8 | async-start | bytes 11796480 | tf_op jit(solution)/shard_map/reduce_scatter | solution.py:1200
  353.9 42.6 %all-to-all-start.3 = ((bf16[8,128,768]{2,1,0:T(8,128)(2,1)}), bf16[8,128,768]{2,1,0:T(8,128)(2,1)S(1)}, u32[]{:S(2)}, u32[]{:S(2)}) async-start(bf16[8,128,768]{2,1,0:T(8,128)(2,1)} %bitcast.28), calls=%async_computation.3 | async-start | bytes 3145728 | tf_op jit(solution)/shard_map/all_to_all | solution.py:1133
  415.8 15.6 %collective-permute-start.8 = (bf16[256,768]{1,0:T(8,128)(2,1)}, bf16[256,768]{1,0:T(8,128)(2,1)}, u32[]{:S(2)}, u32[]{:S(2)}) collective-permute-start(bf16[256,768]{1,0:T(8,128)(2,1)} %get-tuple-element.148), channel_id=1, source_target_pairs={{0,2},{2,4},{4,6},{6,7},{7,5},{5,3},{3,1},{1,0},{8,10},{10,12},{12... | collective-permute-start | bytes 1179656 | tf_op jit(solution)/shard_map/ppermute | solution.py:1041
  415.9 15.5 %collective-permute-start.9 = (bf16[256,768]{1,0:T(8,128)(2,1)}, bf16[256,768]{1,0:T(8,128)(2,1)}, u32[]{:S(2)}, u32[]{:S(2)}) collective-permute-start(bf16[256,768]{1,0:T(8,128)(2,1)} %get-tuple-element.149), channel_id=1, source_target_pairs={{0,1},{2,0},{4,2},{6,4},{7,6},{5,7},{3,5},{1,3},{8,9},{10,8},{12,1... | collective-permute-start | bytes 1179656 | tf_op jit(solution)/shard_map/ppermute | solution.py:1041
  420.3 11.1 %collective-permute-start.10 = (bf16[2,192,896]{2,1,0:T(8,128)(2,1)S(1)}, bf16[2,192,896]{2,1,0:T(8,128)(2,1)S(1)}, u32[]{:S(2)}, u32[]{:S(2)}) collective-permute-start(bf16[2,192,896]{2,1,0:T(8,128)(2,1)S(1)} %fusion.5), channel_id=1, source_target_pairs={{0,8},{8,0},{16,24},{24,16},{1,9},{9,1},{17,25},{25,17},{2,10},{10... | collective-permute-start | bytes 2064392 | tf_op jit(solution)/shard_map/ppermute | solution.py:1049
  436.3 20.2 %collective-permute-start.12 = (bf16[256,1536]{1,0:T(8,128)(2,1)}, bf16[256,1536]{1,0:T(8,128)(2,1)}, u32[]{:S(2)}, u32[]{:S(2)}) collective-permute-start(bf16[256,1536]{1,0:T(8,128)(2,1)} %pad_maximum_fusion.2), channel_id=1, source_target_pairs={{0,1},{2,0},{4,2},{6,4},{7,6},{5,7},{3,5},{1,3},{8,9},{10,8},{12,1... | collective-permute-start | bytes 2359304 | tf_op jit(solution)/shard_map/ppermute | solution.py:1041
  439.8 22.8 %collective-permute-start.11 = (bf16[256,1536]{1,0:T(8,128)(2,1)}, bf16[256,1536]{1,0:T(8,128)(2,1)}, u32[]{:S(2)}, u32[]{:S(2)}) collective-permute-start(bf16[256,1536]{1,0:T(8,128)(2,1)} %pad_maximum_fusion.1), channel_id=1, source_target_pairs={{0,2},{2,4},{4,6},{6,7},{7,5},{5,3},{3,1},{1,0},{8,10},{10,12},{12... | collective-permute-start | bytes 2359304 | tf_op jit(solution)/shard_map/ppermute | solution.py:1041
  440.6 12.2 %collective-permute-start.13 = (bf16[192,896]{1,0:T(8,128)(2,1)S(1)}, bf16[192,896]{1,0:T(8,128)(2,1)S(1)}, u32[]{:S(2)}, u32[]{:S(2)}) collective-permute-start(bf16[192,896]{1,0:T(8,128)(2,1)S(1)} %fusion.7), channel_id=1, source_target_pairs={{0,16},{16,0},{8,24},{24,8},{1,17},{17,1},{9,25},{25,9},{2,18},{18... | collective-permute-start | bytes 1032200 | tf_op jit(solution)/shard_map/ppermute | solution.py:1057
  464.5 22.7 %collective-permute-start.15 = (bf16[256,1536]{1,0:T(8,128)(2,1)S(1)}, bf16[256,1536]{1,0:T(8,128)(2,1)S(1)}, u32[]{:S(2)}, u32[]{:S(2)}) collective-permute-start(bf16[256,1536]{1,0:T(8,128)(2,1)S(1)} %add_convert_fusion.2), channel_id=1, source_target_pairs={{0,1},{2,0},{4,2},{6,4},{7,6},{5,7},{3,5},{1,3},{8,9},{10,8},{12,1... | collective-permute-start | bytes 2359304 | tf_op jit(solution)/shard_map/ppermute | solution.py:1041
  471.9 19.1 %collective-permute-start.14 = (bf16[256,1536]{1,0:T(8,128)(2,1)S(1)}, bf16[256,1536]{1,0:T(8,128)(2,1)}, u32[]{:S(2)}, u32[]{:S(2)}) collective-permute-start(bf16[256,1536]{1,0:T(8,128)(2,1)S(1)} %add_convert_fusion.3), channel_id=1, source_target_pairs={{0,2},{2,4},{4,6},{6,7},{7,5},{5,3},{3,1},{1,0},{8,10},{10,12},{12... | collective-permute-start | bytes 2359304 | tf_op jit(solution)/shard_map/ppermute | solution.py:1041
  515.0 2.3 collective-permute-start.16
  515.0 20.5 %collective-permute-start.18 = (bf16[256,1536]{1,0:T(8,128)(2,1)}, bf16[256,1536]{1,0:T(8,128)(2,1)}, u32[]{:S(2)}, u32[]{:S(2)}) collective-permute-start(bf16[256,1536]{1,0:T(8,128)(2,1)} %add_convert_fusion.1), channel_id=1, source_target_pairs={{0,2},{2,4},{4,6},{6,7},{7,5},{5,3},{3,1},{1,0},{8,10},{10,12},{12... | collective-permute-start | bytes 2359304 | tf_op jit(solution)/shard_map/ppermute | solution.py:1041
  515.4 20.1 %collective-permute-start.19 = (bf16[256,1536]{1,0:T(8,128)(2,1)}, bf16[256,1536]{1,0:T(8,128)(2,1)}, u32[]{:S(2)}, u32[]{:S(2)}) collective-permute-start(bf16[256,1536]{1,0:T(8,128)(2,1)} %add_convert_fusion), channel_id=1, source_target_pairs={{0,1},{2,0},{4,2},{6,4},{7,6},{5,7},{3,5},{1,3},{8,9},{10,8},{12,1... | collective-permute-start | bytes 2359304 | tf_op jit(solution)/shard_map/ppermute | solution.py:1041
  519.4 16.2 %collective-permute-start.17 = (bf16[192,768]{1,0:T(8,128)(2,1)}, bf16[192,768]{1,0:T(8,128)(2,1)}, u32[]{:S(2)}, u32[]{:S(2)}) collective-permute-start(bf16[192,768]{1,0:T(8,128)(2,1)} %fusion.8), channel_id=1, source_target_pairs={{0,16},{16,0},{8,24},{24,8},{1,17},{17,1},{9,25},{25,9},{2,18},{18... | collective-permute-start | bytes 884744 | tf_op jit(solution)/shard_map/ppermute | solution.py:1057
  549.2 8.9 %collective-permute-start.20 = (bf16[2,192,1536]{2,1,0:T(8,128)(2,1)}, bf16[2,192,1536]{2,1,0:T(8,128)(2,1)S(1)}, u32[]{:S(2)}, u32[]{:S(2)}) collective-permute-start(bf16[2,192,1536]{2,1,0:T(8,128)(2,1)} %get-tuple-element.193), channel_id=1, source_target_pairs={{0,8},{8,0},{16,24},{24,16},{1,9},{9,1},{17,25},{25,17},{2,10},{10... | collective-permute-start | bytes 3538952 | tf_op jit(solution)/shard_map/ppermute | solution.py:1049
  551.3 28.9 %all-to-all-start.4 = ((bf16[8,24,1664]{2,1,0:T(8,128)(2,1)}), bf16[8,24,1664]{2,1,0:T(8,128)(2,1)S(1)}, u32[]{:S(2)}, u32[]{:S(2)}) async-start(bf16[8,24,1664]{2,1,0:T(8,128)(2,1)} %fusion.1), calls=%async_computation.5 | async-start | bytes 1277952 | tf_op jit(solution)/shard_map/all_to_all | solution.py:1063
  562.4 15.8 %collective-permute-start.21 = (bf16[192,1536]{1,0:T(8,128)(2,1)}, bf16[192,1536]{1,0:T(8,128)(2,1)}, u32[]{:S(2)}, u32[]{:S(2)}) collective-permute-start(bf16[192,1536]{1,0:T(8,128)(2,1)} %fusion.6), channel_id=1, source_target_pairs={{0,16},{16,0},{8,24},{24,8},{1,17},{17,1},{9,25},{25,9},{2,18},{18... | collective-permute-start | bytes 1769480 | tf_op jit(solution)/shard_map/ppermute | solution.py:1057
  580.2 20.9 %all-to-all-start.5 = ((bf16[8,24,1536]{2,1,0:T(8,128)(2,1)}), bf16[8,24,1536]{2,1,0:T(8,128)(2,1)S(1)}, u32[]{:S(2)}, u32[]{:S(2)}) async-start(bf16[8,24,1536]{2,1,0:T(8,128)(2,1)} %bitcast.89), calls=%async_computation.6 | async-start | bytes 1179648 | tf_op jit(solution)/shard_map/all_to_all | solution.py:1063
  (28 other events, 149.8 us)
Sparse Core Ops, SparseCore 0:
  12.8 67.0 all-gather.3
  81.5 62.5 all-gather.5
  354.0 79.1 reduce-scatter.1
where the time goes:
time: 618 us; the launch traced here: 609 us
  Pallas kernels  243 us (39%)
  waiting for transfers between devices  205 us (33%)
  starting transfers between devices  68.3 us (11%)
  local copies, waits for them, and re-layouts  43.2 us (7%)
  other arithmetic  35 us (6%)
  between operations  14.4 us (2%)
    all_to_all x4, waiting for transfers between devices, exchange(): lax.all_to_all(rows, 'expert', split_axis=0, concat_axis=0, tiled=True)  85 us
    all_gather x1, waiting for transfers between devices, per_device(): lax.all_gather(jnp.concatenate([qkv_weight, out_weight, small], axis=1),...  58.9 us
    ppermute x16, waiting for transfers between devices, along_ring(): return lax.ppermute(array, 'expert', pairs)  49 us
    pallas_call x4, Pallas kernels, bwd_remote(): pl.pallas_call(functools.partial(bwd_remote_body, tuple(offsets), len(kvs...  41.1 us
    pallas_call x1, Pallas kernels, expert_in(): pl.pallas_call(expert_in_body, grid=(wide // part,), in_specs=[whole((row...  39.3 us
    pallas_call x4, Pallas kernels, fwd_remote(): pl.pallas_call(functools.partial(fwd_remote_body, tuple(offsets), len(kvs...  37.3 us
    all_to_all x4, starting transfers between devices, exchange(): lax.all_to_all(rows, 'expert', split_axis=0, concat_axis=0, tiled=True)  30.6 us
    ppermute x16, starting transfers between devices, along_ring(): return lax.ppermute(array, 'expert', pairs)  21.2 us
  transfers between devices with their start and end apart: 31, of which 18 were waited for; matrix products, arithmetic and copies ran while one was open for 10% of the time, Pallas kernels for 35%

commit v1 on v0

--- a/solution.py
+++ b/solution.py
@@ -15,7 +15,6 @@
 CONT_LEN = 256
 PROMPT = 2048
 LANES = 128
-ROW_TILE = 512
 EPS = 1e-06
 NEG = -1e30
 LOG2E = 1.4426950408889634
@@ -221,14 +220,14 @@
             attend_update(qz, kv[:, :LANES], kv[:, LANES:].T, lo, hi, mask, st_ref, a_ref, False)
 
         if r % LANES == 0:
-            if count != len(offsets) and not halves:
-                pl.when(block != me)(lambda: go(r, t, None))
-            else:
-                go(r, t, None)
 
             @pl.when(block < me)
             def _():
-                go(0, r, None)
+                go(0, t, None)
+
+            @pl.when(block > me)
+            def _():
+                go(r, t, None)
 
         else:
 
@@ -367,7 +366,6 @@
     src, refs = refs[0], refs[1:]
     dq_ref, refs = refs[0], refs[1:]
     out_refs, refs = refs[:count], refs[count:]
-    sum_ref = refs[-1]
     if first:
         st_ref, refs = refs[0], refs[1:]
         st_ref[...] = st_in[...]
@@ -402,7 +400,7 @@
     for j, offset in enumerate(offsets):
         block = sc_ref[3 + offset]
 
-        def go(lo, hi, mask, add):
+        def go(lo, mask):
             if halves:
                 kv = halves_value(*kv_refs)
             elif split:
@@ -410,36 +408,60 @@
             else:
                 kv = kv_refs[j][...]
             kb = kv[:, :LANES]
-            dk, dv = back_block(ops, kb, kv[:, LANES:], kb.T, lo, hi, mask, dq_ref)
-            if add:
-                dk, dv = dk + sum_ref[:, :LANES], dv + sum_ref[:, LANES:]
-            sum_ref[:, :LANES] = dk
-            sum_ref[:, LANES:] = dv
+            dk, dv = back_block(ops, kb, kv[:, LANES:], kb.T, lo, t, mask, dq_ref)
+            store(j, (dk * SCALE).astype(dtype), dv.astype(dtype))
 
         if split:
 
             @pl.when(block == me)
             def _():
-                sum_ref[...] = jnp.zeros_like(sum_ref)
+                zero = jnp.zeros((r, LANES), dtype)
+                store(j, zero, zero)
 
         if r % LANES == 0:
-            if split:
-                pl.when(block != me)(lambda: go(r, t, None, False))
-            else:
-                go(r, t, None, False)
 
             @pl.when(block < me)
             def _():
-                go(0, r, None, True)
+                go(0, None)
+
+            @pl.when(block > me)
+            def _():
+                go(r, None)
 
         else:
 
             @pl.when(block != me)
             def _():
                 col = lax.broadcasted_iota(jnp.int32, (r, t), 1)
-                go(0, t, (col >= r) | (block < me), False)
-
-        store(j, (sum_ref[:, :LANES] * SCALE).astype(dtype), sum_ref[:, LANES:].astype(dtype))
+                go(0, (col >= r) | (block < me))
+
+
+def ring_add_body(half, pr_ref, gr_ref, pl_ref, gl_ref, sr_ref, sl_ref):
+    if not half:
+        sr_ref[...] = (pr_ref[...] + gr_ref[...].astype(F32)).astype(BF16)
+        sl_ref[...] = (pl_ref[...] + gl_ref[...].astype(F32)).astype(BF16)
+        return
+    sr_ref[:, :D] = (pr_ref[:, :D] + gr_ref[...].astype(F32)).astype(BF16)
+    sr_ref[:, D:] = pr_ref[:, D:].astype(BF16)
+    sl_ref[:, :D] = pl_ref[:, :D].astype(BF16)
+    sl_ref[:, D:] = (pl_ref[:, D:] + gl_ref[...].astype(F32)).astype(BF16)
+
+
+def ring_add(part_r, got_r, part_l, got_l):
+    r = part_r.shape[0]
+    part = r // 2
+    half = got_r.shape[1] == D
+    wide = spec((part, 2 * D), lambda i: (i, 0))
+    got = spec((part, got_r.shape[1]), lambda i: (i, 0))
+    return pl.pallas_call(
+        functools.partial(ring_add_body, half),
+        grid=(2,),
+        in_specs=[wide, got, wide, got],
+        out_specs=[wide, wide],
+        out_shape=[shape((r, 2 * D), BF16)] * 2,
+        name="ring_add",
+        **params((4 * r * D, 16 * r * D)),
+    )(part_r, got_r, part_l, got_l)
 
 
 def q_specs(t):
@@ -493,7 +515,6 @@
         + [spec((LANES, t), lambda i: (i, 0))],
         out_specs=out_specs,
         out_shape=out_shape,
-        scratch_shapes=[pltpu.VMEM((t // 2, 2 * LANES), F32)],
         name="attend_back_remote",
         **params((10 * 4 * t * rows * D, 16 * D * t + 8 * D * rows)),
     )(sc, qt, q, do_t, do, st, *kvs, src)
@@ -604,7 +625,7 @@
     )(x, att, pack, pack, gain, res, rt, tr)
 
 
-def expert_fwd_body(x_ref, w_ref, o_ref, acc_ref):
+def expert_fwd_body(x_ref, w_ref, o_ref, gate_ref, up_ref, acc_ref):
     step = pl.program_id(0)
     x = x_ref[...]
     wide = w_ref.shape[-1]
@@ -613,6 +634,8 @@
     wd = w_ref[:, 2].reshape(D, wide)
     gate = dot(x, wg)
     up = dot(x, wu)
+    gate_ref[...] = gate
+    up_ref[...] = up
     act = (gate / (1.0 + jnp.exp(-gate)) * up).astype(BF16)
     out = dot_nt(act, wd)
 
@@ -637,67 +660,62 @@
         expert_fwd_body,
         grid=(wide // part,),
         in_specs=[whole((rows, D)), spec((shards, 3, per, part), lambda i: (0, 0, 0, i))],
-        out_specs=whole((rows, D)),
-        out_shape=shape((rows, D), BF16),
+        out_specs=[whole((rows, D))] + [spec((rows, part), lambda i: (0, i))] * 2,
+        out_shape=[shape((rows, D), BF16)] + [shape((rows, wide), F32)] * 2,
         scratch_shapes=[pltpu.VMEM((rows, D), F32)],
         name="expert_forward",
         **params((6 * rows * D * wide, 6 * D * wide)),
     )(xr, w)
 
 
-def expert_in_body(x_ref, g_ref, w_ref, gi_ref, act_ref, dg_ref, du_ref, acc_ref):
+def expert_in_body(gate_ref, up_ref, g_ref, w_ref, gi_ref, act_ref, dg_ref, du_ref, acc_ref):
     step = pl.program_id(0)
     wide = w_ref.shape[-1]
     wg = w_ref[:, 0].reshape(D, wide)
     wu = w_ref[:, 1].reshape(D, wide)
     wd = w_ref[:, 2].reshape(D, wide)
-
-    @pl.loop(0, x_ref.shape[0] // ROW_TILE)
-    def _(i):
-        rows = pl.ds(pl.multiple_of(i * ROW_TILE, ROW_TILE), ROW_TILE)
-        gate = dot(x_ref[rows, :], wg)
-        up = dot(x_ref[rows, :], wu)
-        ga = dot(g_ref[rows, :], wd)
-        sig = 1.0 / (1.0 + jnp.exp(-gate))
-        silu = gate * sig
-        act_ref[rows, :] = (silu * up).astype(BF16)
-        d_gate = (ga * up * sig * (1.0 + gate * (1.0 - sig))).astype(BF16)
-        d_up = (ga * silu).astype(BF16)
-        dg_ref[rows, :] = d_gate
-        du_ref[rows, :] = d_up
-        gi = dot_nt(d_gate, wg) + dot_nt(d_up, wu)
-
-        @pl.when(step == 0)
-        def _():
-            acc_ref[rows, :] = gi
-
-        @pl.when(step > 0)
-        def _():
-            acc_ref[rows, :] += gi
+    gate = gate_ref[...]
+    up = up_ref[...]
+    ga = dot(g_ref[...], wd)
+    sig = 1.0 / (1.0 + jnp.exp(-gate))
+    silu = gate * sig
+    act_ref[...] = (silu * up).astype(BF16)
+    d_gate = (ga * up * sig * (1.0 + gate * (1.0 - sig))).astype(BF16)
+    d_up = (ga * silu).astype(BF16)
+    dg_ref[...] = d_gate
+    du_ref[...] = d_up
+    gi = dot_nt(
+        jnp.concatenate([d_gate, d_up], axis=1), jnp.concatenate([wg, wu], axis=1)
+    )
+
+    @pl.when(step == 0)
+    def _():
+        acc_ref[...] = gi
+
+    @pl.when(step > 0)
+    def _():
+        acc_ref[...] += gi
 
     @pl.when(step == pl.num_programs(0) - 1)
     def _():
         gi_ref[...] = acc_ref[...].astype(BF16)
 
 
-def expert_in(xr, gr, w):
-    rows = xr.shape[0]
+def expert_in(gate, up, gr, w):
+    rows = gr.shape[0]
     shards, _, per, wide = w.shape
     part = min(wide, 256)
     tile = spec((rows, part), lambda i: (0, i))
     return pl.pallas_call(
         expert_in_body,
         grid=(wide // part,),
-        in_specs=[
-            whole((rows, D)), whole((rows, D)),
-            spec((shards, 3, per, part), lambda i: (0, 0, 0, i)),
-        ],
+        in_specs=[tile, tile, whole((rows, D)), spec((shards, 3, per, part), lambda i: (0, 0, 0, i))],
         out_specs=[whole((rows, D)), tile, tile, tile],
         out_shape=[shape((rows, D), BF16)] + [shape((rows, wide), BF16)] * 3,
         scratch_shapes=[pltpu.VMEM((rows, D), F32)],
         name="expert_back_in",
-        **params((10 * rows * D * wide, 12 * D * wide)),
-    )(xr, gr, w)
+        **params((6 * rows * D * wide, 12 * D * wide)),
+    )(gate, up, gr, w)
 
 
 def expert_weights_body(x_ref, gl_ref, act_ref, dg_ref, du_ref, dw_ref, xt_ref, gt_ref):
@@ -1188,9 +1206,9 @@
     g_send = grad_rows_call(g, pr, target_rows, slots)
     x_got, g_send = tie(x_got, g_send)
     g_got = exchange(to_owners(g_send))
-    expert_rows = expert_fwd(x_got, weights)
+    expert_rows, gate_pre, up_pre = expert_fwd(x_got, weights)
     out_back = from_owners(expert_rows)
-    grad_in, act, d_gate, d_up = expert_in(x_got, g_got, weights)
+    grad_in, act, d_gate, d_up = expert_in(gate_pre, up_pre, g_got, weights)
     in_back = from_owners(grad_in)
     output, gn, grad_logits, grad_small = mix_call(
         hidden, g, pr, picked, target_cols, out_back, low_two, pack, rows_two
@@ -1199,7 +1217,9 @@
     grad_w = expert_weights(x_got, g_got, act, d_gate, d_up, weights.shape)
     grad_expert = lax.psum_scatter(
         grad_w.reshape(-1, grad_w.shape[-1]), "dp", scatter_dimension=0, tiled=True
-    ).astype(F32)
+    )
+    per = gate_weight.shape[0]
+    grad_expert = [grad_expert[i * per : (i + 1) * per].astype(F32) for i in range(3)]
     gh, d_att, d_att_t, grad_ow, gg_two = norm_back_call(
         hidden, g, gn, target_cols, in_back, rows_two, pack, att
     )
@@ -1227,13 +1247,9 @@
             got_r, got_l, part_r, part_l, dq_t, early_got = tie(
                 got_r, got_l, part_r, part_l, dq_t, early_got
             )
+            send_r, send_l = ring_add(part_r, got_r, part_l, got_l)
             if i == 3:
-                send_r = jnp.concatenate([part_r[:, :D] + got_r.astype(F32), part_r[:, D:]], axis=1)
-                send_l = jnp.concatenate([part_l[:, :D], part_l[:, D:] + got_l.astype(F32)], axis=1)
                 early_keep, early_got = add_and_cross(early_keep, early_got)
-            else:
-                send_r, send_l = part_r + got_r.astype(F32), part_l + got_l.astype(F32)
-            send_r, send_l = send_r.astype(BF16), send_l.astype(BF16)
         send_r, send_l, dq_t = tie(send_r, send_l, dq_t)
         got_r = along_ring(send_r, 1)
         got_l = along_ring(send_l, -1)
@@ -1252,20 +1268,22 @@
         )
     gn_q, *grad_q = q_back_call(sc, low_one, dq, cosine, sine, pack, ring)
     if ring:
-        keep_q, got_q = add_and_cross(grad_q[1], swap_core(grad_q[0]))
-        keep_q, got_q, got_0, got_1 = tie(keep_q, got_q, *got)
-        got = (got_0, got_1)
+        got_q = swap_core(grad_q[0])
+        keep_q, got_q = add_and_cross(grad_q[1], got_q)
+        keep_q, *got = tie(keep_q, *got)
     grad_input, *grad_kv = kv_back_call(
         sc, x, low_one, gn_q, gh, gain_one, cosine, sine, pack, dkv_own, dkv_cont, got, ring
     )
     output, grad_input = from_rows(output), from_rows(grad_input)
     if ring:
         got_kv = swap_core(grad_kv[0])
+        keep_kv, got_kv = add_and_cross(grad_kv[1], got_kv)
+        keep_kv, got_q, early_got = tie(keep_kv, got_q, early_got)
         got_q = add_and_scatter(
-            jnp.concatenate([early_keep, keep_q], axis=1), jnp.concatenate([early_got, got_q], axis=1)
+            jnp.concatenate([early_keep, keep_q], axis=1),
+            jnp.concatenate([early_got, got_q], axis=1),
         )
-        keep_kv, got_kv = add_and_cross(grad_kv[1], got_kv)
-        got_kv, grad_expert, output, grad_input = tie(got_kv, grad_expert, output, grad_input)
+        got_kv, output, grad_input, *grad_expert = tie(got_kv, output, grad_input, *grad_expert)
         summed = add_up(got_q)
         early, late_q = summed[:, : D + LANES], summed[:, D + LANES :]
         late_kv = add_up(add_and_scatter(keep_kv, got_kv))
@@ -1276,7 +1294,6 @@
     late = jnp.concatenate([late_q, late_kv.reshape(per, 2 * D)], axis=1)
     grad_gain = jnp.sum(late * qkv_weight.astype(F32), axis=1) / attn_gain.astype(F32)
     tail = early[:, D:]
-    per = grad_expert.shape[0] // 3
     return (
         output,
         grad_input,
@@ -1288,9 +1305,9 @@
         tail[:, :12],
         tail[:, 12:16],
         tail[:, 16:18],
-        grad_expert[:per],
-        grad_expert[per : 2 * per],
-        grad_expert[2 * per :],
+        grad_expert[0],
+        grad_expert[1],
+        grad_expert[2],
     )
 
 

time: 618 us -> 596 us (0.964)
  starting transfers between devices: 68.3 us -> 48.2 us
  waiting for transfers between devices: 205 us -> 222 us
  other arithmetic: 35 us -> 23.3 us
    all_to_all x4, starting transfers between devices: 30.6 us -> 16.7 us  [exchange(): lax.all_to_all(rows, 'expert', split_axis=0, concat_axis=0, tiled=True)]
    all_to_all x4, waiting for transfers between devices: 85 us -> 95 us  [exchange(): lax.all_to_all(rows, 'expert', split_axis=0, concat_axis=0, tiled=True)]
    convert_element_type x5 -> x1, other arithmetic: 11.6 us -> 3.96 us  [per_device(): grad_expert[i * per:(i + 1) * per].astype(F32)]
    slice x3 -> x0, local copies, waits for them, and re-layouts: 7.33 us -> none  [the longest x1 4.68 us: per_device(): grad_expert[2 * per:]]
    pallas_call x1 -> x4, Pallas kernels: 39.3 us -> 33.6 us  [the longest x1 23.7 us: expert_in(): pl.pallas_call(expert_in_body, grid=(wide // part,), in_specs=[tile, tile...]
    unnamed x65 -> x69, local copies, waits for them, and re-layouts: 12.5 us -> 14.2 us
  transfers between devices with their start and end apart: 31 -> 31, of which waited for: 18 -> 23; matrix products, arithmetic and copies ran while one was open for 10% -> 8% of each run, Pallas kernels for 35% -> 36%
where the time goes in v1:
time: 596 us; the launch traced here: 586 us
  Pallas kernels  241 us (40%)
  waiting for transfers between devices  222 us (37%)
  starting transfers between devices  48.2 us (8%)
  local copies, waits for them, and re-layouts  37.7 us (6%)
  other arithmetic  23.3 us (4%)
  between operations  14.5 us (2%)
    all_to_all x4, waiting for transfers between devices, exchange(): lax.all_to_all(rows, 'expert', split_axis=0, concat_axis=0, tiled=True)  95 us
    all_gather x1, waiting for transfers between devices, per_device(): lax.all_gather(jnp.concatenate([qkv_weight, out_weight, small], axis=1),...  58.7 us
    ppermute x16, waiting for transfers between devices, along_ring(): return lax.ppermute(array, 'expert', pairs)  46.6 us
    pallas_call x4, Pallas kernels, bwd_remote(): pl.pallas_call(functools.partial(bwd_remote_body, tuple(offsets), len(kvs...  41.7 us
    pallas_call x4, Pallas kernels, fwd_remote(): pl.pallas_call(functools.partial(fwd_remote_body, tuple(offsets), len(kvs...  38 us
    pallas_call x1, Pallas kernels, expert_in(): pl.pallas_call(expert_in_body, grid=(wide // part,), in_specs=[tile, tile...  23.7 us
    pallas_call x1, Pallas kernels, expert_fwd(): pl.pallas_call(expert_fwd_body, grid=(wide // part,), in_specs=[whole((ro...  19.1 us
    ppermute x16, starting transfers between devices, along_ring(): return lax.ppermute(array, 'expert', pairs)  18.6 us
  transfers between devices with their start and end apart: 31, of which 23 were waited for; matrix products, arithmetic and copies ran while one was open for 8% of the time, Pallas kernels for 36%

profile of v1, /device:TPU:0, one launch (start us, length us, event | category | flops | bytes accessed | tf_op | source)
XLA Modules:
  0.0 586.3 jit_solution(9664601255066579260)
XLA Ops:
  21.2 58.7 %all-gather.4.cloned.1.call-done.wq_ref.wk_ref.wv_ref.ow_ref.sw_ref.w_ref = bf16[768,3200]{1,0:T(8,128)(2,1)} async-done(((bf16[24,3200]{1,0:T(8,128)(2,1)}), bf16[768,3200]{1,0:T(8,128)(2,1)}) %all-gather.4.cloned.1.call-update) | async-done | bytes 4915216 | tf_op jit(solution)/shard_map/all_gather | solution.py:1117
  82.0 9.1 %qkv_rope.1 = (bf16[512,768]{1,0:T(8,128)(2,1)}, bf16[512,768]{1,0:T(8,128)(2,1)}, bf16[768,512]{1,0:T(8,128)(2,1)}, bf16[256,1536]{1,0:T(8,128)(2,1)}, bf16[256,1536]{1,0:T(8,128)(2,1)}) custom-call(bf16[512,768]{1,0:T(8,128)(2,1)} %bitcast.70, f32[1,768]{1,0:T(1,128)} %copy.137.gain_ref, ...), custom_call_target="tpu_custom_call" | custom-call | flops 1811939328 | bytes 3538944 | tf_op jit(solution)/shard_map/qkv_rope/pallas_call | solution.py:98
  95.6 12.4 %attend_local.1 = (f32[48,512]{1,0:T(8,128)}, f32[768,512]{1,0:T(8,128)}) custom-call(s32[12]{0:T(128)} %concatenate.51.sc_ref, bf16[768,512]{1,0:T(8,128)(2,1)} %get-tuple-element.124.qt_ref, bf16[256,1536]{1,0:T(8,128)(2,1)} %get-tuple-element.126.kv_ref, bf16[256,1536]{1,0:T(8,128)(2,1)} %get-tuple-element.127.kvo_ref), custom_call_target="tpu_custom_call" | custom-call | flops 1610612736 | bytes 1572864 | tf_op jit(solution)/shard_map/attend_local/pallas_call | solution.py:262
  114.2 10.2 %attend_remote.4 = (f32[48,512]{1,0:T(8,128)}, f32[768,512]{1,0:T(8,128)}) custom-call(s32[12]{0:T(128)} %concatenate.51.sc_ref, bf16[768,512]{1,0:T(8,128)(2,1)} %get-tuple-element.124.qt_ref, bf16[256,1536]{1,0:T(8,128)(2,1)} %copy-done.28, bf16[256,1536]{1,0:T(8,128)(2,1)} %copy-done.27, f32[48,512]{1,0:T(8,128)} %get-tuple-element.131.refs_2_, ...), custom_call_target="tpu_custom_call" | custom-call | flops 3221225472 | bytes 4718592 | tf_op jit(solution)/shard_map/attend_remote/pallas_call | solution.py:286
  124.4 6.5 %collective-permute-done.2.refs_0_.refs_1_ = bf16[256,1536]{1,0:T(8,128)(2,1)S(1)} collective-permute-done((bf16[256,1536]{1,0:T(8,128)(2,1)S(1)}, bf16[256,1536]{1,0:T(8,128)(2,1)S(1)}, u32[]{:S(2)}, u32[]{:S(2)}) %collective-permute-start.2) | collective-permute-done | bytes 786464 | tf_op jit(solution)/shard_map/ppermute | solution.py:1059
  134.8 10.2 %attend_remote.5 = (f32[48,512]{1,0:T(8,128)}, f32[768,512]{1,0:T(8,128)}) custom-call(s32[12]{0:T(128)} %concatenate.51.sc_ref, bf16[768,512]{1,0:T(8,128)(2,1)} %get-tuple-element.124.qt_ref, bf16[256,1536]{1,0:T(8,128)(2,1)} %copy-done.29, bf16[256,1536]{1,0:T(8,128)(2,1)} %collective-permute-done.3.refs_1_.refs_0_, ...), custom_call_target="tpu_custom_call" | custom-call | flops 3221225472 | bytes 4718592 | tf_op jit(solution)/shard_map/attend_remote/pallas_call | solution.py:286
  156.8 10.2 %attend_remote.6 = (f32[48,512]{1,0:T(8,128)}, f32[768,512]{1,0:T(8,128)}) custom-call(s32[12]{0:T(128)} %concatenate.51.sc_ref, bf16[768,512]{1,0:T(8,128)(2,1)} %get-tuple-element.124.qt_ref, bf16[256,1536]{1,0:T(8,128)(2,1)} %copy-done.21, bf16[256,1536]{1,0:T(8,128)(2,1)} %copy-done.22, f32[48,512]{1,0:T(8,128)} %get-tuple-element.141.refs_2_, ...), custom_call_target="tpu_custom_call" | custom-call | flops 3221225472 | bytes 4718592 | tf_op jit(solution)/shard_map/attend_remote/pallas_call | solution.py:286
  167.0 7.5 %attend_remote.7 = (f32[48,512]{1,0:T(8,128)}, f32[768,512]{1,0:T(8,128)}, bf16[512,768]{1,0:T(8,128)(2,1)}) custom-call(s32[12]{0:T(128)} %concatenate.51.sc_ref, bf16[768,512]{1,0:T(8,128)(2,1)} %get-tuple-element.124.qt_ref, bf16[256,768]{1,0:T(8,128)(2,1)} %collective-permute-done.6.refs_0_, bf16[256,768]{1,0:T(8,128)(2,1)} %collective-permute-done.7.refs_1_, ...), custom_call_target="tpu_custom_call" | custom-call | flops 1610612736 | bytes 3932160 | tf_op jit(solution)/shard_map/attend_remote/pallas_call | solution.py:286
  174.4 9.4 %route_dispatch.1 = (f32[512,768]{1,0:T(8,128)}, bf16[512,768]{1,0:T(8,128)(2,1)}, f32[512,128]{1,0:T(8,128)}, bf16[1024,768]{1,0:T(8,128)(2,1)}) custom-call(bf16[512,768]{1,0:T(8,128)(2,1)} %bitcast.71, bf16[512,768]{1,0:T(8,128)(2,1)} %get-tuple-element.145.att_ref, ...), custom_call_target="tpu_custom_call" | custom-call | flops 1409286144 | bytes 3145728 | tf_op jit(solution)/shard_map/route_dispatch/pallas_call | solution.py:608
  183.9 5.9 %all-to-all-start = ((bf16[8,128,768]{2,1,0:T(8,128)(2,1)}), bf16[8,128,768]{2,1,0:T(8,128)(2,1)S(1)}, u32[]{:S(2)}, u32[]{:S(2)}) async-start(bf16[8,128,768]{2,1,0:T(8,128)(2,1)} %bitcast.96), calls=%async_computation | async-start | bytes 3145728 | tf_op jit(solution)/shard_map/all_to_all | solution.py:1151
  195.6 28.2 %all-to-all-done = bf16[8,128,768]{2,1,0:T(8,128)(2,1)S(1)} async-done(((bf16[8,128,768]{2,1,0:T(8,128)(2,1)}), bf16[8,128,768]{2,1,0:T(8,128)(2,1)S(1)}, u32[]{:S(2)}, u32[]{:S(2)}) %all-to-all-start) | async-done | bytes 1572896 | tf_op jit(solution)/shard_map/all_to_all | solution.py:1151
  228.5 19.1 %expert_forward.1 = (bf16[1024,768]{1,0:T(8,128)(2,1)}, f32[1024,2048]{1,0:T(8,128)}, f32[1024,2048]{1,0:T(8,128)}) custom-call(bf16[1024,768]{1,0:T(8,128)(2,1)} %bitcast.89, bf16[4,3,192,2048]{3,2,1,0:T(8,128)(2,1)} %bitcast.117), custom_call_target="tpu_custom_call" | custom-call | flops 9663676416 | bytes 9437184 | tf_op jit(solution)/shard_map/expert_forward/pallas_call | solution.py:659
  247.6 17.6 %all-to-all-done.1 = bf16[8,128,768]{2,1,0:T(8,128)(2,1)S(1)} async-done(((bf16[8,128,768]{2,1,0:T(8,128)(2,1)}), bf16[8,128,768]{2,1,0:T(8,128)(2,1)S(1)}, u32[]{:S(2)}, u32[]{:S(2)}) %all-to-all-start.1) | async-done | bytes 1572896 | tf_op jit(solution)/shard_map/all_to_all | solution.py:1151
  271.3 23.7 %expert_back_in.1 = (bf16[1024,768]{1,0:T(8,128)(2,1)}, bf16[1024,2048]{1,0:T(8,128)(2,1)}, bf16[1024,2048]{1,0:T(8,128)(2,1)}, bf16[1024,2048]{1,0:T(8,128)(2,1)}) custom-call(f32[1024,2048]{1,0:T(8,128)} %get-tuple-element.150.gate_ref, f32[1024,2048]{1,0:T(8,128)} %get-tuple-element.151.up_ref, bf16[1024,768]{1,0:T(8,128)(2,1)} %bitcast.91, ...), custom_call_target="tpu_custom_call" | custom-call | flops 9663676416 | bytes 18874368 | tf_op jit(solution)/shard_map/expert_back_in/pallas_call | solution.py:709
  295.0 12.1 %all-to-all-done.2 = bf16[8,128,768]{2,1,0:T(8,128)(2,1)S(1)} async-done(((bf16[8,128,768]{2,1,0:T(8,128)(2,1)}), bf16[8,128,768]{2,1,0:T(8,128)(2,1)S(1)}, u32[]{:S(2)}, u32[]{:S(2)}) %all-to-all-start.2) | async-done | bytes 1572896 | tf_op jit(solution)/shard_map/all_to_all | solution.py:1151
  308.3 12.4 %mixture.1 = (bf16[512,768]{1,0:T(8,128)(2,1)}, f32[512,768]{1,0:T(8,128)}, f32[512,128]{1,0:T(8,128)}, f32[768,128]{1,0:T(8,128)}) custom-call(f32[512,768]{1,0:T(8,128)} %get-tuple-element.146.h_ref, bf16[512,768]{1,0:T(8,128)(2,1)} %bitcast.76, f32[512,128]{1,0:T(8,128)} %get-tuple-element.148.pr_ref, s32[512,2]{1,0:T(8,128)} %bitcast.80, ...), custom_call_target="tpu_custom_call" | custom-call | flops 1610612736 | bytes 4718592 | tf_op jit(solution)/shard_map/mixture/pallas_call | solution.py:826
  320.7 17.3 %expert_weight_grads.1 = bf16[4,3,192,2048]{3,2,1,0:T(8,128)(2,1)} custom-call(bf16[1024,768]{1,0:T(8,128)(2,1)} %bitcast.90, bf16[1024,768]{1,0:T(8,128)(2,1)} %bitcast.92, bf16[1024,2048]{1,0:T(8,128)(2,1)} %get-tuple-element.218.act_ref, bf16[1024,2048]{1,0:T(8,128)(2,1)} %get-tuple-element.219.dg_ref, bf16[1024,2048]{1,0:T(8,128)(2,1)} %get-tuple-element.220.du_ref), custom_call_target="tpu_custom_call" | custom-call | flops 9663676416 | bytes 18874368 | tf_op jit(solution)/shard_map/expert_weight_grads/pallas_call | solution.py:739
  341.7 37.1 %all-to-all-done.3 = bf16[8,128,768]{2,1,0:T(8,128)(2,1)S(1)} async-done(((bf16[8,128,768]{2,1,0:T(8,128)(2,1)}), bf16[8,128,768]{2,1,0:T(8,128)(2,1)S(1)}, u32[]{:S(2)}, u32[]{:S(2)}) %all-to-all-start.3) | async-done | bytes 1572896 | tf_op jit(solution)/shard_map/all_to_all | solution.py:1151
  380.0 8.9 %norm_two_back.1 = (f32[512,768]{1,0:T(8,128)}, bf16[512,768]{1,0:T(8,128)(2,1)}, bf16[768,512]{1,0:T(8,128)(2,1)}, f32[768,768]{1,0:T(8,128)}, f32[8,768]{1,0:T(8,128)}) custom-call(f32[512,768]{1,0:T(8,128)} %get-tuple-element.146.h_ref, bf16[512,768]{1,0:T(8,128)(2,1)} %bitcast.77, f32[512,768]{1,0:T(8,128)} %get-tuple-element.157.gn_ref, ...), custom_call_target="tpu_custom_call" | custom-call | flops 2013265920 | bytes 6291456 | tf_op jit(solution)/shard_map/norm_two_back/pallas_call | solution.py:880
  389.9 8.4 %attend_back_remote.4 = (f32[768,512]{1,0:T(8,128)}, bf16[256,768]{1,0:T(8,128)(2,1)}, bf16[256,768]{1,0:T(8,128)(2,1)}, f32[48,512]{1,0:T(8,128)}) custom-call(s32[12]{0:T(128)} %concatenate.51.sc_ref, bf16[768,512]{1,0:T(8,128)(2,1)} %get-tuple-element.124.qt_ref, bf16[512,768]{1,0:T(8,128)(2,1)} %get-tuple-element.125.q_ref, ...), custom_call_target="tpu_custom_call" | custom-call | flops 4026531840 | bytes 7864320 | tf_op jit(solution)/shard_map/attend_back_remote/pallas_call | solution.py:509
  403.0 11.1 %attend_back_remote.5 = (f32[768,512]{1,0:T(8,128)}, f32[256,1536]{1,0:T(8,128)}, f32[256,1536]{1,0:T(8,128)}) custom-call(s32[12]{0:T(128)} %concatenate.51.sc_ref, bf16[768,512]{1,0:T(8,128)(2,1)} %get-tuple-element.124.qt_ref, bf16[512,768]{1,0:T(8,128)(2,1)} %get-tuple-element.125.q_ref, bf16[768,512]{1,0:T(8,128)(2,1)} %get-tuple-element.159.dot_ref, ...), custom_call_target="tpu_custom_call" | custom-call | flops 8053063680 | bytes 9437184 | tf_op jit(solution)/shard_map/attend_back_remote/pallas_call | solution.py:509
  421.7 11.1 %attend_back_remote.6 = (f32[768,512]{1,0:T(8,128)}, f32[256,1536]{1,0:T(8,128)}, f32[256,1536]{1,0:T(8,128)}) custom-call(s32[12]{0:T(128)} %concatenate.51.sc_ref, bf16[768,512]{1,0:T(8,128)(2,1)} %get-tuple-element.124.qt_ref, bf16[512,768]{1,0:T(8,128)(2,1)} %get-tuple-element.125.q_ref, bf16[768,512]{1,0:T(8,128)(2,1)} %get-tuple-element.159.dot_ref, ...), custom_call_target="tpu_custom_call" | custom-call | flops 8053063680 | bytes 9437184 | tf_op jit(solution)/shard_map/attend_back_remote/pallas_call | solution.py:509
  432.8 5.0 collective-permute-done.11.gr_ref
  446.4 11.1 %attend_back_remote.7 = (f32[768,512]{1,0:T(8,128)}, f32[256,1536]{1,0:T(8,128)}, f32[256,1536]{1,0:T(8,128)}) custom-call(s32[12]{0:T(128)} %concatenate.51.sc_ref, bf16[768,512]{1,0:T(8,128)(2,1)} %get-tuple-element.124.qt_ref, bf16[512,768]{1,0:T(8,128)(2,1)} %get-tuple-element.125.q_ref, bf16[768,512]{1,0:T(8,128)(2,1)} %get-tuple-element.159.dot_ref, ...), custom_call_target="tpu_custom_call" | custom-call | flops 8053063680 | bytes 9437184 | tf_op jit(solution)/shard_map/attend_back_remote/pallas_call | solution.py:509
  457.5 5.6 collective-permute-done.14.gr_ref
  469.5 12.2 %attend_back_local.1 = (f32[512,768]{1,0:T(8,128)}, f32[256,1536]{1,0:T(8,128)}, f32[256,1536]{1,0:T(8,128)}) custom-call(s32[12]{0:T(128)} %concatenate.51.sc_ref, bf16[768,512]{1,0:T(8,128)(2,1)} %get-tuple-element.124.qt_ref, bf16[512,768]{1,0:T(8,128)(2,1)} %get-tuple-element.125.q_ref, bf16[768,512]{1,0:T(8,128)(2,1)} %get-tuple-element.159.dot_ref, ...), custom_call_target="tpu_custom_call" | custom-call | flops 4026531840 | bytes 6291456 | tf_op jit(solution)/shard_map/attend_back_local/pallas_call | solution.py:480
  481.8 7.8 %q_back.1 = (f32[512,768]{1,0:T(8,128)}, bf16[2,192,768]{2,1,0:T(8,128)(2,1)}, f32[2,192,768]{2,1,0:T(8,128)}) custom-call(s32[12]{0:T(128)} %concatenate.51.sc_ref, bf16[512,768]{1,0:T(8,128)(2,1)} %get-tuple-element.123.n_ref, f32[512,768]{1,0:T(8,128)} %get-tuple-element.203.dq_ref, f32[512,128]{1,0:T(8,128)} %pad_maximum_fusion.1.c_ref, ...), custom_call_target="tpu_custom_call" | custom-call | flops 1207959552 | bytes 4718592 | tf_op jit(solution)/shard_map/q_back/pallas_call | solution.py:957
  495.0 14.8 %collective-permute-done.17.refs_0_ = bf16[256,1536]{1,0:T(8,128)(2,1)S(1)} collective-permute-done((bf16[256,1536]{1,0:T(8,128)(2,1)}, bf16[256,1536]{1,0:T(8,128)(2,1)S(1)}, u32[]{:S(2)}, u32[]{:S(2)}) %collective-permute-start.17) | collective-permute-done | bytes 786464 | tf_op jit(solution)/shard_map/ppermute | solution.py:1059
  511.8 13.7 %kv_back.1 = (f32[512,768]{1,0:T(8,128)}, bf16[2,192,1536]{2,1,0:T(8,128)(2,1)}, f32[2,192,1536]{2,1,0:T(8,128)}) custom-call(s32[12]{0:T(128)} %concatenate.51.sc_ref, bf16[512,768]{1,0:T(8,128)(2,1)} %bitcast.72, bf16[512,768]{1,0:T(8,128)(2,1)} %get-tuple-element.123.n_ref, f32[512,768]{1,0:T(8,128)} %get-tuple-element.204.gnq_ref, ...), custom_call_target="tpu_custom_call" | custom-call | flops 2415919104 | bytes 9437184 | tf_op jit(solution)/shard_map/kv_back/pallas_call | solution.py:1010
  551.3 5.2 collective-permute-done.20
  557.6 5.6 all-to-all-start.5
  568.6 9.2 %all-to-all-done.5 = bf16[8,24,1536]{2,1,0:T(8,128)(2,1)S(1)} async-done(((bf16[8,24,1536]{2,1,0:T(8,128)(2,1)}), bf16[8,24,1536]{2,1,0:T(8,128)(2,1)S(1)}, u32[]{:S(2)}, u32[]{:S(2)}) %all-to-all-start.5) | async-done | bytes 589856 | tf_op jit(solution)/shard_map/all_to_all | solution.py:1081
  (195 shorter events, 134.5 us)
Async XLA Ops:
  7.2 72.7 %all-gather.4.cloned.1.call-start = ((), (), s32[]{:S(2)}) async-start(), calls=%async_computation.7 | async-start | bytes 5068800 | tf_op jit(solution)/shard_map/all_gather | solution.py:1117
  12.7 215.8 %all-gather.6.cloned.1.call-start = ((), (), s32[]{:S(2)}) async-start(), calls=%async_computation.9 | async-start | bytes 11796480 | tf_op jit(solution)/shard_map/all_gather | solution.py:1181
  91.0 20.0 %collective-permute-start.1 = (bf16[256,1536]{1,0:T(8,128)(2,1)}, bf16[256,1536]{1,0:T(8,128)(2,1)S(1)}, u32[]{:S(2)}, u32[]{:S(2)}) collective-permute-start(bf16[256,1536]{1,0:T(8,128)(2,1)} %get-tuple-element.126.kv_ref), channel_id=1, source_target_pairs={{0,1},{2,0},{4,2},{6,4},{7,6},{5,7},{3,5},{1,3},{8,9},{10,8},{12,1... | collective-permute-start | bytes 2359304 | tf_op jit(solution)/shard_map/ppermute | solution.py:1059
  92.5 19.7 %collective-permute-start = (bf16[256,1536]{1,0:T(8,128)(2,1)}, bf16[256,1536]{1,0:T(8,128)(2,1)S(1)}, u32[]{:S(2)}, u32[]{:S(2)}) collective-permute-start(bf16[256,1536]{1,0:T(8,128)(2,1)} %get-tuple-element.126.kv_ref), channel_id=1, source_target_pairs={{0,2},{2,4},{4,6},{6,7},{7,5},{5,3},{3,1},{1,0},{8,10},{10,12},{12... | collective-permute-start | bytes 2359304 | tf_op jit(solution)/shard_map/ppermute | solution.py:1059
  112.1 18.7 %collective-permute-start.2 = (bf16[256,1536]{1,0:T(8,128)(2,1)S(1)}, bf16[256,1536]{1,0:T(8,128)(2,1)S(1)}, u32[]{:S(2)}, u32[]{:S(2)}) collective-permute-start(bf16[256,1536]{1,0:T(8,128)(2,1)S(1)} %collective-permute-done.refs_0_.refs_1_), channel_id=1, source_target_pairs={{0,2},{2,4},{4,6},{6,7},{7,5},{5,3},{3,1},{1,0},{8,10},{10,12},{12... | collective-permute-start | bytes 2359304 | tf_op jit(solution)/shard_map/ppermute | solution.py:1059
  112.7 18.5 %collective-permute-start.3 = (bf16[256,1536]{1,0:T(8,128)(2,1)S(1)}, bf16[256,1536]{1,0:T(8,128)(2,1)}, u32[]{:S(2)}, u32[]{:S(2)}) collective-permute-start(bf16[256,1536]{1,0:T(8,128)(2,1)S(1)} %collective-permute-done.1.refs_1_.refs_0_), channel_id=1, source_target_pairs={{0,1},{2,0},{4,2},{6,4},{7,6},{5,7},{3,5},{1,3},{8,9},{10,8},{12,1... | collective-permute-start | bytes 2359304 | tf_op jit(solution)/shard_map/ppermute | solution.py:1059
  131.8 18.2 %collective-permute-start.4 = (bf16[256,1536]{1,0:T(8,128)(2,1)}, bf16[256,1536]{1,0:T(8,128)(2,1)S(1)}, u32[]{:S(2)}, u32[]{:S(2)}) collective-permute-start(bf16[256,1536]{1,0:T(8,128)(2,1)} %copy-done.29), channel_id=1, source_target_pairs={{0,2},{2,4},{4,6},{6,7},{7,5},{5,3},{3,1},{1,0},{8,10},{10,12},{12... | collective-permute-start | bytes 2359304 | tf_op jit(solution)/shard_map/ppermute | solution.py:1059
  132.6 17.6 %collective-permute-start.5 = (bf16[256,1536]{1,0:T(8,128)(2,1)}, bf16[256,1536]{1,0:T(8,128)(2,1)S(1)}, u32[]{:S(2)}, u32[]{:S(2)}) collective-permute-start(bf16[256,1536]{1,0:T(8,128)(2,1)} %collective-permute-done.3.refs_1_.refs_0_), channel_id=1, source_target_pairs={{0,1},{2,0},{4,2},{6,4},{7,6},{5,7},{3,5},{1,3},{8,9},{10,8},{12,1... | collective-permute-start | bytes 2359304 | tf_op jit(solution)/shard_map/ppermute | solution.py:1059
  134.0 20.4 %copy-start = (s32[2,256,2]{2,1,0:T(8,128)}, s32[2,256,2]{2,1,0:T(8,128)S(1)}, u32[]{:S(2)}) copy-start(s32[2,256,2]{2,1,0:T(8,128)S(1)} %copy.139) | copy-start | bytes 12292
  152.2 14.8 %collective-permute-start.7 = (bf16[256,768]{1,0:T(8,128)(2,1)S(1)}, bf16[256,768]{1,0:T(8,128)(2,1)}, u32[]{:S(2)}, u32[]{:S(2)}) collective-permute-start(bf16[256,768]{1,0:T(8,128)(2,1)S(1)} %slice.71), channel_id=1, source_target_pairs={{0,1},{2,0},{4,2},{6,4},{7,6},{5,7},{3,5},{1,3},{8,9},{10,8},{12,1... | collective-permute-start | bytes 1179656 | tf_op jit(solution)/shard_map/ppermute | solution.py:1059
  153.7 13.2 %collective-permute-start.6 = (bf16[256,768]{1,0:T(8,128)(2,1)S(1)}, bf16[256,768]{1,0:T(8,128)(2,1)}, u32[]{:S(2)}, u32[]{:S(2)}) collective-permute-start(bf16[256,768]{1,0:T(8,128)(2,1)S(1)} %slice.70), channel_id=1, source_target_pairs={{0,2},{2,4},{4,6},{6,7},{7,5},{5,3},{3,1},{1,0},{8,10},{10,12},{12... | collective-permute-start | bytes 1179656 | tf_op jit(solution)/shard_map/ppermute | solution.py:1059
  183.9 39.9 %all-to-all-start = ((bf16[8,128,768]{2,1,0:T(8,128)(2,1)}), bf16[8,128,768]{2,1,0:T(8,128)(2,1)S(1)}, u32[]{:S(2)}, u32[]{:S(2)}) async-start(bf16[8,128,768]{2,1,0:T(8,128)(2,1)} %bitcast.96), calls=%async_computation | async-start | bytes 3145728 | tf_op jit(solution)/shard_map/all_to_all | solution.py:1151
  224.9 40.3 %all-to-all-start.1 = ((bf16[8,128,768]{2,1,0:T(8,128)(2,1)}), bf16[8,128,768]{2,1,0:T(8,128)(2,1)S(1)}, u32[]{:S(2)}, u32[]{:S(2)}) async-start(bf16[8,128,768]{2,1,0:T(8,128)(2,1)} %bitcast.95), calls=%async_computation.1 | async-start | bytes 3145728 | tf_op jit(solution)/shard_map/all_to_all | solution.py:1151
  266.3 40.8 %all-to-all-start.2 = ((bf16[8,128,768]{2,1,0:T(8,128)(2,1)}), bf16[8,128,768]{2,1,0:T(8,128)(2,1)S(1)}, u32[]{:S(2)}, u32[]{:S(2)}) async-start(bf16[8,128,768]{2,1,0:T(8,128)(2,1)} %bitcast.94), calls=%async_computation.2 | async-start | bytes 3145728 | tf_op jit(solution)/shard_map/all_to_all | solution.py:1151
  270.0 277.4 %reduce-scatter.2.cloned.1.call-start = ((), (), s32[]{:S(2)}) async-start(), calls=%async_computation.8 | async-start | bytes 11796480 | tf_op jit(solution)/shard_map/reduce_scatter | solution.py:1218
  338.0 40.8 %all-to-all-start.3 = ((bf16[8,128,768]{2,1,0:T(8,128)(2,1)}), bf16[8,128,768]{2,1,0:T(8,128)(2,1)S(1)}, u32[]{:S(2)}, u32[]{:S(2)}) async-start(bf16[8,128,768]{2,1,0:T(8,128)(2,1)} %bitcast.28), calls=%async_computation.3 | async-start | bytes 3145728 | tf_op jit(solution)/shard_map/all_to_all | solution.py:1151
  398.3 15.8 %collective-permute-start.8 = (bf16[256,768]{1,0:T(8,128)(2,1)}, bf16[256,768]{1,0:T(8,128)(2,1)}, u32[]{:S(2)}, u32[]{:S(2)}) collective-permute-start(bf16[256,768]{1,0:T(8,128)(2,1)} %get-tuple-element.164), channel_id=1, source_target_pairs={{0,2},{2,4},{4,6},{6,7},{7,5},{5,3},{3,1},{1,0},{8,10},{10,12},{12... | collective-permute-start | bytes 1179656 | tf_op jit(solution)/shard_map/ppermute | solution.py:1059
  398.4 15.7 %collective-permute-start.9 = (bf16[256,768]{1,0:T(8,128)(2,1)}, bf16[256,768]{1,0:T(8,128)(2,1)}, u32[]{:S(2)}, u32[]{:S(2)}) collective-permute-start(bf16[256,768]{1,0:T(8,128)(2,1)} %get-tuple-element.165), channel_id=1, source_target_pairs={{0,1},{2,0},{4,2},{6,4},{7,6},{5,7},{3,5},{1,3},{8,9},{10,8},{12,1... | collective-permute-start | bytes 1179656 | tf_op jit(solution)/shard_map/ppermute | solution.py:1059
  402.9 11.2 %collective-permute-start.10 = (bf16[2,192,896]{2,1,0:T(8,128)(2,1)S(1)}, bf16[2,192,896]{2,1,0:T(8,128)(2,1)S(1)}, u32[]{:S(2)}, u32[]{:S(2)}) collective-permute-start(bf16[2,192,896]{2,1,0:T(8,128)(2,1)S(1)} %fusion.4), channel_id=1, source_target_pairs={{0,8},{8,0},{16,24},{24,16},{1,9},{9,1},{17,25},{25,17},{2,10},{10... | collective-permute-start | bytes 2064392 | tf_op jit(solution)/shard_map/ppermute | solution.py:1067
  417.5 20.3 %collective-permute-start.11 = (bf16[256,1536]{1,0:T(8,128)(2,1)}, bf16[256,1536]{1,0:T(8,128)(2,1)}, u32[]{:S(2)}, u32[]{:S(2)}) collective-permute-start(bf16[256,1536]{1,0:T(8,128)(2,1)} %get-tuple-element.177), channel_id=1, source_target_pairs={{0,2},{2,4},{4,6},{6,7},{7,5},{5,3},{3,1},{1,0},{8,10},{10,12},{12... | collective-permute-start | bytes 2359304 | tf_op jit(solution)/shard_map/ppermute | solution.py:1059
  417.8 21.6 %collective-permute-start.12 = (bf16[256,1536]{1,0:T(8,128)(2,1)}, bf16[256,1536]{1,0:T(8,128)(2,1)}, u32[]{:S(2)}, u32[]{:S(2)}) collective-permute-start(bf16[256,1536]{1,0:T(8,128)(2,1)} %get-tuple-element.178), channel_id=1, source_target_pairs={{0,1},{2,0},{4,2},{6,4},{7,6},{5,7},{3,5},{1,3},{8,9},{10,8},{12,1... | collective-permute-start | bytes 2359304 | tf_op jit(solution)/shard_map/ppermute | solution.py:1059
  420.8 12.0 %collective-permute-start.13 = (bf16[192,896]{1,0:T(8,128)(2,1)S(1)}, bf16[192,896]{1,0:T(8,128)(2,1)S(1)}, u32[]{:S(2)}, u32[]{:S(2)}) collective-permute-start(bf16[192,896]{1,0:T(8,128)(2,1)S(1)} %fusion.6), channel_id=1, source_target_pairs={{0,16},{16,0},{8,24},{24,8},{1,17},{17,1},{9,25},{25,9},{2,18},{18... | collective-permute-start | bytes 1032200 | tf_op jit(solution)/shard_map/ppermute | solution.py:1075
  442.7 20.4 %collective-permute-start.14 = (bf16[256,1536]{1,0:T(8,128)(2,1)}, bf16[256,1536]{1,0:T(8,128)(2,1)S(1)}, u32[]{:S(2)}, u32[]{:S(2)}) collective-permute-start(bf16[256,1536]{1,0:T(8,128)(2,1)} %get-tuple-element.188), channel_id=1, source_target_pairs={{0,2},{2,4},{4,6},{6,7},{7,5},{5,3},{3,1},{1,0},{8,10},{10,12},{12... | collective-permute-start | bytes 2359304 | tf_op jit(solution)/shard_map/ppermute | solution.py:1059
  446.2 19.2 %collective-permute-start.15 = (bf16[256,1536]{1,0:T(8,128)(2,1)}, bf16[256,1536]{1,0:T(8,128)(2,1)S(1)}, u32[]{:S(2)}, u32[]{:S(2)}) collective-permute-start(bf16[256,1536]{1,0:T(8,128)(2,1)} %get-tuple-element.189), channel_id=1, source_target_pairs={{0,1},{2,0},{4,2},{6,4},{7,6},{5,7},{3,5},{1,3},{8,9},{10,8},{12,1... | collective-permute-start | bytes 2359304 | tf_op jit(solution)/shard_map/ppermute | solution.py:1059
  489.6 2.2 collective-permute-start.16
  489.6 20.2 %collective-permute-start.17 = (bf16[256,1536]{1,0:T(8,128)(2,1)}, bf16[256,1536]{1,0:T(8,128)(2,1)S(1)}, u32[]{:S(2)}, u32[]{:S(2)}) collective-permute-start(bf16[256,1536]{1,0:T(8,128)(2,1)} %get-tuple-element.210), channel_id=1, source_target_pairs={{0,2},{2,4},{4,6},{6,7},{7,5},{5,3},{3,1},{1,0},{8,10},{10,12},{12... | collective-permute-start | bytes 2359304 | tf_op jit(solution)/shard_map/ppermute | solution.py:1059
  491.1 19.8 %collective-permute-start.18 = (bf16[256,1536]{1,0:T(8,128)(2,1)}, bf16[256,1536]{1,0:T(8,128)(2,1)S(1)}, u32[]{:S(2)}, u32[]{:S(2)}) collective-permute-start(bf16[256,1536]{1,0:T(8,128)(2,1)} %get-tuple-element.211), channel_id=1, source_target_pairs={{0,1},{2,0},{4,2},{6,4},{7,6},{5,7},{3,5},{1,3},{8,9},{10,8},{12,1... | collective-permute-start | bytes 2359304 | tf_op jit(solution)/shard_map/ppermute | solution.py:1059
  525.5 3.1 collective-permute-start.19
  525.7 9.5 %collective-permute-start.21 = (bf16[192,768]{1,0:T(8,128)(2,1)S(1)}, bf16[192,768]{1,0:T(8,128)(2,1)S(1)}, u32[]{:S(2)}, u32[]{:S(2)}) collective-permute-start(bf16[192,768]{1,0:T(8,128)(2,1)S(1)} %fusion.7), channel_id=1, source_target_pairs={{0,16},{16,0},{8,24},{24,8},{1,17},{17,1},{9,25},{25,9},{2,18},{18... | collective-permute-start | bytes 884744 | tf_op jit(solution)/shard_map/ppermute | solution.py:1075
  536.2 21.4 %all-to-all-start.4 = ((bf16[8,24,1664]{2,1,0:T(8,128)(2,1)}), bf16[8,24,1664]{2,1,0:T(8,128)(2,1)}, u32[]{:S(2)}, u32[]{:S(2)}) async-start(bf16[8,24,1664]{2,1,0:T(8,128)(2,1)} %fusion.1), calls=%async_computation.5 | async-start | bytes 1277952 | tf_op jit(solution)/shard_map/all_to_all | solution.py:1081
  541.5 15.1 %collective-permute-start.20 = (bf16[192,1536]{1,0:T(8,128)(2,1)}, bf16[192,1536]{1,0:T(8,128)(2,1)S(1)}, u32[]{:S(2)}, u32[]{:S(2)}) collective-permute-start(bf16[192,1536]{1,0:T(8,128)(2,1)} %fusion.5), channel_id=1, source_target_pairs={{0,16},{16,0},{8,24},{24,8},{1,17},{17,1},{9,25},{25,9},{2,18},{18... | collective-permute-start | bytes 1769480 | tf_op jit(solution)/shard_map/ppermute | solution.py:1075
  557.6 20.3 %all-to-all-start.5 = ((bf16[8,24,1536]{2,1,0:T(8,128)(2,1)}), bf16[8,24,1536]{2,1,0:T(8,128)(2,1)S(1)}, u32[]{:S(2)}, u32[]{:S(2)}) async-start(bf16[8,24,1536]{2,1,0:T(8,128)(2,1)} %bitcast.50), calls=%async_computation.6 | async-start | bytes 1179648 | tf_op jit(solution)/shard_map/all_to_all | solution.py:1081
  (30 other events, 159.0 us)
Sparse Core Ops, SparseCore 0:
  12.8 67.0 all-gather.3
  81.5 62.5 all-gather.5
  338.1 76.2 reduce-scatter.1

commit v2 on v1

--- a/solution.py
+++ b/solution.py
@@ -89,8 +89,9 @@
     kvc_ref[:, LANES:] = v[r:]
     q = dot(n, wq_ref[...])
     q = q * cosine + partner(q) * sine
-    q_ref[...] = q.astype(BF16)
-    qt_ref[...] = q.T.astype(BF16)
+    q = q.astype(BF16)
+    q_ref[...] = q
+    qt_ref[...] = q.T
 
 
 def qkv_call(x, gain, pack, cosine, sine):
@@ -184,12 +185,10 @@
     vto = kvo_ref[:, LANES:].T
     st_ref[...] = jnp.zeros_like(st_ref)
     own, cont = local_masks(sc_ref, r, keys, 0, t)
+    attend_update(qz, kb, vt, 0, t, own, st_ref, a_ref, True)
     if r % LANES == 0:
-        attend_update(qz, kb, vt, 0, r, own[:, :r], st_ref, a_ref, True)
-        attend_update(qz, kb, vt, r, t, None, st_ref, a_ref, True)
         attend_update(qz, kbo, vto, r, t, cont[:, r:], st_ref, a_ref, False)
     else:
-        attend_update(qz, kb, vt, 0, t, own, st_ref, a_ref, True)
         attend_update(qz, kbo, vto, 0, t, cont, st_ref, a_ref, False)
 
 
@@ -243,7 +242,7 @@
             total = st_ref[2 + h : 3 + h, :]
             a_ref[rows, :] = a_ref[rows, :] / total
             st_ref[h : h + 1, :] = st_ref[h : h + 1, :] * LC + jnp.log2(total)
-        low_ref[...] = a_ref[...].T.astype(BF16)
+        low_ref[...] = a_ref[...].astype(BF16).T
 
 
 def kv_specs(kvs, halves):
@@ -341,13 +340,10 @@
     kbo, vbo = kvo_ref[:, :LANES], kvo_ref[:, LANES:]
     kt, kto = kb.T, kbo.T
     own, cont = local_masks(sc_ref, r, keys, 0, t)
+    dk, dv = back_block(ops, kb, vb, kt, 0, t, own, dq_ref)
     if r % LANES == 0:
-        dk, dv = back_block(ops, kb, vb, kt, 0, r, own[:, :r], dq_ref)
-        dk2, dv2 = back_block(ops, kb, vb, kt, r, t, None, dq_ref)
-        dk, dv = dk + dk2, dv + dv2
         dko, dvo = back_block(ops, kbo, vbo, kto, r, t, cont[:, r:], dq_ref)
     else:
-        dk, dv = back_block(ops, kb, vb, kt, 0, t, own, dq_ref)
         dko, dvo = back_block(ops, kbo, vbo, kto, 0, t, cont, dq_ref)
     dkv_ref[:, :LANES] = dk * SCALE
     dkv_ref[:, LANES:] = dv
@@ -436,15 +432,19 @@
                 go(0, (col >= r) | (block < me))
 
 
+def add_low(a, b):
+    return (a.astype(F32) + b.astype(F32)).astype(BF16)
+
+
 def ring_add_body(half, pr_ref, gr_ref, pl_ref, gl_ref, sr_ref, sl_ref):
     if not half:
-        sr_ref[...] = (pr_ref[...] + gr_ref[...].astype(F32)).astype(BF16)
-        sl_ref[...] = (pl_ref[...] + gl_ref[...].astype(F32)).astype(BF16)
+        sr_ref[...] = add_low(pr_ref[...], gr_ref[...])
+        sl_ref[...] = add_low(pl_ref[...], gl_ref[...])
         return
-    sr_ref[:, :D] = (pr_ref[:, :D] + gr_ref[...].astype(F32)).astype(BF16)
-    sr_ref[:, D:] = pr_ref[:, D:].astype(BF16)
-    sl_ref[:, :D] = pl_ref[:, :D].astype(BF16)
-    sl_ref[:, D:] = (pl_ref[:, D:] + gl_ref[...].astype(F32)).astype(BF16)
+    sr_ref[:, :D] = add_low(pr_ref[:, :D], gr_ref[...])
+    sr_ref[:, D:] = pr_ref[:, D:]
+    sl_ref[:, :D] = pl_ref[:, :D]
+    sl_ref[:, D:] = add_low(pl_ref[:, D:], gl_ref[...])
 
 
 def ring_add(part_r, got_r, part_l, got_l):
@@ -855,9 +855,9 @@
     gh = g_ref[...].astype(F32) + q * u - hidden * (q * q * q * mean)
     gh_ref[...] = gh
     gb = gh.astype(BF16)
-    d_out = dot_nt(gb, ow_ref[...])
-    do_ref[...] = d_out.astype(BF16)
-    dot_ref[...] = d_out.T.astype(BF16)
+    d_out = dot_nt(gb, ow_ref[...]).astype(BF16)
+    do_ref[...] = d_out
+    dot_ref[...] = d_out.T
     gow = dot(att_ref[...].T, gb)
     gain = jnp.sum(gn * hidden * q, axis=0, keepdims=True)
 
@@ -920,8 +920,7 @@
     return [tile, tile], [shape(dims, BF16), shape(dims, F32)]
 
 
-def q_back_body(split, sc_ref, n_ref, dq_ref, c_ref, s_ref, w_ref, gn_ref, *refs):
-    nt_ref = refs[-1]
+def q_back_body(split, sc_ref, n_ref, dq_ref, c_ref, s_ref, w_ref, gn_ref, nt_ref, *refs):
     step = pl.program_id(0)
 
     @pl.when(step == 0)
@@ -939,7 +938,7 @@
         ],
         axis=1,
     )
-    store_grad(sc_ref, split, dot(nt_ref[...], gq), refs[:-1])
+    store_grad(sc_ref, split, dot(nt_ref[...], gq), refs)
     gn = dot_nt(gq, w_ref[...])
 
     @pl.when(step == 0)
@@ -961,25 +960,23 @@
             SMEM_SPEC, whole((t, D)), spec((t, 2 * LANES), lambda i: (0, i)), whole((t, LANES)),
             whole((t, LANES)), spec((D, 2 * LANES), lambda i: (0, i)),
         ],
-        out_specs=[whole((t, D))] + specs,
-        out_shape=[shape((t, D), F32)] + shapes,
-        scratch_shapes=[pltpu.VMEM((D, t), BF16)],
+        out_specs=[whole((t, D)), whole((D, t))] + specs,
+        out_shape=[shape((t, D), F32), shape((D, t), BF16)] + shapes,
         name="q_back",
         **params((4 * t * D * D, 12 * t * D)),
     )(sc, low, dq, cosine, sine, pack)
 
 
 def kv_back_body(
-    split, count, sc_ref, x_ref, n_ref, gnq_ref, gh_ref, gain_ref, c_ref, s_ref, wk_ref, wv_ref,
+    split, count, sc_ref, x_ref, nt_ref, gnq_ref, gh_ref, gain_ref, c_ref, s_ref, wk_ref, wv_ref,
     own_ref, cont_ref, *refs
 ):
     got_refs, refs = refs[:count], refs[count:]
-    gi_ref, grads, (nt_ref, gn_ref) = refs[0], refs[1:-2], refs[-2:]
+    gi_ref, grads, gn_ref = refs[0], refs[1:-1], refs[-1]
     step = pl.program_id(0)
 
     @pl.when(step == 0)
     def _():
-        nt_ref[...] = n_ref[...].T
         gn_ref[...] = gnq_ref[...]
 
     own = own_ref[...]
@@ -1002,7 +999,7 @@
         gi_ref[...] = gh_ref[...] + q * u - x * (q * q * q * mean)
 
 
-def kv_back_call(sc, x, low, gn, gh, gain, cosine, sine, pack, own, cont, got, split):
+def kv_back_call(sc, x, low_t, gn, gh, gain, cosine, sine, pack, own, cont, got, split):
     t = x.shape[0]
     r = t // 2
     specs, shapes = grad_outs(split, 2 * D)
@@ -1011,7 +1008,7 @@
         functools.partial(kv_back_body, split, len(got)),
         grid=(PAIRS,),
         in_specs=[
-            SMEM_SPEC, whole((t, D)), whole((t, D)), whole((t, D)), whole((t, D)), whole((1, D)),
+            SMEM_SPEC, whole((t, D)), whole((D, t)), whole((t, D)), whole((t, D)), whole((1, D)),
             whole((t, LANES)), whole((t, LANES)),
             spec((D, LANES), lambda i: (0, PAIRS + i)),
             spec((D, LANES), lambda i: (0, 2 * PAIRS + i)),
@@ -1020,10 +1017,10 @@
         + [wide] * len(got),
         out_specs=[whole((t, D))] + specs,
         out_shape=[shape((t, D), F32)] + shapes,
-        scratch_shapes=[pltpu.VMEM((D, t), BF16), pltpu.VMEM((t, D), F32)],
+        scratch_shapes=[pltpu.VMEM((t, D), F32)],
         name="kv_back",
         **params((8 * t * D * D, 24 * t * D)),
-    )(sc, x, low, gn, gh, gain, cosine, sine, pack, pack, own, cont, *got)
+    )(sc, x, low_t, gn, gh, gain, cosine, sine, pack, pack, own, cont, *got)
 
 
 def rotation_tables(position):
@@ -1242,7 +1239,7 @@
         for i in range(3, 0, -1):
             got_r, got_l = along_ring(send_r, 1), along_ring(send_l, -1)
             dq_t, part_r, part_l = bwd_remote(
-                *back, st, dq_t, (left[i], right[i]), (i, 8 - i)
+                *back, st, dq_t, (left[i], right[i]), (i, 8 - i), dtype=BF16
             )
             got_r, got_l, part_r, part_l, dq_t, early_got = tie(
                 got_r, got_l, part_r, part_l, dq_t, early_got
@@ -1266,13 +1263,13 @@
         dkv_cont = lax.psum_scatter(
             dkv_cont, "expert", scatter_dimension=0, tiled=True, axis_index_groups=cont_groups
         )
-    gn_q, *grad_q = q_back_call(sc, low_one, dq, cosine, sine, pack, ring)
+    gn_q, low_one_t, *grad_q = q_back_call(sc, low_one, dq, cosine, sine, pack, ring)
     if ring:
         got_q = swap_core(grad_q[0])
         keep_q, got_q = add_and_cross(grad_q[1], got_q)
         keep_q, *got = tie(keep_q, *got)
     grad_input, *grad_kv = kv_back_call(
-        sc, x, low_one, gn_q, gh, gain_one, cosine, sine, pack, dkv_own, dkv_cont, got, ring
+        sc, x, low_one_t, gn_q, gh, gain_one, cosine, sine, pack, dkv_own, dkv_cont, got, ring
     )
     output, grad_input = from_rows(output), from_rows(grad_input)
     if ring:

time: 596 us -> 592 us (level)
  Pallas kernels: 241 us -> 235 us
  transfers between devices with their start and end apart: 31 -> 31, of which waited for: 23 -> 23; matrix products, arithmetic and copies ran while one was open for 8% -> 8% of each run, Pallas kernels for 36% -> 35%
where the time goes in v2:
time: 592 us; the launch traced here: 583 us
  Pallas kernels  235 us (40%)
  waiting for transfers between devices  225 us (38%)
  starting transfers between devices  47.8 us (8%)
  local copies, waits for them, and re-layouts  37.7 us (6%)
  other arithmetic  23.3 us (4%)
  between operations  14.4 us (2%)
    all_to_all x4, waiting for transfers between devices, exchange(): lax.all_to_all(rows, 'expert', split_axis=0, concat_axis=0, tiled=True)  94.8 us
    all_gather x1, waiting for transfers between devices, per_device(): lax.all_gather(jnp.concatenate([qkv_weight, out_weight, small], axis=1),...  58.7 us
    ppermute x16, waiting for transfers between devices, along_ring(): return lax.ppermute(array, 'expert', pairs)  49.7 us
    pallas_call x4, Pallas kernels, bwd_remote(): pl.pallas_call(functools.partial(bwd_remote_body, tuple(offsets), len(kvs...  41 us
    pallas_call x4, Pallas kernels, fwd_remote(): pl.pallas_call(functools.partial(fwd_remote_body, tuple(offsets), len(kvs...  38 us
    pallas_call x1, Pallas kernels, expert_in(): pl.pallas_call(expert_in_body, grid=(wide // part,), in_specs=[tile, tile...  23.7 us
    pallas_call x1, Pallas kernels, expert_fwd(): pl.pallas_call(expert_fwd_body, grid=(wide // part,), in_specs=[whole((ro...  19.1 us
    ppermute x16, starting transfers between devices, along_ring(): return lax.ppermute(array, 'expert', pairs)  18.6 us
  transfers between devices with their start and end apart: 31, of which 23 were waited for; matrix products, arithmetic and copies ran while one was open for 8% of the time, Pallas kernels for 35%

profile of v2, /device:TPU:0, one launch (start us, length us, event | category | flops | bytes accessed | tf_op | source)
XLA Modules:
  0.0 582.9 jit_solution(8354898108319254088)
XLA Ops:
  21.2 58.7 %all-gather.4.cloned.1.call-done.wq_ref.wk_ref.wv_ref.ow_ref.sw_ref.w_ref = bf16[768,3200]{1,0:T(8,128)(2,1)} async-done(((bf16[24,3200]{1,0:T(8,128)(2,1)}), bf16[768,3200]{1,0:T(8,128)(2,1)}) %all-gather.4.cloned.1.call-update) | async-done | bytes 4915216 | tf_op jit(solution)/shard_map/all_gather | solution.py:1114
  82.0 9.0 %qkv_rope.1 = (bf16[512,768]{1,0:T(8,128)(2,1)}, bf16[512,768]{1,0:T(8,128)(2,1)}, bf16[768,512]{1,0:T(8,128)(2,1)}, bf16[256,1536]{1,0:T(8,128)(2,1)}, bf16[256,1536]{1,0:T(8,128)(2,1)}) custom-call(bf16[512,768]{1,0:T(8,128)(2,1)} %bitcast.70, f32[1,768]{1,0:T(1,128)} %copy.137.gain_ref, ...), custom_call_target="tpu_custom_call" | custom-call | flops 1811939328 | bytes 3538944 | tf_op jit(solution)/shard_map/qkv_rope/pallas_call | solution.py:99
  95.6 9.9 %attend_local.1 = (f32[48,512]{1,0:T(8,128)}, f32[768,512]{1,0:T(8,128)}) custom-call(s32[12]{0:T(128)} %concatenate.51.sc_ref, bf16[768,512]{1,0:T(8,128)(2,1)} %get-tuple-element.125.qt_ref, bf16[256,1536]{1,0:T(8,128)(2,1)} %get-tuple-element.127.kv_ref, bf16[256,1536]{1,0:T(8,128)(2,1)} %get-tuple-element.128.kvo_ref), custom_call_target="tpu_custom_call" | custom-call | flops 1610612736 | bytes 1572864 | tf_op jit(solution)/shard_map/attend_local/pallas_call | solution.py:261
  105.4 5.5 collective-permute-done.1.refs_1_.refs_0_
  114.2 10.2 %attend_remote.4 = (f32[48,512]{1,0:T(8,128)}, f32[768,512]{1,0:T(8,128)}) custom-call(s32[12]{0:T(128)} %concatenate.51.sc_ref, bf16[768,512]{1,0:T(8,128)(2,1)} %get-tuple-element.125.qt_ref, bf16[256,1536]{1,0:T(8,128)(2,1)} %copy-done.28, bf16[256,1536]{1,0:T(8,128)(2,1)} %copy-done.27, f32[48,512]{1,0:T(8,128)} %get-tuple-element.132.refs_2_, ...), custom_call_target="tpu_custom_call" | custom-call | flops 3221225472 | bytes 4718592 | tf_op jit(solution)/shard_map/attend_remote/pallas_call | solution.py:285
  124.4 6.5 %collective-permute-done.2.refs_0_.refs_1_ = bf16[256,1536]{1,0:T(8,128)(2,1)S(1)} collective-permute-done((bf16[256,1536]{1,0:T(8,128)(2,1)S(1)}, bf16[256,1536]{1,0:T(8,128)(2,1)S(1)}, u32[]{:S(2)}, u32[]{:S(2)}) %collective-permute-start.2) | collective-permute-done | bytes 786464 | tf_op jit(solution)/shard_map/ppermute | solution.py:1056
  134.7 10.2 %attend_remote.5 = (f32[48,512]{1,0:T(8,128)}, f32[768,512]{1,0:T(8,128)}) custom-call(s32[12]{0:T(128)} %concatenate.51.sc_ref, bf16[768,512]{1,0:T(8,128)(2,1)} %get-tuple-element.125.qt_ref, bf16[256,1536]{1,0:T(8,128)(2,1)} %copy-done.29, bf16[256,1536]{1,0:T(8,128)(2,1)} %collective-permute-done.3.refs_1_.refs_0_, ...), custom_call_target="tpu_custom_call" | custom-call | flops 3221225472 | bytes 4718592 | tf_op jit(solution)/shard_map/attend_remote/pallas_call | solution.py:285
  156.8 10.2 %attend_remote.6 = (f32[48,512]{1,0:T(8,128)}, f32[768,512]{1,0:T(8,128)}) custom-call(s32[12]{0:T(128)} %concatenate.51.sc_ref, bf16[768,512]{1,0:T(8,128)(2,1)} %get-tuple-element.125.qt_ref, bf16[256,1536]{1,0:T(8,128)(2,1)} %copy-done.21, bf16[256,1536]{1,0:T(8,128)(2,1)} %copy-done.22, f32[48,512]{1,0:T(8,128)} %get-tuple-element.142.refs_2_, ...), custom_call_target="tpu_custom_call" | custom-call | flops 3221225472 | bytes 4718592 | tf_op jit(solution)/shard_map/attend_remote/pallas_call | solution.py:285
  167.0 7.5 %attend_remote.7 = (f32[48,512]{1,0:T(8,128)}, f32[768,512]{1,0:T(8,128)}, bf16[512,768]{1,0:T(8,128)(2,1)}) custom-call(s32[12]{0:T(128)} %concatenate.51.sc_ref, bf16[768,512]{1,0:T(8,128)(2,1)} %get-tuple-element.125.qt_ref, bf16[256,768]{1,0:T(8,128)(2,1)} %collective-permute-done.6.refs_0_, bf16[256,768]{1,0:T(8,128)(2,1)} %collective-permute-done.7.refs_1_, ...), custom_call_target="tpu_custom_call" | custom-call | flops 1610612736 | bytes 3932160 | tf_op jit(solution)/shard_map/attend_remote/pallas_call | solution.py:285
  174.4 9.4 %route_dispatch.1 = (f32[512,768]{1,0:T(8,128)}, bf16[512,768]{1,0:T(8,128)(2,1)}, f32[512,128]{1,0:T(8,128)}, bf16[1024,768]{1,0:T(8,128)(2,1)}) custom-call(bf16[512,768]{1,0:T(8,128)(2,1)} %bitcast.71, bf16[512,768]{1,0:T(8,128)(2,1)} %get-tuple-element.146.att_ref, ...), custom_call_target="tpu_custom_call" | custom-call | flops 1409286144 | bytes 3145728 | tf_op jit(solution)/shard_map/route_dispatch/pallas_call | solution.py:608
  183.8 5.8 %all-to-all-start = ((bf16[8,128,768]{2,1,0:T(8,128)(2,1)}), bf16[8,128,768]{2,1,0:T(8,128)(2,1)S(1)}, u32[]{:S(2)}, u32[]{:S(2)}) async-start(bf16[8,128,768]{2,1,0:T(8,128)(2,1)} %bitcast.96), calls=%async_computation | async-start | bytes 3145728 | tf_op jit(solution)/shard_map/all_to_all | solution.py:1148
  195.5 28.1 %all-to-all-done = bf16[8,128,768]{2,1,0:T(8,128)(2,1)S(1)} async-done(((bf16[8,128,768]{2,1,0:T(8,128)(2,1)}), bf16[8,128,768]{2,1,0:T(8,128)(2,1)S(1)}, u32[]{:S(2)}, u32[]{:S(2)}) %all-to-all-start) | async-done | bytes 1572896 | tf_op jit(solution)/shard_map/all_to_all | solution.py:1148
  228.4 19.1 %expert_forward.1 = (bf16[1024,768]{1,0:T(8,128)(2,1)}, f32[1024,2048]{1,0:T(8,128)}, f32[1024,2048]{1,0:T(8,128)}) custom-call(bf16[1024,768]{1,0:T(8,128)(2,1)} %bitcast.89, bf16[4,3,192,2048]{3,2,1,0:T(8,128)(2,1)} %bitcast.117), custom_call_target="tpu_custom_call" | custom-call | flops 9663676416 | bytes 9437184 | tf_op jit(solution)/shard_map/expert_forward/pallas_call | solution.py:659
  247.4 17.5 %all-to-all-done.1 = bf16[8,128,768]{2,1,0:T(8,128)(2,1)S(1)} async-done(((bf16[8,128,768]{2,1,0:T(8,128)(2,1)}), bf16[8,128,768]{2,1,0:T(8,128)(2,1)S(1)}, u32[]{:S(2)}, u32[]{:S(2)}) %all-to-all-start.1) | async-done | bytes 1572896 | tf_op jit(solution)/shard_map/all_to_all | solution.py:1148
  271.2 23.7 %expert_back_in.1 = (bf16[1024,768]{1,0:T(8,128)(2,1)}, bf16[1024,2048]{1,0:T(8,128)(2,1)}, bf16[1024,2048]{1,0:T(8,128)(2,1)}, bf16[1024,2048]{1,0:T(8,128)(2,1)}) custom-call(f32[1024,2048]{1,0:T(8,128)} %get-tuple-element.151.gate_ref, f32[1024,2048]{1,0:T(8,128)} %get-tuple-element.152.up_ref, bf16[1024,768]{1,0:T(8,128)(2,1)} %bitcast.91, ...), custom_call_target="tpu_custom_call" | custom-call | flops 9663676416 | bytes 18874368 | tf_op jit(solution)/shard_map/expert_back_in/pallas_call | solution.py:709
  294.8 12.1 %all-to-all-done.2 = bf16[8,128,768]{2,1,0:T(8,128)(2,1)S(1)} async-done(((bf16[8,128,768]{2,1,0:T(8,128)(2,1)}), bf16[8,128,768]{2,1,0:T(8,128)(2,1)S(1)}, u32[]{:S(2)}, u32[]{:S(2)}) %all-to-all-start.2) | async-done | bytes 1572896 | tf_op jit(solution)/shard_map/all_to_all | solution.py:1148
  308.1 12.3 %mixture.1 = (bf16[512,768]{1,0:T(8,128)(2,1)}, f32[512,768]{1,0:T(8,128)}, f32[512,128]{1,0:T(8,128)}, f32[768,128]{1,0:T(8,128)}) custom-call(f32[512,768]{1,0:T(8,128)} %get-tuple-element.147.h_ref, bf16[512,768]{1,0:T(8,128)(2,1)} %bitcast.76, f32[512,128]{1,0:T(8,128)} %get-tuple-element.149.pr_ref, s32[512,2]{1,0:T(8,128)} %bitcast.80, ...), custom_call_target="tpu_custom_call" | custom-call | flops 1610612736 | bytes 4718592 | tf_op jit(solution)/shard_map/mixture/pallas_call | solution.py:826
  320.5 17.3 %expert_weight_grads.1 = bf16[4,3,192,2048]{3,2,1,0:T(8,128)(2,1)} custom-call(bf16[1024,768]{1,0:T(8,128)(2,1)} %bitcast.90, bf16[1024,768]{1,0:T(8,128)(2,1)} %bitcast.92, bf16[1024,2048]{1,0:T(8,128)(2,1)} %get-tuple-element.220.act_ref, bf16[1024,2048]{1,0:T(8,128)(2,1)} %get-tuple-element.221.dg_ref, bf16[1024,2048]{1,0:T(8,128)(2,1)} %get-tuple-element.222.du_ref), custom_call_target="tpu_custom_call" | custom-call | flops 9663676416 | bytes 18874368 | tf_op jit(solution)/shard_map/expert_weight_grads/pallas_call | solution.py:739
  341.5 37.1 %all-to-all-done.3 = bf16[8,128,768]{2,1,0:T(8,128)(2,1)S(1)} async-done(((bf16[8,128,768]{2,1,0:T(8,128)(2,1)}), bf16[8,128,768]{2,1,0:T(8,128)(2,1)S(1)}, u32[]{:S(2)}, u32[]{:S(2)}) %all-to-all-start.3) | async-done | bytes 1572896 | tf_op jit(solution)/shard_map/all_to_all | solution.py:1148
  379.8 8.9 %norm_two_back.1 = (f32[512,768]{1,0:T(8,128)}, bf16[512,768]{1,0:T(8,128)(2,1)}, bf16[768,512]{1,0:T(8,128)(2,1)}, f32[768,768]{1,0:T(8,128)}, f32[8,768]{1,0:T(8,128)}) custom-call(f32[512,768]{1,0:T(8,128)} %get-tuple-element.147.h_ref, bf16[512,768]{1,0:T(8,128)(2,1)} %bitcast.77, f32[512,768]{1,0:T(8,128)} %get-tuple-element.158.gn_ref, ...), custom_call_target="tpu_custom_call" | custom-call | flops 2013265920 | bytes 6291456 | tf_op jit(solution)/shard_map/norm_two_back/pallas_call | solution.py:880
  389.7 8.4 %attend_back_remote.4 = (f32[768,512]{1,0:T(8,128)}, bf16[256,768]{1,0:T(8,128)(2,1)}, bf16[256,768]{1,0:T(8,128)(2,1)}, f32[48,512]{1,0:T(8,128)}) custom-call(s32[12]{0:T(128)} %concatenate.51.sc_ref, bf16[768,512]{1,0:T(8,128)(2,1)} %get-tuple-element.125.qt_ref, bf16[512,768]{1,0:T(8,128)(2,1)} %get-tuple-element.126.q_ref, ...), custom_call_target="tpu_custom_call" | custom-call | flops 4026531840 | bytes 7864320 | tf_op jit(solution)/shard_map/attend_back_remote/pallas_call | solution.py:509
  402.8 10.9 %attend_back_remote.5 = (f32[768,512]{1,0:T(8,128)}, bf16[256,1536]{1,0:T(8,128)(2,1)}, bf16[256,1536]{1,0:T(8,128)(2,1)}) custom-call(s32[12]{0:T(128)} %concatenate.51.sc_ref, bf16[768,512]{1,0:T(8,128)(2,1)} %get-tuple-element.125.qt_ref, bf16[512,768]{1,0:T(8,128)(2,1)} %get-tuple-element.126.q_ref, bf16[768,512]{1,0:T(8,128)(2,1)} %get-tuple-element.160.dot_ref, ...), custom_call_target="tpu_custom_call" | custom-call | flops 8053063680 | bytes 9437184 | tf_op jit(solution)/shard_map/attend_back_remote/pallas_call | solution.py:509
  420.7 10.9 %attend_back_remote.6 = (f32[768,512]{1,0:T(8,128)}, bf16[256,1536]{1,0:T(8,128)(2,1)}, bf16[256,1536]{1,0:T(8,128)(2,1)}) custom-call(s32[12]{0:T(128)} %concatenate.51.sc_ref, bf16[768,512]{1,0:T(8,128)(2,1)} %get-tuple-element.125.qt_ref, bf16[512,768]{1,0:T(8,128)(2,1)} %get-tuple-element.126.q_ref, bf16[768,512]{1,0:T(8,128)(2,1)} %get-tuple-element.160.dot_ref, ...), custom_call_target="tpu_custom_call" | custom-call | flops 8053063680 | bytes 9437184 | tf_op jit(solution)/shard_map/attend_back_remote/pallas_call | solution.py:509
  431.5 5.2 collective-permute-done.11.gr_ref
  445.0 10.9 %attend_back_remote.7 = (f32[768,512]{1,0:T(8,128)}, bf16[256,1536]{1,0:T(8,128)(2,1)}, bf16[256,1536]{1,0:T(8,128)(2,1)}) custom-call(s32[12]{0:T(128)} %concatenate.51.sc_ref, bf16[768,512]{1,0:T(8,128)(2,1)} %get-tuple-element.125.qt_ref, bf16[512,768]{1,0:T(8,128)(2,1)} %get-tuple-element.126.q_ref, bf16[768,512]{1,0:T(8,128)(2,1)} %get-tuple-element.160.dot_ref, ...), custom_call_target="tpu_custom_call" | custom-call | flops 8053063680 | bytes 9437184 | tf_op jit(solution)/shard_map/attend_back_remote/pallas_call | solution.py:509
  455.9 5.9 %collective-permute-done.14.gr_ref = bf16[256,1536]{1,0:T(8,128)(2,1)S(1)} collective-permute-done((bf16[256,1536]{1,0:T(8,128)(2,1)}, bf16[256,1536]{1,0:T(8,128)(2,1)S(1)}, u32[]{:S(2)}, u32[]{:S(2)}) %collective-permute-start.14) | collective-permute-done | bytes 786464 | tf_op jit(solution)/shard_map/ppermute | solution.py:1056
  467.8 11.0 %attend_back_local.1 = (f32[512,768]{1,0:T(8,128)}, f32[256,1536]{1,0:T(8,128)}, f32[256,1536]{1,0:T(8,128)}) custom-call(s32[12]{0:T(128)} %concatenate.51.sc_ref, bf16[768,512]{1,0:T(8,128)(2,1)} %get-tuple-element.125.qt_ref, bf16[512,768]{1,0:T(8,128)(2,1)} %get-tuple-element.126.q_ref, bf16[768,512]{1,0:T(8,128)(2,1)} %get-tuple-element.160.dot_ref, ...), custom_call_target="tpu_custom_call" | custom-call | flops 4026531840 | bytes 6291456 | tf_op jit(solution)/shard_map/attend_back_local/pallas_call | solution.py:480
  478.7 8.1 %q_back.1 = (f32[512,768]{1,0:T(8,128)}, bf16[768,512]{1,0:T(8,128)(2,1)}, bf16[2,192,768]{2,1,0:T(8,128)(2,1)}, f32[2,192,768]{2,1,0:T(8,128)}) custom-call(s32[12]{0:T(128)} %concatenate.51.sc_ref, bf16[512,768]{1,0:T(8,128)(2,1)} %get-tuple-element.124.n_ref, f32[512,768]{1,0:T(8,128)} %get-tuple-element.204.dq_ref, f32[512,128]{1,0:T(8,128)} %pad_maximum_fusion.1.c_ref, ...), custom_call_target="tpu_custom_call" | custom-call | flops 1207959552 | bytes 4718592 | tf_op jit(solution)/shard_map/q_back/pallas_call | solution.py:956
  492.2 14.7 %collective-permute-done.17.refs_0_ = bf16[256,1536]{1,0:T(8,128)(2,1)S(1)} collective-permute-done((bf16[256,1536]{1,0:T(8,128)(2,1)}, bf16[256,1536]{1,0:T(8,128)(2,1)S(1)}, u32[]{:S(2)}, u32[]{:S(2)}) %collective-permute-start.17) | collective-permute-done | bytes 786464 | tf_op jit(solution)/shard_map/ppermute | solution.py:1056
  509.0 13.5 %kv_back.1 = (f32[512,768]{1,0:T(8,128)}, bf16[2,192,1536]{2,1,0:T(8,128)(2,1)}, f32[2,192,1536]{2,1,0:T(8,128)}) custom-call(s32[12]{0:T(128)} %concatenate.51.sc_ref, bf16[512,768]{1,0:T(8,128)(2,1)} %bitcast.72, bf16[768,512]{1,0:T(8,128)(2,1)} %get-tuple-element.205.nt_ref, f32[512,768]{1,0:T(8,128)} %get-tuple-element.206.gnq_ref, ...), custom_call_target="tpu_custom_call" | custom-call | flops 2415919104 | bytes 9437184 | tf_op jit(solution)/shard_map/kv_back/pallas_call | solution.py:1007
  554.4 5.5 all-to-all-start.5
  565.4 9.2 %all-to-all-done.5 = bf16[8,24,1536]{2,1,0:T(8,128)(2,1)S(1)} async-done(((bf16[8,24,1536]{2,1,0:T(8,128)(2,1)}), bf16[8,24,1536]{2,1,0:T(8,128)(2,1)S(1)}, u32[]{:S(2)}, u32[]{:S(2)}) %all-to-all-start.5) | async-done | bytes 589856 | tf_op jit(solution)/shard_map/all_to_all | solution.py:1078
  (195 shorter events, 135.3 us)
Async XLA Ops:
  7.2 72.7 %all-gather.4.cloned.1.call-start = ((), (), s32[]{:S(2)}) async-start(), calls=%async_computation.7 | async-start | bytes 5068800 | tf_op jit(solution)/shard_map/all_gather | solution.py:1114
  12.7 215.7 %all-gather.6.cloned.1.call-start = ((), (), s32[]{:S(2)}) async-start(), calls=%async_computation.9 | async-start | bytes 11796480 | tf_op jit(solution)/shard_map/all_gather | solution.py:1178
  91.0 20.0 %collective-permute-start.1 = (bf16[256,1536]{1,0:T(8,128)(2,1)}, bf16[256,1536]{1,0:T(8,128)(2,1)S(1)}, u32[]{:S(2)}, u32[]{:S(2)}) collective-permute-start(bf16[256,1536]{1,0:T(8,128)(2,1)} %get-tuple-element.127.kv_ref), channel_id=1, source_target_pairs={{0,1},{2,0},{4,2},{6,4},{7,6},{5,7},{3,5},{1,3},{8,9},{10,8},{12,1... | collective-permute-start | bytes 2359304 | tf_op jit(solution)/shard_map/ppermute | solution.py:1056
  92.5 19.7 %collective-permute-start = (bf16[256,1536]{1,0:T(8,128)(2,1)}, bf16[256,1536]{1,0:T(8,128)(2,1)S(1)}, u32[]{:S(2)}, u32[]{:S(2)}) collective-permute-start(bf16[256,1536]{1,0:T(8,128)(2,1)} %get-tuple-element.127.kv_ref), channel_id=1, source_target_pairs={{0,2},{2,4},{4,6},{6,7},{7,5},{5,3},{3,1},{1,0},{8,10},{10,12},{12... | collective-permute-start | bytes 2359304 | tf_op jit(solution)/shard_map/ppermute | solution.py:1056
  112.1 18.7 %collective-permute-start.2 = (bf16[256,1536]{1,0:T(8,128)(2,1)S(1)}, bf16[256,1536]{1,0:T(8,128)(2,1)S(1)}, u32[]{:S(2)}, u32[]{:S(2)}) collective-permute-start(bf16[256,1536]{1,0:T(8,128)(2,1)S(1)} %collective-permute-done.refs_0_.refs_1_), channel_id=1, source_target_pairs={{0,2},{2,4},{4,6},{6,7},{7,5},{5,3},{3,1},{1,0},{8,10},{10,12},{12... | collective-permute-start | bytes 2359304 | tf_op jit(solution)/shard_map/ppermute | solution.py:1056
  112.7 18.5 %collective-permute-start.3 = (bf16[256,1536]{1,0:T(8,128)(2,1)S(1)}, bf16[256,1536]{1,0:T(8,128)(2,1)}, u32[]{:S(2)}, u32[]{:S(2)}) collective-permute-start(bf16[256,1536]{1,0:T(8,128)(2,1)S(1)} %collective-permute-done.1.refs_1_.refs_0_), channel_id=1, source_target_pairs={{0,1},{2,0},{4,2},{6,4},{7,6},{5,7},{3,5},{1,3},{8,9},{10,8},{12,1... | collective-permute-start | bytes 2359304 | tf_op jit(solution)/shard_map/ppermute | solution.py:1056
  131.8 18.2 %collective-permute-start.4 = (bf16[256,1536]{1,0:T(8,128)(2,1)}, bf16[256,1536]{1,0:T(8,128)(2,1)S(1)}, u32[]{:S(2)}, u32[]{:S(2)}) collective-permute-start(bf16[256,1536]{1,0:T(8,128)(2,1)} %copy-done.29), channel_id=1, source_target_pairs={{0,2},{2,4},{4,6},{6,7},{7,5},{5,3},{3,1},{1,0},{8,10},{10,12},{12... | collective-permute-start | bytes 2359304 | tf_op jit(solution)/shard_map/ppermute | solution.py:1056
  132.6 17.6 %collective-permute-start.5 = (bf16[256,1536]{1,0:T(8,128)(2,1)}, bf16[256,1536]{1,0:T(8,128)(2,1)S(1)}, u32[]{:S(2)}, u32[]{:S(2)}) collective-permute-start(bf16[256,1536]{1,0:T(8,128)(2,1)} %collective-permute-done.3.refs_1_.refs_0_), channel_id=1, source_target_pairs={{0,1},{2,0},{4,2},{6,4},{7,6},{5,7},{3,5},{1,3},{8,9},{10,8},{12,1... | collective-permute-start | bytes 2359304 | tf_op jit(solution)/shard_map/ppermute | solution.py:1056
  133.9 20.4 %copy-start = (s32[2,256,2]{2,1,0:T(8,128)}, s32[2,256,2]{2,1,0:T(8,128)S(1)}, u32[]{:S(2)}) copy-start(s32[2,256,2]{2,1,0:T(8,128)S(1)} %copy.139) | copy-start | bytes 12292
  152.2 14.8 %collective-permute-start.7 = (bf16[256,768]{1,0:T(8,128)(2,1)S(1)}, bf16[256,768]{1,0:T(8,128)(2,1)}, u32[]{:S(2)}, u32[]{:S(2)}) collective-permute-start(bf16[256,768]{1,0:T(8,128)(2,1)S(1)} %slice.71), channel_id=1, source_target_pairs={{0,1},{2,0},{4,2},{6,4},{7,6},{5,7},{3,5},{1,3},{8,9},{10,8},{12,1... | collective-permute-start | bytes 1179656 | tf_op jit(solution)/shard_map/ppermute | solution.py:1056
  153.7 13.2 %collective-permute-start.6 = (bf16[256,768]{1,0:T(8,128)(2,1)S(1)}, bf16[256,768]{1,0:T(8,128)(2,1)}, u32[]{:S(2)}, u32[]{:S(2)}) collective-permute-start(bf16[256,768]{1,0:T(8,128)(2,1)S(1)} %slice.70), channel_id=1, source_target_pairs={{0,2},{2,4},{4,6},{6,7},{7,5},{5,3},{3,1},{1,0},{8,10},{10,12},{12... | collective-permute-start | bytes 1179656 | tf_op jit(solution)/shard_map/ppermute | solution.py:1056
  183.8 39.8 %all-to-all-start = ((bf16[8,128,768]{2,1,0:T(8,128)(2,1)}), bf16[8,128,768]{2,1,0:T(8,128)(2,1)S(1)}, u32[]{:S(2)}, u32[]{:S(2)}) async-start(bf16[8,128,768]{2,1,0:T(8,128)(2,1)} %bitcast.96), calls=%async_computation | async-start | bytes 3145728 | tf_op jit(solution)/shard_map/all_to_all | solution.py:1148
  224.7 40.2 %all-to-all-start.1 = ((bf16[8,128,768]{2,1,0:T(8,128)(2,1)}), bf16[8,128,768]{2,1,0:T(8,128)(2,1)S(1)}, u32[]{:S(2)}, u32[]{:S(2)}) async-start(bf16[8,128,768]{2,1,0:T(8,128)(2,1)} %bitcast.95), calls=%async_computation.1 | async-start | bytes 3145728 | tf_op jit(solution)/shard_map/all_to_all | solution.py:1148
  266.1 40.8 %all-to-all-start.2 = ((bf16[8,128,768]{2,1,0:T(8,128)(2,1)}), bf16[8,128,768]{2,1,0:T(8,128)(2,1)S(1)}, u32[]{:S(2)}, u32[]{:S(2)}) async-start(bf16[8,128,768]{2,1,0:T(8,128)(2,1)} %bitcast.94), calls=%async_computation.2 | async-start | bytes 3145728 | tf_op jit(solution)/shard_map/all_to_all | solution.py:1148
  269.8 274.4 %reduce-scatter.2.cloned.1.call-start = ((), (), s32[]{:S(2)}) async-start(), calls=%async_computation.8 | async-start | bytes 11796480 | tf_op jit(solution)/shard_map/reduce_scatter | solution.py:1215
  337.8 40.8 %all-to-all-start.3 = ((bf16[8,128,768]{2,1,0:T(8,128)(2,1)}), bf16[8,128,768]{2,1,0:T(8,128)(2,1)S(1)}, u32[]{:S(2)}, u32[]{:S(2)}) async-start(bf16[8,128,768]{2,1,0:T(8,128)(2,1)} %bitcast.28), calls=%async_computation.3 | async-start | bytes 3145728 | tf_op jit(solution)/shard_map/all_to_all | solution.py:1148
  398.1 15.5 %collective-permute-start.8 = (bf16[256,768]{1,0:T(8,128)(2,1)}, bf16[256,768]{1,0:T(8,128)(2,1)}, u32[]{:S(2)}, u32[]{:S(2)}) collective-permute-start(bf16[256,768]{1,0:T(8,128)(2,1)} %get-tuple-element.165), channel_id=1, source_target_pairs={{0,2},{2,4},{4,6},{6,7},{7,5},{5,3},{3,1},{1,0},{8,10},{10,12},{12... | collective-permute-start | bytes 1179656 | tf_op jit(solution)/shard_map/ppermute | solution.py:1056
  398.2 15.5 %collective-permute-start.9 = (bf16[256,768]{1,0:T(8,128)(2,1)}, bf16[256,768]{1,0:T(8,128)(2,1)}, u32[]{:S(2)}, u32[]{:S(2)}) collective-permute-start(bf16[256,768]{1,0:T(8,128)(2,1)} %get-tuple-element.166), channel_id=1, source_target_pairs={{0,1},{2,0},{4,2},{6,4},{7,6},{5,7},{3,5},{1,3},{8,9},{10,8},{12,1... | collective-permute-start | bytes 1179656 | tf_op jit(solution)/shard_map/ppermute | solution.py:1056
  402.7 11.0 %collective-permute-start.10 = (bf16[2,192,896]{2,1,0:T(8,128)(2,1)S(1)}, bf16[2,192,896]{2,1,0:T(8,128)(2,1)S(1)}, u32[]{:S(2)}, u32[]{:S(2)}) collective-permute-start(bf16[2,192,896]{2,1,0:T(8,128)(2,1)S(1)} %fusion.4), channel_id=1, source_target_pairs={{0,8},{8,0},{16,24},{24,16},{1,9},{9,1},{17,25},{25,17},{2,10},{10... | collective-permute-start | bytes 2064392 | tf_op jit(solution)/shard_map/ppermute | solution.py:1064
  416.5 20.3 %collective-permute-start.11 = (bf16[256,1536]{1,0:T(8,128)(2,1)}, bf16[256,1536]{1,0:T(8,128)(2,1)}, u32[]{:S(2)}, u32[]{:S(2)}) collective-permute-start(bf16[256,1536]{1,0:T(8,128)(2,1)} %get-tuple-element.178), channel_id=1, source_target_pairs={{0,2},{2,4},{4,6},{6,7},{7,5},{5,3},{3,1},{1,0},{8,10},{10,12},{12... | collective-permute-start | bytes 2359304 | tf_op jit(solution)/shard_map/ppermute | solution.py:1056
  416.6 21.9 %collective-permute-start.12 = (bf16[256,1536]{1,0:T(8,128)(2,1)}, bf16[256,1536]{1,0:T(8,128)(2,1)}, u32[]{:S(2)}, u32[]{:S(2)}) collective-permute-start(bf16[256,1536]{1,0:T(8,128)(2,1)} %get-tuple-element.179), channel_id=1, source_target_pairs={{0,1},{2,0},{4,2},{6,4},{7,6},{5,7},{3,5},{1,3},{8,9},{10,8},{12,1... | collective-permute-start | bytes 2359304 | tf_op jit(solution)/shard_map/ppermute | solution.py:1056
  419.8 11.7 %collective-permute-start.13 = (bf16[192,896]{1,0:T(8,128)(2,1)S(1)}, bf16[192,896]{1,0:T(8,128)(2,1)S(1)}, u32[]{:S(2)}, u32[]{:S(2)}) collective-permute-start(bf16[192,896]{1,0:T(8,128)(2,1)S(1)} %fusion.6), channel_id=1, source_target_pairs={{0,16},{16,0},{8,24},{24,8},{1,17},{17,1},{9,25},{25,9},{2,18},{18... | collective-permute-start | bytes 1032200 | tf_op jit(solution)/shard_map/ppermute | solution.py:1072
  441.4 20.4 %collective-permute-start.14 = (bf16[256,1536]{1,0:T(8,128)(2,1)}, bf16[256,1536]{1,0:T(8,128)(2,1)S(1)}, u32[]{:S(2)}, u32[]{:S(2)}) collective-permute-start(bf16[256,1536]{1,0:T(8,128)(2,1)} %get-tuple-element.189), channel_id=1, source_target_pairs={{0,2},{2,4},{4,6},{6,7},{7,5},{5,3},{3,1},{1,0},{8,10},{10,12},{12... | collective-permute-start | bytes 2359304 | tf_op jit(solution)/shard_map/ppermute | solution.py:1056
  444.9 19.2 %collective-permute-start.15 = (bf16[256,1536]{1,0:T(8,128)(2,1)}, bf16[256,1536]{1,0:T(8,128)(2,1)S(1)}, u32[]{:S(2)}, u32[]{:S(2)}) collective-permute-start(bf16[256,1536]{1,0:T(8,128)(2,1)} %get-tuple-element.190), channel_id=1, source_target_pairs={{0,1},{2,0},{4,2},{6,4},{7,6},{5,7},{3,5},{1,3},{8,9},{10,8},{12,1... | collective-permute-start | bytes 2359304 | tf_op jit(solution)/shard_map/ppermute | solution.py:1056
  486.8 2.2 collective-permute-start.16
  486.8 20.2 %collective-permute-start.17 = (bf16[256,1536]{1,0:T(8,128)(2,1)}, bf16[256,1536]{1,0:T(8,128)(2,1)S(1)}, u32[]{:S(2)}, u32[]{:S(2)}) collective-permute-start(bf16[256,1536]{1,0:T(8,128)(2,1)} %get-tuple-element.212), channel_id=1, source_target_pairs={{0,2},{2,4},{4,6},{6,7},{7,5},{5,3},{3,1},{1,0},{8,10},{10,12},{12... | collective-permute-start | bytes 2359304 | tf_op jit(solution)/shard_map/ppermute | solution.py:1056
  488.3 19.8 %collective-permute-start.18 = (bf16[256,1536]{1,0:T(8,128)(2,1)}, bf16[256,1536]{1,0:T(8,128)(2,1)S(1)}, u32[]{:S(2)}, u32[]{:S(2)}) collective-permute-start(bf16[256,1536]{1,0:T(8,128)(2,1)} %get-tuple-element.213), channel_id=1, source_target_pairs={{0,1},{2,0},{4,2},{6,4},{7,6},{5,7},{3,5},{1,3},{8,9},{10,8},{12,1... | collective-permute-start | bytes 2359304 | tf_op jit(solution)/shard_map/ppermute | solution.py:1056
  522.5 3.1 collective-permute-start.19
  522.7 9.5 %collective-permute-start.21 = (bf16[192,768]{1,0:T(8,128)(2,1)S(1)}, bf16[192,768]{1,0:T(8,128)(2,1)S(1)}, u32[]{:S(2)}, u32[]{:S(2)}) collective-permute-start(bf16[192,768]{1,0:T(8,128)(2,1)S(1)} %fusion.7), channel_id=1, source_target_pairs={{0,16},{16,0},{8,24},{24,8},{1,17},{17,1},{9,25},{25,9},{2,18},{18... | collective-permute-start | bytes 884744 | tf_op jit(solution)/shard_map/ppermute | solution.py:1072
  533.2 21.2 %all-to-all-start.4 = ((bf16[8,24,1664]{2,1,0:T(8,128)(2,1)}), bf16[8,24,1664]{2,1,0:T(8,128)(2,1)}, u32[]{:S(2)}, u32[]{:S(2)}) async-start(bf16[8,24,1664]{2,1,0:T(8,128)(2,1)} %fusion.1), calls=%async_computation.5 | async-start | bytes 1277952 | tf_op jit(solution)/shard_map/all_to_all | solution.py:1078
  538.3 15.1 %collective-permute-start.20 = (bf16[192,1536]{1,0:T(8,128)(2,1)}, bf16[192,1536]{1,0:T(8,128)(2,1)S(1)}, u32[]{:S(2)}, u32[]{:S(2)}) collective-permute-start(bf16[192,1536]{1,0:T(8,128)(2,1)} %fusion.5), channel_id=1, source_target_pairs={{0,16},{16,0},{8,24},{24,8},{1,17},{17,1},{9,25},{25,9},{2,18},{18... | collective-permute-start | bytes 1769480 | tf_op jit(solution)/shard_map/ppermute | solution.py:1072
  554.4 20.2 %all-to-all-start.5 = ((bf16[8,24,1536]{2,1,0:T(8,128)(2,1)}), bf16[8,24,1536]{2,1,0:T(8,128)(2,1)S(1)}, u32[]{:S(2)}, u32[]{:S(2)}) async-start(bf16[8,24,1536]{2,1,0:T(8,128)(2,1)} %bitcast.50), calls=%async_computation.6 | async-start | bytes 1179648 | tf_op jit(solution)/shard_map/all_to_all | solution.py:1078
  (30 other events, 158.5 us)
Sparse Core Ops, SparseCore 0:
  12.8 67.0 all-gather.3
  81.5 62.5 all-gather.5
  337.9 76.2 reduce-scatter.1

commit v3 on v2

--- a/solution.py
+++ b/solution.py
@@ -625,7 +625,8 @@
     )(x, att, pack, pack, gain, res, rt, tr)
 
 
-def expert_fwd_body(x_ref, w_ref, o_ref, gate_ref, up_ref, acc_ref):
+def expert_fwd_body(blocks, sc_ref, x_ref, w_ref, gate_ref, up_ref, *refs):
+    o_refs, acc_ref = refs[:-1], refs[-1]
     step = pl.program_id(0)
     x = x_ref[...]
     wide = w_ref.shape[-1]
@@ -649,23 +650,31 @@
 
     @pl.when(step == pl.num_programs(0) - 1)
     def _():
-        o_ref[...] = acc_ref[...].astype(BF16)
-
-
-def expert_fwd(xr, w):
+        if blocks == 1:
+            o_refs[0][...] = acc_ref[...].astype(BF16)
+        else:
+            size = acc_ref.shape[0] // blocks
+            for k in range(blocks):
+                first = pl.multiple_of((sc_ref[0] ^ k) * size, size)
+                o_refs[k][...] = acc_ref[pl.ds(first, size), :].astype(BF16)
+
+
+def expert_fwd(sc, xr, w, blocks):
     rows = xr.shape[0]
     shards, _, per, wide = w.shape
     part = min(wide, 256)
     return pl.pallas_call(
-        expert_fwd_body,
+        functools.partial(expert_fwd_body, blocks),
         grid=(wide // part,),
-        in_specs=[whole((rows, D)), spec((shards, 3, per, part), lambda i: (0, 0, 0, i))],
-        out_specs=[whole((rows, D))] + [spec((rows, part), lambda i: (0, i))] * 2,
-        out_shape=[shape((rows, D), BF16)] + [shape((rows, wide), F32)] * 2,
+        in_specs=[
+            SMEM_SPEC, whole((rows, D)), spec((shards, 3, per, part), lambda i: (0, 0, 0, i)),
+        ],
+        out_specs=[spec((rows, part), lambda i: (0, i))] * 2 + [whole((rows // blocks, D))] * blocks,
+        out_shape=[shape((rows, wide), F32)] * 2 + [shape((rows // blocks, D), BF16)] * blocks,
         scratch_shapes=[pltpu.VMEM((rows, D), F32)],
         name="expert_forward",
         **params((6 * rows * D * wide, 6 * D * wide)),
-    )(xr, w)
+    )(sc, xr, w)
 
 
 def expert_in_body(gate_ref, up_ref, g_ref, w_ref, gi_ref, act_ref, dg_ref, du_ref, acc_ref):
@@ -748,12 +757,10 @@
     )(xr, low, act, d_gate, d_up)
 
 
-def mix_body(
-    h_ref, g_ref, pr_ref, rt_ref, tc_ref, ret_ref, n_ref, sw_ref, rows_ref,
-    out_ref, gn_ref, gl_ref, gs_ref,
-):
+def mix_body(h_ref, g_ref, pr_ref, rt_ref, tc_ref, n_ref, sw_ref, rows_ref, *refs):
+    ret_refs, (out_ref, gn_ref, gl_ref, gs_ref) = refs[:-4], refs[-4:]
     t = h_ref.shape[0]
-    slots = ret_ref.shape[0]
+    slots = sum(ret_ref.shape[0] for ret_ref in ret_refs)
     hidden = h_ref[...]
     g16 = g_ref[...]
     g = g16.astype(F32)
@@ -763,7 +770,7 @@
     lane = lax.broadcasted_iota(jnp.int32, (t, LANES), 1)
     slot = lax.broadcasted_iota(jnp.int32, (t, slots), 1)
     first = EXPERTS + 4
-    ret = ret_ref[...]
+    ret = jnp.concatenate([ret_ref[...] for ret_ref in ret_refs], axis=0)
     c0 = [pr[:, first + 2 * k : first + 2 * k + 1] for k in range(2)]
     c1 = [pr[:, first + 2 * k + 1 : first + 2 * k + 2] for k in range(2)]
     total = hidden
@@ -819,7 +826,7 @@
 def mix_call(hidden, g, pr, rt, tc, ret, low, pack, rows):
     t = hidden.shape[0]
     half = min(t, LANES)
-    slots = ret.shape[0]
+    slots = sum(block.shape[0] for block in ret)
     tile = spec((half, D), lambda i: (i, 0))
     lane_tile = spec((half, LANES), lambda i: (i, 0))
     pair = spec((half, 2), lambda i: (i, 0))
@@ -827,16 +834,16 @@
         mix_body,
         grid=(t // half,),
         in_specs=[
-            tile, tile, lane_tile, pair, pair, whole((slots, D)), tile, small_w_spec(),
-            whole((8, D)),
-        ],
+            tile, tile, lane_tile, pair, pair, tile, small_w_spec(), whole((8, D)),
+        ]
+        + [whole(block.shape) for block in ret],
         out_specs=[tile, tile, lane_tile, whole((D, LANES))],
         out_shape=[
             shape((t, D), BF16), shape((t, D), F32), shape((t, LANES), F32), shape((D, LANES), F32),
         ],
         name="mixture",
         **params((4 * t * slots * D, 12 * t * D)),
-    )(hidden, g, pr, rt, tc, ret, low, pack, rows)
+    )(hidden, g, pr, rt, tc, low, pack, rows, *ret)
 
 
 def norm_back_body(
@@ -858,7 +865,7 @@
     d_out = dot_nt(gb, ow_ref[...]).astype(BF16)
     do_ref[...] = d_out
     dot_ref[...] = d_out.T
-    gow = dot(att_ref[...].T, gb)
+    gow = dot(att_ref[...].astype(BF16), gb)
     gain = jnp.sum(gn * hidden * q, axis=0, keepdims=True)
 
     @pl.when(pl.program_id(0) == 0)
@@ -882,7 +889,7 @@
         grid=(t // half,),
         in_specs=[
             tile, tile, tile, spec((half, 2), lambda i: (i, 0)), whole((slots, D)), whole((8, D)),
-            out_w_spec(), tile,
+            out_w_spec(), spec((D, half), lambda i: (0, i)),
         ],
         out_specs=[tile, tile, spec((D, half), lambda i: (0, i)), whole((D, D)), whole((8, D))],
         out_shape=[
@@ -892,6 +899,24 @@
         name="norm_two_back",
         **params((2 * t * slots * D + 4 * t * D * D, 16 * t * D)),
     )(hidden, g, gn, tc, ret, rows, pack, att)
+
+
+def turn_body(x_ref, o_ref):
+    o_ref[...] = x_ref[...].T
+
+
+def turn(x):
+    rows, wide = x.shape
+    part = 256
+    return pl.pallas_call(
+        turn_body,
+        grid=(wide // part,),
+        in_specs=[spec((rows, part), lambda i: (0, i))],
+        out_specs=spec((part, rows), lambda i: (i, 0)),
+        out_shape=shape((wide, rows), x.dtype),
+        name="turn",
+        **params((rows * wide, 4 * rows * wide)),
+    )(x)
 
 
 def store_grad(sc_ref, split, value, refs):
@@ -920,13 +945,8 @@
     return [tile, tile], [shape(dims, BF16), shape(dims, F32)]
 
 
-def q_back_body(split, sc_ref, n_ref, dq_ref, c_ref, s_ref, w_ref, gn_ref, nt_ref, *refs):
+def q_back_body(split, sc_ref, nt_ref, dq_ref, c_ref, s_ref, w_ref, gn_ref, *refs):
     step = pl.program_id(0)
-
-    @pl.when(step == 0)
-    def _():
-        nt_ref[...] = n_ref[...].T
-
     cosine = c_ref[...]
     sine = s_ref[...]
     v0 = dq_ref[:, :LANES]
@@ -950,21 +970,21 @@
         gn_ref[...] += gn
 
 
-def q_back_call(sc, low, dq, cosine, sine, pack, split):
-    t = low.shape[0]
+def q_back_call(sc, low_t, dq, cosine, sine, pack, split):
+    t = low_t.shape[1]
     specs, shapes = grad_outs(split, D)
     return pl.pallas_call(
         functools.partial(q_back_body, split),
         grid=(PAIRS // 2,),
         in_specs=[
-            SMEM_SPEC, whole((t, D)), spec((t, 2 * LANES), lambda i: (0, i)), whole((t, LANES)),
+            SMEM_SPEC, whole((D, t)), spec((t, 2 * LANES), lambda i: (0, i)), whole((t, LANES)),
             whole((t, LANES)), spec((D, 2 * LANES), lambda i: (0, i)),
         ],
-        out_specs=[whole((t, D)), whole((D, t))] + specs,
-        out_shape=[shape((t, D), F32), shape((D, t), BF16)] + shapes,
+        out_specs=[whole((t, D))] + specs,
+        out_shape=[shape((t, D), F32)] + shapes,
         name="q_back",
         **params((4 * t * D * D, 12 * t * D)),
-    )(sc, low, dq, cosine, sine, pack)
+    )(sc, low_t, dq, cosine, sine, pack)
 
 
 def kv_back_body(
@@ -1080,6 +1100,38 @@
     )
 
 
+def swap_blocks(blocks):
+    out = [blocks[0]]
+    for k in range(1, 8):
+        out.append(lax.ppermute(blocks[k], "expert", [(e, e ^ k) for e in range(8)]))
+    return out
+
+
+def spread_body(sc_ref, keep_ref, got_ref, *refs):
+    o_refs, sum_ref = refs[:-1], refs[-1]
+    sum_ref[...] = keep_ref[...] + got_ref[...].astype(F32)
+    size = sum_ref.shape[0] // 8
+    for k in range(8):
+        first = pl.multiple_of((sc_ref[0] ^ k) * size, size)
+        o_refs[k][...] = sum_ref[pl.ds(first, size), :].astype(BF16)
+
+
+def spread_call(sc, keep, got):
+    rows, w = keep.shape
+    part = w // 2
+    tile = spec((rows, part), lambda i: (0, i))
+    return pl.pallas_call(
+        spread_body,
+        grid=(2,),
+        in_specs=[SMEM_SPEC, tile, tile],
+        out_specs=[spec((rows // 8, part), lambda i: (0, i))] * 8,
+        out_shape=[shape((rows // 8, w), BF16)] * 8,
+        scratch_shapes=[pltpu.VMEM((rows, part), F32)],
+        name="spread",
+        **params((rows * w, 8 * rows * w)),
+    )(sc, keep, got)
+
+
 def add_up(got):
     return jnp.sum(got.astype(F32), axis=0)
 
@@ -1201,14 +1253,21 @@
     )
     x_got = exchange(to_owners(x_send))
     g_send = grad_rows_call(g, pr, target_rows, slots)
+    low_one_t = turn(low_one)
     x_got, g_send = tie(x_got, g_send)
     g_got = exchange(to_owners(g_send))
-    expert_rows, gate_pre, up_pre = expert_fwd(x_got, weights)
-    out_back = from_owners(expert_rows)
+    gate_pre, up_pre, *expert_rows = expert_fwd(sc, x_got, weights, 8 if ring else 1)
+    if ring:
+        out_back = swap_blocks(expert_rows)
+        mix_target = jnp.where(flat < EXPERTS, (flat ^ me) * capacity + slot_index, -1)
+        mix_cols = jnp.transpose(mix_target.reshape(2, t))
+    else:
+        out_back = [from_owners(expert_rows[0])]
+        mix_cols = target_cols
     grad_in, act, d_gate, d_up = expert_in(gate_pre, up_pre, g_got, weights)
     in_back = from_owners(grad_in)
     output, gn, grad_logits, grad_small = mix_call(
-        hidden, g, pr, picked, target_cols, out_back, low_two, pack, rows_two
+        hidden, g, pr, picked, mix_cols, out_back, low_two, pack, rows_two
     )
     act, gn = tie(act, gn)
     grad_w = expert_weights(x_got, g_got, act, d_gate, d_up, weights.shape)
@@ -1218,7 +1277,7 @@
     per = gate_weight.shape[0]
     grad_expert = [grad_expert[i * per : (i + 1) * per].astype(F32) for i in range(3)]
     gh, d_att, d_att_t, grad_ow, gg_two = norm_back_call(
-        hidden, g, gn, target_cols, in_back, rows_two, pack, att
+        hidden, g, gn, target_cols, in_back, rows_two, pack, att_t
     )
 
     early = jnp.concatenate(
@@ -1263,7 +1322,7 @@
         dkv_cont = lax.psum_scatter(
             dkv_cont, "expert", scatter_dimension=0, tiled=True, axis_index_groups=cont_groups
         )
-    gn_q, low_one_t, *grad_q = q_back_call(sc, low_one, dq, cosine, sine, pack, ring)
+    gn_q, *grad_q = q_back_call(sc, low_one_t, dq, cosine, sine, pack, ring)
     if ring:
         got_q = swap_core(grad_q[0])
         keep_q, got_q = add_and_cross(grad_q[1], got_q)
@@ -1283,7 +1342,10 @@
         got_kv, output, grad_input, *grad_expert = tie(got_kv, output, grad_input, *grad_expert)
         summed = add_up(got_q)
         early, late_q = summed[:, : D + LANES], summed[:, D + LANES :]
-        late_kv = add_up(add_and_scatter(keep_kv, got_kv))
+        blocks = swap_blocks(spread_call(sc, keep_kv, got_kv))
+        late_kv = blocks[0].astype(F32)
+        for block in blocks[1:]:
+            late_kv = late_kv + block.astype(F32)
     else:
         late_q, late_kv = scatter_all(grad_q[0]), scatter_all(grad_kv[0])
     per = late_kv.shape[0]

time: 592 us -> 620 us (1.047)
  starting transfers between devices: 47.8 us -> 65.1 us
    ppermute x0 -> x14, waiting for transfers between devices: none -> 39 us  [swap_blocks(): lax.ppermute(blocks[k], 'expert', [(e, e ^ k) for e in range(8)])]
    all_to_all x4 -> x3, waiting for transfers between devices: 94.8 us -> 65.5 us  [exchange(): lax.all_to_all(rows, 'expert', split_axis=0, concat_axis=0, tiled=True)]
    ppermute x0 -> x14, starting transfers between devices: none -> 23.2 us  [swap_blocks(): lax.ppermute(blocks[k], 'expert', [(e, e ^ k) for e in range(8)])]
    pallas_call x1 -> x3, Pallas kernels: 19.1 us -> 24.4 us  [the longest x1 19.1 us: expert_fwd(): pl.pallas_call(functools.partial(expert_fwd_body, blocks), grid=(wide //...]
    all_to_all x4 -> x3, starting transfers between devices: 16.7 us -> 18.6 us  [exchange(): lax.all_to_all(rows, 'expert', split_axis=0, concat_axis=0, tiled=True)]
    unnamed x69 -> x79, local copies, waits for them, and re-layouts: 14.2 us -> 13.6 us
  transfers between devices with their start and end apart: 31 -> 43, of which waited for: 23 -> 27; matrix products, arithmetic and copies ran while one was open for 8% -> 8% of each run, Pallas kernels for 35% -> 32%
where the time goes in v3:
time: 620 us; the launch traced here: 610 us
  Pallas kernels  239 us (39%)
  waiting for transfers between devices  227 us (37%)
  starting transfers between devices  65.1 us (10%)
  local copies, waits for them, and re-layouts  40.3 us (6%)
  other arithmetic  23.6 us (4%)
  between operations  14.6 us (2%)
    all_to_all x3, waiting for transfers between devices, exchange(): lax.all_to_all(rows, 'expert', split_axis=0, concat_axis=0, tiled=True)  65.5 us
    all_gather x1, waiting for transfers between devices, per_device(): lax.all_gather(jnp.concatenate([qkv_weight, out_weight, small], axis=1),...  58.7 us
    ppermute x16, waiting for transfers between devices, along_ring(): return lax.ppermute(array, 'expert', pairs)  46.4 us
    pallas_call x4, Pallas kernels, bwd_remote(): pl.pallas_call(functools.partial(bwd_remote_body, tuple(offsets), len(kvs...  41 us
    ppermute x14, waiting for transfers between devices, swap_blocks(): lax.ppermute(blocks[k], 'expert', [(e, e ^ k) for e in range(8)])  39 us
    pallas_call x4, Pallas kernels, fwd_remote(): pl.pallas_call(functools.partial(fwd_remote_body, tuple(offsets), len(kvs...  38 us
    pallas_call x1, Pallas kernels, expert_in(): pl.pallas_call(expert_in_body, grid=(wide // part,), in_specs=[tile, tile...  23.7 us
    ppermute x14, starting transfers between devices, swap_blocks(): lax.ppermute(blocks[k], 'expert', [(e, e ^ k) for e in range(8)])  23.2 us
  transfers between devices with their start and end apart: 43, of which 27 were waited for; matrix products, arithmetic and copies ran while one was open for 8% of the time, Pallas kernels for 32%

profile of v3, /device:TPU:0, one launch (start us, length us, event | category | flops | bytes accessed | tf_op | source)
XLA Modules:
  0.0 610.0 jit_solution(3750977443365326875)
XLA Ops:
  21.2 58.7 %all-gather.4.cloned.1.call-done.wq_ref.wk_ref.wv_ref.ow_ref.sw_ref.w_ref = bf16[768,3200]{1,0:T(8,128)(2,1)} async-done(((bf16[24,3200]{1,0:T(8,128)(2,1)}), bf16[768,3200]{1,0:T(8,128)(2,1)}) %all-gather.4.cloned.1.call-update) | async-done | bytes 4915216 | tf_op jit(solution)/shard_map/all_gather | solution.py:1166
  82.0 9.0 %qkv_rope.1 = (bf16[512,768]{1,0:T(8,128)(2,1)}, bf16[512,768]{1,0:T(8,128)(2,1)}, bf16[768,512]{1,0:T(8,128)(2,1)}, bf16[256,1536]{1,0:T(8,128)(2,1)}, bf16[256,1536]{1,0:T(8,128)(2,1)}) custom-call(bf16[512,768]{1,0:T(8,128)(2,1)} %bitcast.72, f32[1,768]{1,0:T(1,128)} %copy.141.gain_ref, ...), custom_call_target="tpu_custom_call" | custom-call | flops 1811939328 | bytes 3538944 | tf_op jit(solution)/shard_map/qkv_rope/pallas_call | solution.py:99
  95.6 9.9 %attend_local.1 = (f32[48,512]{1,0:T(8,128)}, f32[768,512]{1,0:T(8,128)}) custom-call(s32[12]{0:T(128)} %concatenate.51.sc_ref, bf16[768,512]{1,0:T(8,128)(2,1)} %get-tuple-element.139.qt_ref, bf16[256,1536]{1,0:T(8,128)(2,1)} %get-tuple-element.141.kv_ref, bf16[256,1536]{1,0:T(8,128)(2,1)} %get-tuple-element.142.kvo_ref), custom_call_target="tpu_custom_call" | custom-call | flops 1610612736 | bytes 1572864 | tf_op jit(solution)/shard_map/attend_local/pallas_call | solution.py:261
  105.5 5.4 collective-permute-done.refs_0_.refs_1_
  114.0 10.2 %attend_remote.4 = (f32[48,512]{1,0:T(8,128)}, f32[768,512]{1,0:T(8,128)}) custom-call(s32[12]{0:T(128)} %concatenate.51.sc_ref, bf16[768,512]{1,0:T(8,128)(2,1)} %get-tuple-element.139.qt_ref, bf16[256,1536]{1,0:T(8,128)(2,1)} %copy-done.32, bf16[256,1536]{1,0:T(8,128)(2,1)} %copy-done.33, f32[48,512]{1,0:T(8,128)} %get-tuple-element.146.refs_2_, ...), custom_call_target="tpu_custom_call" | custom-call | flops 3221225472 | bytes 4718592 | tf_op jit(solution)/shard_map/attend_remote/pallas_call | solution.py:285
  124.2 6.5 %collective-permute-done.2.refs_0_.refs_1_ = bf16[256,1536]{1,0:T(8,128)(2,1)S(1)} collective-permute-done((bf16[256,1536]{1,0:T(8,128)(2,1)S(1)}, bf16[256,1536]{1,0:T(8,128)(2,1)S(1)}, u32[]{:S(2)}, u32[]{:S(2)}) %collective-permute-start.2) | collective-permute-done | bytes 786464 | tf_op jit(solution)/shard_map/ppermute | solution.py:1076
  134.6 10.2 %attend_remote.5 = (f32[48,512]{1,0:T(8,128)}, f32[768,512]{1,0:T(8,128)}) custom-call(s32[12]{0:T(128)} %concatenate.51.sc_ref, bf16[768,512]{1,0:T(8,128)(2,1)} %get-tuple-element.139.qt_ref, bf16[256,1536]{1,0:T(8,128)(2,1)} %copy-done.34, bf16[256,1536]{1,0:T(8,128)(2,1)} %collective-permute-done.3.refs_1_.refs_0_, ...), custom_call_target="tpu_custom_call" | custom-call | flops 3221225472 | bytes 4718592 | tf_op jit(solution)/shard_map/attend_remote/pallas_call | solution.py:285
  144.8 5.0 collective-permute-done.4.refs_0_.refs_1_
  157.5 10.2 %attend_remote.6 = (f32[48,512]{1,0:T(8,128)}, f32[768,512]{1,0:T(8,128)}) custom-call(s32[12]{0:T(128)} %concatenate.51.sc_ref, bf16[768,512]{1,0:T(8,128)(2,1)} %get-tuple-element.139.qt_ref, bf16[256,1536]{1,0:T(8,128)(2,1)} %copy-done.20, bf16[256,1536]{1,0:T(8,128)(2,1)} %copy-done.21, f32[48,512]{1,0:T(8,128)} %get-tuple-element.156.refs_2_, ...), custom_call_target="tpu_custom_call" | custom-call | flops 3221225472 | bytes 4718592 | tf_op jit(solution)/shard_map/attend_remote/pallas_call | solution.py:285
  167.7 7.5 %attend_remote.7 = (f32[48,512]{1,0:T(8,128)}, f32[768,512]{1,0:T(8,128)}, bf16[512,768]{1,0:T(8,128)(2,1)}) custom-call(s32[12]{0:T(128)} %concatenate.51.sc_ref, bf16[768,512]{1,0:T(8,128)(2,1)} %get-tuple-element.139.qt_ref, bf16[256,768]{1,0:T(8,128)(2,1)} %collective-permute-done.6.refs_0_, bf16[256,768]{1,0:T(8,128)(2,1)} %collective-permute-done.7.refs_1_, ...), custom_call_target="tpu_custom_call" | custom-call | flops 1610612736 | bytes 3932160 | tf_op jit(solution)/shard_map/attend_remote/pallas_call | solution.py:285
  175.2 9.4 %route_dispatch.1 = (f32[512,768]{1,0:T(8,128)}, bf16[512,768]{1,0:T(8,128)(2,1)}, f32[512,128]{1,0:T(8,128)}, bf16[1024,768]{1,0:T(8,128)(2,1)}) custom-call(bf16[512,768]{1,0:T(8,128)(2,1)} %bitcast.73, bf16[512,768]{1,0:T(8,128)(2,1)} %get-tuple-element.160.att_ref, ...), custom_call_target="tpu_custom_call" | custom-call | flops 1409286144 | bytes 3145728 | tf_op jit(solution)/shard_map/route_dispatch/pallas_call | solution.py:608
  184.6 6.4 %all-to-all-start = ((bf16[8,128,768]{2,1,0:T(8,128)(2,1)}), bf16[8,128,768]{2,1,0:T(8,128)(2,1)S(1)}, u32[]{:S(2)}, u32[]{:S(2)}) async-start(bf16[8,128,768]{2,1,0:T(8,128)(2,1)} %bitcast.95), calls=%async_computation | async-start | bytes 3145728 | tf_op jit(solution)/shard_map/all_to_all | solution.py:1200
  192.0 4.8 grad_rows.1
  196.8 28.5 %all-to-all-done = bf16[8,128,768]{2,1,0:T(8,128)(2,1)S(1)} async-done(((bf16[8,128,768]{2,1,0:T(8,128)(2,1)}), bf16[8,128,768]{2,1,0:T(8,128)(2,1)S(1)}, u32[]{:S(2)}, u32[]{:S(2)}) %all-to-all-start) | async-done | bytes 1572896 | tf_op jit(solution)/shard_map/all_to_all | solution.py:1200
  230.3 19.1 %expert_forward.1 = (f32[1024,2048]{1,0:T(8,128)}, f32[1024,2048]{1,0:T(8,128)}, bf16[128,768]{1,0:T(8,128)(2,1)}, bf16[128,768]{1,0:T(8,128)(2,1)}, bf16[128,76...) custom-call(s32[12]{0:T(128)} %concatenate.51.sc_ref, ...), custom_call_target="tpu_custom_call" | custom-call | flops 9663676416 | bytes 9437184 | tf_op jit(solution)/shard_map/expert_forward/pallas_call | solution.py:666
  263.3 26.1 %collective-permute-done.11.refs_4_ = bf16[128,768]{1,0:T(8,128)(2,1)S(1)} collective-permute-done((bf16[128,768]{1,0:T(8,128)(2,1)}, bf16[128,768]{1,0:T(8,128)(2,1)S(1)}, u32[]{:S(2)}, u32[]{:S(2)}) %collective-permute-start.11) | collective-permute-done | bytes 196640 | tf_op jit(solution)/shard_map/ppermute | solution.py:1106
  296.6 12.4 %mixture.1 = (bf16[512,768]{1,0:T(8,128)(2,1)}, f32[512,768]{1,0:T(8,128)}, f32[512,128]{1,0:T(8,128)}, f32[768,128]{1,0:T(8,128)}) custom-call(f32[512,768]{1,0:T(8,128)} %get-tuple-element.161.h_ref, bf16[512,768]{1,0:T(8,128)(2,1)} %bitcast.78, f32[512,128]{1,0:T(8,128)} %get-tuple-element.163.pr_ref, s32[512,2]{1,0:T(8,128)} %bitcast.82, ...), custom_call_target="tpu_custom_call" | custom-call | flops 1610612736 | bytes 4718592 | tf_op jit(solution)/shard_map/mixture/pallas_call | solution.py:833
  310.2 23.7 %expert_back_in.1 = (bf16[1024,768]{1,0:T(8,128)(2,1)}, bf16[1024,2048]{1,0:T(8,128)(2,1)}, bf16[1024,2048]{1,0:T(8,128)(2,1)}, bf16[1024,2048]{1,0:T(8,128)(2,1)}) custom-call(f32[1024,2048]{1,0:T(8,128)} %get-tuple-element.165.gate_ref, f32[1024,2048]{1,0:T(8,128)} %get-tuple-element.166.up_ref, bf16[1024,768]{1,0:T(8,128)(2,1)} %bitcast.91, ...), custom_call_target="tpu_custom_call" | custom-call | flops 9663676416 | bytes 18874368 | tf_op jit(solution)/shard_map/expert_back_in/pallas_call | solution.py:718
  333.9 17.3 %expert_weight_grads.1 = bf16[4,3,192,2048]{3,2,1,0:T(8,128)(2,1)} custom-call(bf16[1024,768]{1,0:T(8,128)(2,1)} %bitcast.90, bf16[1024,768]{1,0:T(8,128)(2,1)} %bitcast.92, bf16[1024,2048]{1,0:T(8,128)(2,1)} %get-tuple-element.240.act_ref, bf16[1024,2048]{1,0:T(8,128)(2,1)} %get-tuple-element.241.dg_ref, bf16[1024,2048]{1,0:T(8,128)(2,1)} %get-tuple-element.242.du_ref), custom_call_target="tpu_custom_call" | custom-call | flops 9663676416 | bytes 18874368 | tf_op jit(solution)/shard_map/expert_weight_grads/pallas_call | solution.py:748
  351.2 8.6 %all-to-all-start.2 = ((bf16[8,128,768]{2,1,0:T(8,128)(2,1)}), bf16[8,128,768]{2,1,0:T(8,128)(2,1)S(1)}, u32[]{:S(2)}, u32[]{:S(2)}) async-start(bf16[8,128,768]{2,1,0:T(8,128)(2,1)} %bitcast.27), calls=%async_computation.2 | async-start | bytes 3145728 | tf_op jit(solution)/shard_map/all_to_all | solution.py:1200
  359.9 37.0 %all-to-all-done.2 = bf16[8,128,768]{2,1,0:T(8,128)(2,1)S(1)} async-done(((bf16[8,128,768]{2,1,0:T(8,128)(2,1)}), bf16[8,128,768]{2,1,0:T(8,128)(2,1)S(1)}, u32[]{:S(2)}, u32[]{:S(2)}) %all-to-all-start.2) | async-done | bytes 1572896 | tf_op jit(solution)/shard_map/all_to_all | solution.py:1200
  398.1 9.1 %norm_two_back.1 = (f32[512,768]{1,0:T(8,128)}, bf16[512,768]{1,0:T(8,128)(2,1)}, bf16[768,512]{1,0:T(8,128)(2,1)}, f32[768,768]{1,0:T(8,128)}, f32[8,768]{1,0:T(8,128)}) custom-call(f32[512,768]{1,0:T(8,128)} %get-tuple-element.161.h_ref, bf16[512,768]{1,0:T(8,128)(2,1)} %bitcast.79, f32[512,768]{1,0:T(8,128)} %get-tuple-element.179.gn_ref, ...), custom_call_target="tpu_custom_call" | custom-call | flops 2013265920 | bytes 6291456 | tf_op jit(solution)/shard_map/norm_two_back/pallas_call | solution.py:887
  410.4 8.4 %attend_back_remote.4 = (f32[768,512]{1,0:T(8,128)}, bf16[256,768]{1,0:T(8,128)(2,1)}, bf16[256,768]{1,0:T(8,128)(2,1)}, f32[48,512]{1,0:T(8,128)}) custom-call(s32[12]{0:T(128)} %concatenate.51.sc_ref, bf16[768,512]{1,0:T(8,128)(2,1)} %get-tuple-element.139.qt_ref, bf16[512,768]{1,0:T(8,128)(2,1)} %get-tuple-element.140.q_ref, ...), custom_call_target="tpu_custom_call" | custom-call | flops 4026531840 | bytes 7864320 | tf_op jit(solution)/shard_map/attend_back_remote/pallas_call | solution.py:509
  420.9 10.9 %attend_back_remote.5 = (f32[768,512]{1,0:T(8,128)}, bf16[256,1536]{1,0:T(8,128)(2,1)}, bf16[256,1536]{1,0:T(8,128)(2,1)}) custom-call(s32[12]{0:T(128)} %concatenate.51.sc_ref, bf16[768,512]{1,0:T(8,128)(2,1)} %get-tuple-element.139.qt_ref, bf16[512,768]{1,0:T(8,128)(2,1)} %get-tuple-element.140.q_ref, bf16[768,512]{1,0:T(8,128)(2,1)} %get-tuple-element.182.dot_ref, ...), custom_call_target="tpu_custom_call" | custom-call | flops 8053063680 | bytes 9437184 | tf_op jit(solution)/shard_map/attend_back_remote/pallas_call | solution.py:509
  438.1 10.9 %attend_back_remote.6 = (f32[768,512]{1,0:T(8,128)}, bf16[256,1536]{1,0:T(8,128)(2,1)}, bf16[256,1536]{1,0:T(8,128)(2,1)}) custom-call(s32[12]{0:T(128)} %concatenate.51.sc_ref, bf16[768,512]{1,0:T(8,128)(2,1)} %get-tuple-element.139.qt_ref, bf16[512,768]{1,0:T(8,128)(2,1)} %get-tuple-element.140.q_ref, bf16[768,512]{1,0:T(8,128)(2,1)} %get-tuple-element.182.dot_ref, ...), custom_call_target="tpu_custom_call" | custom-call | flops 8053063680 | bytes 9437184 | tf_op jit(solution)/shard_map/attend_back_remote/pallas_call | solution.py:509
  449.0 5.2 collective-permute-done.18.gr_ref
  465.4 10.9 %attend_back_remote.7 = (f32[768,512]{1,0:T(8,128)}, bf16[256,1536]{1,0:T(8,128)(2,1)}, bf16[256,1536]{1,0:T(8,128)(2,1)}) custom-call(s32[12]{0:T(128)} %concatenate.51.sc_ref, bf16[768,512]{1,0:T(8,128)(2,1)} %get-tuple-element.139.qt_ref, bf16[512,768]{1,0:T(8,128)(2,1)} %get-tuple-element.140.q_ref, bf16[768,512]{1,0:T(8,128)(2,1)} %get-tuple-element.182.dot_ref, ...), custom_call_target="tpu_custom_call" | custom-call | flops 8053063680 | bytes 9437184 | tf_op jit(solution)/shard_map/attend_back_remote/pallas_call | solution.py:509
  484.5 11.0 %attend_back_local.1 = (f32[512,768]{1,0:T(8,128)}, f32[256,1536]{1,0:T(8,128)}, f32[256,1536]{1,0:T(8,128)}) custom-call(s32[12]{0:T(128)} %concatenate.51.sc_ref, bf16[768,512]{1,0:T(8,128)(2,1)} %get-tuple-element.139.qt_ref, bf16[512,768]{1,0:T(8,128)(2,1)} %get-tuple-element.140.q_ref, bf16[768,512]{1,0:T(8,128)(2,1)} %get-tuple-element.182.dot_ref, ...), custom_call_target="tpu_custom_call" | custom-call | flops 4026531840 | bytes 6291456 | tf_op jit(solution)/shard_map/attend_back_local/pallas_call | solution.py:480
  495.5 7.6 %q_back.1 = (f32[512,768]{1,0:T(8,128)}, bf16[2,192,768]{2,1,0:T(8,128)(2,1)}, f32[2,192,768]{2,1,0:T(8,128)}) custom-call(s32[12]{0:T(128)} %concatenate.51.sc_ref, bf16[768,512]{1,0:T(8,128)(2,1)} %turn.1.nt_ref, f32[512,768]{1,0:T(8,128)} %get-tuple-element.225.dq_ref, f32[512,128]{1,0:T(8,128)} %pad_maximum_fusion.1.c_ref, ...), custom_call_target="tpu_custom_call" | custom-call | flops 1207959552 | bytes 4718592 | tf_op jit(solution)/shard_map/q_back/pallas_call | solution.py:976
  508.5 14.7 %collective-permute-done.24.refs_0_ = bf16[256,1536]{1,0:T(8,128)(2,1)S(1)} collective-permute-done((bf16[256,1536]{1,0:T(8,128)(2,1)}, bf16[256,1536]{1,0:T(8,128)(2,1)S(1)}, u32[]{:S(2)}, u32[]{:S(2)}) %collective-permute-start.24) | collective-permute-done | bytes 786464 | tf_op jit(solution)/shard_map/ppermute | solution.py:1076
  525.3 13.5 %kv_back.1 = (f32[512,768]{1,0:T(8,128)}, bf16[2,192,1536]{2,1,0:T(8,128)(2,1)}, f32[2,192,1536]{2,1,0:T(8,128)}) custom-call(s32[12]{0:T(128)} %concatenate.51.sc_ref, bf16[512,768]{1,0:T(8,128)(2,1)} %bitcast.74, bf16[768,512]{1,0:T(8,128)(2,1)} %turn.1.nt_ref, f32[512,768]{1,0:T(8,128)} %get-tuple-element.226.gnq_ref, ...), custom_call_target="tpu_custom_call" | custom-call | flops 2415919104 | bytes 9437184 | tf_op jit(solution)/shard_map/kv_back/pallas_call | solution.py:1027
  561.9 8.4 %all-to-all-done.3 = bf16[8,24,1664]{2,1,0:T(8,128)(2,1)S(1)} async-done(((bf16[8,24,1664]{2,1,0:T(8,128)(2,1)}), bf16[8,24,1664]{2,1,0:T(8,128)(2,1)S(1)}, u32[]{:S(2)}, u32[]{:S(2)}) %all-to-all-start.3) | async-done | bytes 639008 | tf_op jit(solution)/shard_map/all_to_all | solution.py:1098
  (230 shorter events, 159.2 us)
Async XLA Ops:
  7.2 72.7 %all-gather.4.cloned.1.call-start = ((), (), s32[]{:S(2)}) async-start(), calls=%async_computation.5 | async-start | bytes 5068800 | tf_op jit(solution)/shard_map/all_gather | solution.py:1166
  12.7 217.6 %all-gather.6.cloned.1.call-start = ((), (), s32[]{:S(2)}) async-start(), calls=%async_computation.7 | async-start | bytes 11796480 | tf_op jit(solution)/shard_map/all_gather | solution.py:1230
  91.0 20.0 %collective-permute-start = (bf16[256,1536]{1,0:T(8,128)(2,1)}, bf16[256,1536]{1,0:T(8,128)(2,1)S(1)}, u32[]{:S(2)}, u32[]{:S(2)}) collective-permute-start(bf16[256,1536]{1,0:T(8,128)(2,1)} %get-tuple-element.141.kv_ref), channel_id=1, source_target_pairs={{0,2},{2,4},{4,6},{6,7},{7,5},{5,3},{3,1},{1,0},{8,10},{10,12},{12... | collective-permute-start | bytes 2359304 | tf_op jit(solution)/shard_map/ppermute | solution.py:1076
  92.3 19.7 %collective-permute-start.1 = (bf16[256,1536]{1,0:T(8,128)(2,1)}, bf16[256,1536]{1,0:T(8,128)(2,1)S(1)}, u32[]{:S(2)}, u32[]{:S(2)}) collective-permute-start(bf16[256,1536]{1,0:T(8,128)(2,1)} %get-tuple-element.141.kv_ref), channel_id=1, source_target_pairs={{0,1},{2,0},{4,2},{6,4},{7,6},{5,7},{3,5},{1,3},{8,9},{10,8},{12,1... | collective-permute-start | bytes 2359304 | tf_op jit(solution)/shard_map/ppermute | solution.py:1076
  112.0 18.7 %collective-permute-start.2 = (bf16[256,1536]{1,0:T(8,128)(2,1)S(1)}, bf16[256,1536]{1,0:T(8,128)(2,1)S(1)}, u32[]{:S(2)}, u32[]{:S(2)}) collective-permute-start(bf16[256,1536]{1,0:T(8,128)(2,1)S(1)} %collective-permute-done.refs_0_.refs_1_), channel_id=1, source_target_pairs={{0,2},{2,4},{4,6},{6,7},{7,5},{5,3},{3,1},{1,0},{8,10},{10,12},{12... | collective-permute-start | bytes 2359304 | tf_op jit(solution)/shard_map/ppermute | solution.py:1076
  112.7 18.5 %collective-permute-start.3 = (bf16[256,1536]{1,0:T(8,128)(2,1)S(1)}, bf16[256,1536]{1,0:T(8,128)(2,1)}, u32[]{:S(2)}, u32[]{:S(2)}) collective-permute-start(bf16[256,1536]{1,0:T(8,128)(2,1)S(1)} %collective-permute-done.1.refs_1_.refs_0_), channel_id=1, source_target_pairs={{0,1},{2,0},{4,2},{6,4},{7,6},{5,7},{3,5},{1,3},{8,9},{10,8},{12,1... | collective-permute-start | bytes 2359304 | tf_op jit(solution)/shard_map/ppermute | solution.py:1076
  131.6 18.2 %collective-permute-start.4 = (bf16[256,1536]{1,0:T(8,128)(2,1)}, bf16[256,1536]{1,0:T(8,128)(2,1)S(1)}, u32[]{:S(2)}, u32[]{:S(2)}) collective-permute-start(bf16[256,1536]{1,0:T(8,128)(2,1)} %copy-done.34), channel_id=1, source_target_pairs={{0,2},{2,4},{4,6},{6,7},{7,5},{5,3},{3,1},{1,0},{8,10},{10,12},{12... | collective-permute-start | bytes 2359304 | tf_op jit(solution)/shard_map/ppermute | solution.py:1076
  132.3 17.9 %collective-permute-start.5 = (bf16[256,1536]{1,0:T(8,128)(2,1)}, bf16[256,1536]{1,0:T(8,128)(2,1)S(1)}, u32[]{:S(2)}, u32[]{:S(2)}) collective-permute-start(bf16[256,1536]{1,0:T(8,128)(2,1)} %collective-permute-done.3.refs_1_.refs_0_), channel_id=1, source_target_pairs={{0,1},{2,0},{4,2},{6,4},{7,6},{5,7},{3,5},{1,3},{8,9},{10,8},{12,1... | collective-permute-start | bytes 2359304 | tf_op jit(solution)/shard_map/ppermute | solution.py:1076
  151.1 16.6 %collective-permute-start.6 = (bf16[256,768]{1,0:T(8,128)(2,1)S(1)}, bf16[256,768]{1,0:T(8,128)(2,1)}, u32[]{:S(2)}, u32[]{:S(2)}) collective-permute-start(bf16[256,768]{1,0:T(8,128)(2,1)S(1)} %slice.70), channel_id=1, source_target_pairs={{0,2},{2,4},{4,6},{6,7},{7,5},{5,3},{3,1},{1,0},{8,10},{10,12},{12... | collective-permute-start | bytes 1179656 | tf_op jit(solution)/shard_map/ppermute | solution.py:1076
  152.9 14.8 %collective-permute-start.7 = (bf16[256,768]{1,0:T(8,128)(2,1)S(1)}, bf16[256,768]{1,0:T(8,128)(2,1)}, u32[]{:S(2)}, u32[]{:S(2)}) collective-permute-start(bf16[256,768]{1,0:T(8,128)(2,1)S(1)} %slice.71), channel_id=1, source_target_pairs={{0,1},{2,0},{4,2},{6,4},{7,6},{5,7},{3,5},{1,3},{8,9},{10,8},{12,1... | collective-permute-start | bytes 1179656 | tf_op jit(solution)/shard_map/ppermute | solution.py:1076
  184.6 40.7 %all-to-all-start = ((bf16[8,128,768]{2,1,0:T(8,128)(2,1)}), bf16[8,128,768]{2,1,0:T(8,128)(2,1)S(1)}, u32[]{:S(2)}, u32[]{:S(2)}) async-start(bf16[8,128,768]{2,1,0:T(8,128)(2,1)} %bitcast.95), calls=%async_computation | async-start | bytes 3145728 | tf_op jit(solution)/shard_map/all_to_all | solution.py:1200
  226.4 82.6 %all-to-all-start.1 = ((bf16[8,128,768]{2,1,0:T(8,128)(2,1)}), bf16[8,128,768]{2,1,0:T(8,128)(2,1)S(1)}, u32[]{:S(2)}, u32[]{:S(2)}) async-start(bf16[8,128,768]{2,1,0:T(8,128)(2,1)} %bitcast.93), calls=%async_computation.1 | async-start | bytes 3145728 | tf_op jit(solution)/shard_map/all_to_all | solution.py:1200
  230.0 340.4 %reduce-scatter.2.cloned.1.call-start = ((), (), s32[]{:S(2)}) async-start(), calls=%async_computation.6 | async-start | bytes 11796480 | tf_op jit(solution)/shard_map/reduce_scatter | solution.py:1274
  249.4 12.3 %collective-permute-start.10 = (bf16[128,768]{1,0:T(8,128)(2,1)}, bf16[128,768]{1,0:T(8,128)(2,1)S(1)}, u32[]{:S(2)}, u32[]{:S(2)}) collective-permute-start(bf16[128,768]{1,0:T(8,128)(2,1)} %get-tuple-element.173), channel_id=1, source_target_pairs={{0,3},{1,2},{2,1},{3,0},{4,7},{5,6},{6,5},{7,4},{8,11},{9,10},{10,... | collective-permute-start | bytes 589832 | tf_op jit(solution)/shard_map/ppermute | solution.py:1106
  252.3 37.1 %collective-permute-start.11 = (bf16[128,768]{1,0:T(8,128)(2,1)}, bf16[128,768]{1,0:T(8,128)(2,1)S(1)}, u32[]{:S(2)}, u32[]{:S(2)}) collective-permute-start(bf16[128,768]{1,0:T(8,128)(2,1)} %get-tuple-element.174), channel_id=1, source_target_pairs={{0,4},{1,5},{2,6},{3,7},{4,0},{5,1},{6,2},{7,3},{8,12},{9,13},{10,... | collective-permute-start | bytes 589832 | tf_op jit(solution)/shard_map/ppermute | solution.py:1106
  254.6 39.9 %collective-permute-start.12 = (bf16[128,768]{1,0:T(8,128)(2,1)}, bf16[128,768]{1,0:T(8,128)(2,1)S(1)}, u32[]{:S(2)}, u32[]{:S(2)}) collective-permute-start(bf16[128,768]{1,0:T(8,128)(2,1)} %get-tuple-element.175), channel_id=1, source_target_pairs={{0,5},{1,4},{2,7},{3,6},{4,1},{5,0},{6,3},{7,2},{8,13},{9,12},{10,... | collective-permute-start | bytes 589832 | tf_op jit(solution)/shard_map/ppermute | solution.py:1106
  255.2 39.4 %collective-permute-start.13 = (bf16[128,768]{1,0:T(8,128)(2,1)}, bf16[128,768]{1,0:T(8,128)(2,1)S(1)}, u32[]{:S(2)}, u32[]{:S(2)}) collective-permute-start(bf16[128,768]{1,0:T(8,128)(2,1)} %get-tuple-element.176), channel_id=1, source_target_pairs={{0,6},{1,7},{2,4},{3,5},{4,2},{5,3},{6,0},{7,1},{8,14},{9,15},{10,... | collective-permute-start | bytes 589832 | tf_op jit(solution)/shard_map/ppermute | solution.py:1106
  257.5 37.0 %collective-permute-start.14 = (bf16[128,768]{1,0:T(8,128)(2,1)}, bf16[128,768]{1,0:T(8,128)(2,1)S(1)}, u32[]{:S(2)}, u32[]{:S(2)}) collective-permute-start(bf16[128,768]{1,0:T(8,128)(2,1)} %get-tuple-element.177), channel_id=1, source_target_pairs={{0,7},{1,6},{2,5},{3,4},{4,3},{5,2},{6,1},{7,0},{8,15},{9,14},{10,... | collective-permute-start | bytes 589832 | tf_op jit(solution)/shard_map/ppermute | solution.py:1106
  261.7 32.9 %collective-permute-start.8 = (bf16[128,768]{1,0:T(8,128)(2,1)}, bf16[128,768]{1,0:T(8,128)(2,1)S(1)}, u32[]{:S(2)}, u32[]{:S(2)}) collective-permute-start(bf16[128,768]{1,0:T(8,128)(2,1)} %get-tuple-element.171), channel_id=1, source_target_pairs={{0,1},{1,0},{2,3},{3,2},{4,5},{5,4},{6,7},{7,6},{8,9},{9,8},{10,11... | collective-permute-start | bytes 589832 | tf_op jit(solution)/shard_map/ppermute | solution.py:1106
  351.2 45.8 %all-to-all-start.2 = ((bf16[8,128,768]{2,1,0:T(8,128)(2,1)}), bf16[8,128,768]{2,1,0:T(8,128)(2,1)S(1)}, u32[]{:S(2)}, u32[]{:S(2)}) async-start(bf16[8,128,768]{2,1,0:T(8,128)(2,1)} %bitcast.27), calls=%async_computation.2 | async-start | bytes 3145728 | tf_op jit(solution)/shard_map/all_to_all | solution.py:1200
  410.3 21.4 %collective-permute-start.17 = (bf16[2,192,896]{2,1,0:T(8,128)(2,1)S(1)}, bf16[2,192,896]{2,1,0:T(8,128)(2,1)S(1)}, u32[]{:S(2)}, u32[]{:S(2)}) collective-permute-start(bf16[2,192,896]{2,1,0:T(8,128)(2,1)S(1)} %fusion.4), channel_id=1, source_target_pairs={{0,8},{8,0},{16,24},{24,16},{1,9},{9,1},{17,25},{25,17},{2,10},{10... | collective-permute-start | bytes 2064392 | tf_op jit(solution)/shard_map/ppermute | solution.py:1084
  418.8 12.9 %collective-permute-start.15 = (bf16[256,768]{1,0:T(8,128)(2,1)}, bf16[256,768]{1,0:T(8,128)(2,1)}, u32[]{:S(2)}, u32[]{:S(2)}) collective-permute-start(bf16[256,768]{1,0:T(8,128)(2,1)} %get-tuple-element.186), channel_id=1, source_target_pairs={{0,2},{2,4},{4,6},{6,7},{7,5},{5,3},{3,1},{1,0},{8,10},{10,12},{12... | collective-permute-start | bytes 1179656 | tf_op jit(solution)/shard_map/ppermute | solution.py:1076
  418.9 12.9 %collective-permute-start.16 = (bf16[256,768]{1,0:T(8,128)(2,1)}, bf16[256,768]{1,0:T(8,128)(2,1)}, u32[]{:S(2)}, u32[]{:S(2)}) collective-permute-start(bf16[256,768]{1,0:T(8,128)(2,1)} %get-tuple-element.187), channel_id=1, source_target_pairs={{0,1},{2,0},{4,2},{6,4},{7,6},{5,7},{3,5},{1,3},{8,9},{10,8},{12,1... | collective-permute-start | bytes 1179656 | tf_op jit(solution)/shard_map/ppermute | solution.py:1076
  434.6 19.6 %collective-permute-start.18 = (bf16[256,1536]{1,0:T(8,128)(2,1)}, bf16[256,1536]{1,0:T(8,128)(2,1)}, u32[]{:S(2)}, u32[]{:S(2)}) collective-permute-start(bf16[256,1536]{1,0:T(8,128)(2,1)} %get-tuple-element.199), channel_id=1, source_target_pairs={{0,2},{2,4},{4,6},{6,7},{7,5},{5,3},{3,1},{1,0},{8,10},{10,12},{12... | collective-permute-start | bytes 2359304 | tf_op jit(solution)/shard_map/ppermute | solution.py:1076
  435.7 20.5 %collective-permute-start.19 = (bf16[256,1536]{1,0:T(8,128)(2,1)}, bf16[256,1536]{1,0:T(8,128)(2,1)}, u32[]{:S(2)}, u32[]{:S(2)}) collective-permute-start(bf16[256,1536]{1,0:T(8,128)(2,1)} %get-tuple-element.200), channel_id=1, source_target_pairs={{0,1},{2,0},{4,2},{6,4},{7,6},{5,7},{3,5},{1,3},{8,9},{10,8},{12,1... | collective-permute-start | bytes 2359304 | tf_op jit(solution)/shard_map/ppermute | solution.py:1076
  459.0 19.6 %collective-permute-start.21 = (bf16[256,1536]{1,0:T(8,128)(2,1)}, bf16[256,1536]{1,0:T(8,128)(2,1)S(1)}, u32[]{:S(2)}, u32[]{:S(2)}) collective-permute-start(bf16[256,1536]{1,0:T(8,128)(2,1)} %get-tuple-element.210), channel_id=1, source_target_pairs={{0,2},{2,4},{4,6},{6,7},{7,5},{5,3},{3,1},{1,0},{8,10},{10,12},{12... | collective-permute-start | bytes 2359304 | tf_op jit(solution)/shard_map/ppermute | solution.py:1076
  462.2 18.6 %collective-permute-start.22 = (bf16[256,1536]{1,0:T(8,128)(2,1)}, bf16[256,1536]{1,0:T(8,128)(2,1)S(1)}, u32[]{:S(2)}, u32[]{:S(2)}) collective-permute-start(bf16[256,1536]{1,0:T(8,128)(2,1)} %get-tuple-element.211), channel_id=1, source_target_pairs={{0,1},{2,0},{4,2},{6,4},{7,6},{5,7},{3,5},{1,3},{8,9},{10,8},{12,1... | collective-permute-start | bytes 2359304 | tf_op jit(solution)/shard_map/ppermute | solution.py:1076
  503.0 20.2 %collective-permute-start.24 = (bf16[256,1536]{1,0:T(8,128)(2,1)}, bf16[256,1536]{1,0:T(8,128)(2,1)S(1)}, u32[]{:S(2)}, u32[]{:S(2)}) collective-permute-start(bf16[256,1536]{1,0:T(8,128)(2,1)} %get-tuple-element.232), channel_id=1, source_target_pairs={{0,2},{2,4},{4,6},{6,7},{7,5},{5,3},{3,1},{1,0},{8,10},{10,12},{12... | collective-permute-start | bytes 2359304 | tf_op jit(solution)/shard_map/ppermute | solution.py:1076
  504.6 19.8 %collective-permute-start.25 = (bf16[256,1536]{1,0:T(8,128)(2,1)}, bf16[256,1536]{1,0:T(8,128)(2,1)S(1)}, u32[]{:S(2)}, u32[]{:S(2)}) collective-permute-start(bf16[256,1536]{1,0:T(8,128)(2,1)} %get-tuple-element.233), channel_id=1, source_target_pairs={{0,1},{2,0},{4,2},{6,4},{7,6},{5,7},{3,5},{1,3},{8,9},{10,8},{12,1... | collective-permute-start | bytes 2359304 | tf_op jit(solution)/shard_map/ppermute | solution.py:1076
  549.4 20.8 %all-to-all-start.3 = ((bf16[8,24,1664]{2,1,0:T(8,128)(2,1)}), bf16[8,24,1664]{2,1,0:T(8,128)(2,1)S(1)}, u32[]{:S(2)}, u32[]{:S(2)}) async-start(bf16[8,24,1664]{2,1,0:T(8,128)(2,1)} %fusion.1), calls=%async_computation.4 | async-start | bytes 1277952 | tf_op jit(solution)/shard_map/all_to_all | solution.py:1098
  561.6 15.1 %collective-permute-start.27 = (bf16[192,1536]{1,0:T(8,128)(2,1)}, bf16[192,1536]{1,0:T(8,128)(2,1)S(1)}, u32[]{:S(2)}, u32[]{:S(2)}) collective-permute-start(bf16[192,1536]{1,0:T(8,128)(2,1)} %fusion.5), channel_id=1, source_target_pairs={{0,16},{16,0},{8,24},{24,8},{1,17},{17,1},{9,25},{25,9},{2,18},{18... | collective-permute-start | bytes 1769480 | tf_op jit(solution)/shard_map/ppermute | solution.py:1092
  581.5 11.9 %collective-permute-start.30 = (bf16[24,1536]{1,0:T(8,128)(2,1)}, bf16[24,1536]{1,0:T(8,128)(2,1)S(1)}, u32[]{:S(2)}, u32[]{:S(2)}) collective-permute-start(bf16[24,1536]{1,0:T(8,128)(2,1)} %get-tuple-element.254), channel_id=1, source_target_pairs={{0,2},{1,3},{2,0},{3,1},{4,6},{5,7},{6,4},{7,5},{8,10},{9,11},{10,... | collective-permute-start | bytes 221192 | tf_op jit(solution)/shard_map/ppermute | solution.py:1106
  (47 other events, 372.8 us)
Sparse Core Ops, SparseCore 0:
  12.8 67.0 all-gather.3
  81.5 62.6 all-gather.5
  351.3 80.5 reduce-scatter.1

commit v4 on v2

--- a/solution.py
+++ b/solution.py
@@ -23,7 +23,8 @@
 F32 = jnp.float32
 BF16 = jnp.bfloat16
 ALL_AXES = ("dp", "expert")
-VMEM_LIMIT = 60 * 1024 * 1024
+VMEM_SMALL = 24 * 1024 * 1024
+VMEM_LARGE = 44 * 1024 * 1024
 
 
 def dot(a, b):
@@ -39,9 +40,9 @@
     return hi, (v - hi.astype(F32)).astype(BF16)
 
 
-def params(cost=None):
+def params(cost=None, limit=VMEM_SMALL):
     return dict(
-        compiler_params=pltpu.CompilerParams(vmem_limit_bytes=VMEM_LIMIT),
+        compiler_params=pltpu.CompilerParams(vmem_limit_bytes=limit),
         cost_estimate=None if cost is None else pl.CostEstimate(
             flops=int(cost[0]), bytes_accessed=int(cost[1]), transcendentals=0
         ),
@@ -664,7 +665,7 @@
         out_shape=[shape((rows, D), BF16)] + [shape((rows, wide), F32)] * 2,
         scratch_shapes=[pltpu.VMEM((rows, D), F32)],
         name="expert_forward",
-        **params((6 * rows * D * wide, 6 * D * wide)),
+        **params((6 * rows * D * wide, 6 * D * wide), VMEM_LARGE),
     )(xr, w)
 
 
@@ -714,7 +715,7 @@
         out_shape=[shape((rows, D), BF16)] + [shape((rows, wide), BF16)] * 3,
         scratch_shapes=[pltpu.VMEM((rows, D), F32)],
         name="expert_back_in",
-        **params((6 * rows * D * wide, 12 * D * wide)),
+        **params((6 * rows * D * wide, 12 * D * wide), VMEM_LARGE),
     )(gate, up, gr, w)
 
 
@@ -744,7 +745,7 @@
         out_shape=shape(dims, BF16),
         scratch_shapes=[pltpu.VMEM((D, rows), BF16), pltpu.VMEM((D, rows), BF16)],
         name="expert_weight_grads",
-        **params((6 * rows * D * wide, 12 * D * wide)),
+        **params((6 * rows * D * wide, 12 * D * wide), VMEM_LARGE),
     )(xr, low, act, d_gate, d_up)
 
 
@@ -894,6 +895,24 @@
     )(hidden, g, gn, tc, ret, rows, pack, att)
 
 
+def turn_body(x_ref, o_ref):
+    o_ref[...] = x_ref[...].T
+
+
+def turn(x):
+    rows, wide = x.shape
+    part = 256
+    return pl.pallas_call(
+        turn_body,
+        grid=(wide // part,),
+        in_specs=[spec((rows, part), lambda i: (0, i))],
+        out_specs=spec((part, rows), lambda i: (i, 0)),
+        out_shape=shape((wide, rows), x.dtype),
+        name="turn",
+        **params((rows * wide, 4 * rows * wide)),
+    )(x)
+
+
 def store_grad(sc_ref, split, value, refs):
     if not split:
         refs[0][...] = value
@@ -920,13 +939,8 @@
     return [tile, tile], [shape(dims, BF16), shape(dims, F32)]
 
 
-def q_back_body(split, sc_ref, n_ref, dq_ref, c_ref, s_ref, w_ref, gn_ref, nt_ref, *refs):
+def q_back_body(split, sc_ref, nt_ref, dq_ref, c_ref, s_ref, w_ref, gn_ref, *refs):
     step = pl.program_id(0)
-
-    @pl.when(step == 0)
-    def _():
-        nt_ref[...] = n_ref[...].T
-
     cosine = c_ref[...]
     sine = s_ref[...]
     v0 = dq_ref[:, :LANES]
@@ -950,21 +964,21 @@
         gn_ref[...] += gn
 
 
-def q_back_call(sc, low, dq, cosine, sine, pack, split):
-    t = low.shape[0]
+def q_back_call(sc, low_t, dq, cosine, sine, pack, split):
+    t = low_t.shape[1]
     specs, shapes = grad_outs(split, D)
     return pl.pallas_call(
         functools.partial(q_back_body, split),
         grid=(PAIRS // 2,),
         in_specs=[
-            SMEM_SPEC, whole((t, D)), spec((t, 2 * LANES), lambda i: (0, i)), whole((t, LANES)),
+            SMEM_SPEC, whole((D, t)), spec((t, 2 * LANES), lambda i: (0, i)), whole((t, LANES)),
             whole((t, LANES)), spec((D, 2 * LANES), lambda i: (0, i)),
         ],
-        out_specs=[whole((t, D)), whole((D, t))] + specs,
-        out_shape=[shape((t, D), F32), shape((D, t), BF16)] + shapes,
+        out_specs=[whole((t, D))] + specs,
+        out_shape=[shape((t, D), F32)] + shapes,
         name="q_back",
         **params((4 * t * D * D, 12 * t * D)),
-    )(sc, low, dq, cosine, sine, pack)
+    )(sc, low_t, dq, cosine, sine, pack)
 
 
 def kv_back_body(
@@ -1201,6 +1215,7 @@
     )
     x_got = exchange(to_owners(x_send))
     g_send = grad_rows_call(g, pr, target_rows, slots)
+    low_one_t = turn(low_one)
     x_got, g_send = tie(x_got, g_send)
     g_got = exchange(to_owners(g_send))
     expert_rows, gate_pre, up_pre = expert_fwd(x_got, weights)
@@ -1263,7 +1278,7 @@
         dkv_cont = lax.psum_scatter(
             dkv_cont, "expert", scatter_dimension=0, tiled=True, axis_index_groups=cont_groups
         )
-    gn_q, low_one_t, *grad_q = q_back_call(sc, low_one, dq, cosine, sine, pack, ring)
+    gn_q, *grad_q = q_back_call(sc, low_one_t, dq, cosine, sine, pack, ring)
     if ring:
         got_q = swap_core(grad_q[0])
         keep_q, got_q = add_and_cross(grad_q[1], got_q)

time: 592 us -> 603 us (1.019)
  local copies, waits for them, and re-layouts: 37.7 us -> 91.5 us
  Pallas kernels: 235 us -> 198 us
  other arithmetic: 23.3 us -> 17.1 us
    unnamed x69 -> x179, local copies, waits for them, and re-layouts: 14.2 us -> 65.8 us
    pallas_call x3, Pallas kernels: 8.48 us -> 2.02 us  [ring_add(): pl.pallas_call(functools.partial(ring_add_body, half), grid=(2,), in_spec...]
  transfers between devices with their start and end apart: 31 -> 31, of which waited for: 23 -> 23; matrix products, arithmetic and copies ran while one was open for 8% -> 7% of each run, Pallas kernels for 35% -> 29%
where the time goes in v4:
time: 603 us; the launch traced here: 593 us
  waiting for transfers between devices  222 us (37%)
  Pallas kernels  198 us (33%)
  local copies, waits for them, and re-layouts  91.5 us (15%)
  starting transfers between devices  49.6 us (8%)
  other arithmetic  17.1 us (3%)
  between operations  14.9 us (2%)
    all_to_all x4, waiting for transfers between devices, exchange(): lax.all_to_all(rows, 'expert', split_axis=0, concat_axis=0, tiled=True)  89.5 us
    unnamed x179, local copies, waits for them, and re-layouts  65.8 us
    all_gather x1, waiting for transfers between devices, per_device(): lax.all_gather(jnp.concatenate([qkv_weight, out_weight, small], axis=1),...  61 us
    ppermute x16, waiting for transfers between devices, along_ring(): return lax.ppermute(array, 'expert', pairs)  47.9 us
    pallas_call x4, Pallas kernels, bwd_remote(): pl.pallas_call(functools.partial(bwd_remote_body, tuple(offsets), len(kvs...  36.8 us
    pallas_call x4, Pallas kernels, fwd_remote(): pl.pallas_call(functools.partial(fwd_remote_body, tuple(offsets), len(kvs...  33.8 us
    pallas_call x1, Pallas kernels, expert_in(): pl.pallas_call(expert_in_body, grid=(wide // part,), in_specs=[tile, tile...  22.6 us
    all_to_all x4, starting transfers between devices, exchange(): lax.all_to_all(rows, 'expert', split_axis=0, concat_axis=0, tiled=True)  19 us
  transfers between devices with their start and end apart: 31, of which 23 were waited for; matrix products, arithmetic and copies ran while one was open for 7% of the time, Pallas kernels for 29%

profile of v4, /device:TPU:0, one launch (start us, length us, event | category | flops | bytes accessed | tf_op | source)
XLA Modules:
  0.0 593.3 jit_solution(4891066825591549609)
XLA Ops:
  18.9 61.0 %all-gather.4.cloned.1.call-done.wq_ref.wk_ref.wv_ref.ow_ref.sw_ref.w_ref = bf16[768,3200]{1,0:T(8,128)(2,1)} async-done(((bf16[24,3200]{1,0:T(8,128)(2,1)}), bf16[768,3200]{1,0:T(8,128)(2,1)}) %all-gather.4.cloned.1.call-update) | async-done | bytes 4915216 | tf_op jit(solution)/shard_map/all_gather | solution.py:1128
  84.5 7.0 %qkv_rope.1 = (bf16[512,768]{1,0:T(8,128)(2,1)S(1)}, bf16[512,768]{1,0:T(8,128)(2,1)S(1)}, bf16[768,512]{1,0:T(8,128)(2,1)S(1)}, bf16[256,1536]{1,0:T(8,128)(2,1)}, bf16[256,1536]{1,0:T(8,128)(2,1)S(1)}) custom-call(bf16[512,768]{1,0:T(8,128)(2,1)S(1)} %bitcast.74, f32[1,768]{1,0:T(1,128)S(1)} %copy.137.gain_ref, bf16[768,3200]{1,0:T(8,128)(2,1)S(1)} %copy-done, ...), custom_call_target="tpu_custom_call" | custom-call | flops 1811939328 | bytes 3538944 | tf_op jit(solution)/shard_map/qkv_rope/pallas_call | solution.py:100
  100.5 9.1 %attend_local.1 = (f32[48,512]{1,0:T(8,128)S(1)}, f32[768,512]{1,0:T(8,128)S(1)}) custom-call(s32[12]{0:T(128)S(1)} %concatenate.51.sc_ref, bf16[768,512]{1,0:T(8,128)(2,1)S(1)} %copy-done.45, bf16[256,1536]{1,0:T(8,128)(2,1)} %get-tuple-element.126.kv_ref, bf16[256,1536]{1,0:T(8,128)(2,1)S(1)} %copy-done.52), custom_call_target="tpu_custom_call" | custom-call | flops 1610612736 | bytes 1572864 | tf_op jit(solution)/shard_map/attend_local/pallas_call | solution.py:262
  117.5 9.2 %attend_remote.4 = (f32[48,512]{1,0:T(8,128)S(1)}, f32[768,512]{1,0:T(8,128)S(1)}) custom-call(s32[12]{0:T(128)S(1)} %concatenate.51.sc_ref, bf16[768,512]{1,0:T(8,128)(2,1)S(1)} %copy-done.46, bf16[256,1536]{1,0:T(8,128)(2,1)} %collective-permute-done.refs_0_.refs_1_, bf16[256,1536]{1,0:T(8,128)(2,1)} %collective-permute-done.1.refs_1_.refs_0_, ...), custom_call_target="tpu_custom_call" | custom-call | flops 3221225472 | bytes 4718592 | tf_op jit(solution)/shard_map/attend_remote/pallas_call | solution.py:286
  127.8 6.5 %collective-permute-done.2.refs_0_.refs_1_ = bf16[256,1536]{1,0:T(8,128)(2,1)} collective-permute-done((bf16[256,1536]{1,0:T(8,128)(2,1)}, bf16[256,1536]{1,0:T(8,128)(2,1)}, u32[]{:S(2)}, u32[]{:S(2)}) %collective-permute-start.2) | collective-permute-done | bytes 786464 | tf_op jit(solution)/shard_map/ppermute | solution.py:1070
  140.1 9.2 %attend_remote.5 = (f32[48,512]{1,0:T(8,128)S(1)}, f32[768,512]{1,0:T(8,128)S(1)}) custom-call(s32[12]{0:T(128)S(1)} %concatenate.51.sc_ref, bf16[768,512]{1,0:T(8,128)(2,1)S(1)} %copy-done.47, bf16[256,1536]{1,0:T(8,128)(2,1)} %collective-permute-done.2.refs_0_.refs_1_, bf16[256,1536]{1,0:T(8,128)(2,1)} %collective-permute-done.3.refs_1_.refs_0_, ...), custom_call_target="tpu_custom_call" | custom-call | flops 3221225472 | bytes 4718592 | tf_op jit(solution)/shard_map/attend_remote/pallas_call | solution.py:286
  165.0 9.3 %attend_remote.6 = (f32[48,512]{1,0:T(8,128)S(1)}, f32[768,512]{1,0:T(8,128)S(1)}) custom-call(s32[12]{0:T(128)S(1)} %concatenate.51.sc_ref, bf16[768,512]{1,0:T(8,128)(2,1)S(1)} %copy-done.48, bf16[256,1536]{1,0:T(8,128)(2,1)S(1)} %copy-done.39, bf16[256,1536]{1,0:T(8,128)(2,1)} %collective-permute-done.5.refs_1_.refs_0_, ...), custom_call_target="tpu_custom_call" | custom-call | flops 3221225472 | bytes 4718592 | tf_op jit(solution)/shard_map/attend_remote/pallas_call | solution.py:286
  174.4 6.2 %attend_remote.7 = (f32[48,512]{1,0:T(8,128)S(1)}, f32[768,512]{1,0:T(8,128)S(1)}, bf16[512,768]{1,0:T(8,128)(2,1)S(1)}) custom-call(s32[12]{0:T(128)S(1)} %concatenate.51.sc_ref, bf16[768,512]{1,0:T(8,128)(2,1)S(1)} %copy-done.48, bf16[256,768]{1,0:T(8,128)(2,1)} %collective-permute-done.6.refs_0_, bf16[256,768]{1,0:T(8,128)(2,1)} %collective-permute-done.7.refs_1_, ...), custom_call_target="tpu_custom_call" | custom-call | flops 1610612736 | bytes 3932160 | tf_op jit(solution)/shard_map/attend_remote/pallas_call | solution.py:286
  181.7 5.9 route_dispatch.1
  191.5 5.9 all-to-all-start
  202.5 28.7 %all-to-all-done = bf16[8,128,768]{2,1,0:T(8,128)(2,1)} async-done(((bf16[8,128,768]{2,1,0:T(8,128)(2,1)}), bf16[8,128,768]{2,1,0:T(8,128)(2,1)}, u32[]{:S(2)}, u32[]{:S(2)}) %all-to-all-start) | async-done | bytes 1572896 | tf_op jit(solution)/shard_map/all_to_all | solution.py:1162
  235.5 18.6 %expert_forward.1 = (bf16[1024,768]{1,0:T(8,128)(2,1)S(1)}, f32[1024,2048]{1,0:T(8,128)}, f32[1024,2048]{1,0:T(8,128)}) custom-call(bf16[1024,768]{1,0:T(8,128)(2,1)} %bitcast.18.x_ref, bf16[4,3,192,2048]{3,2,1,0:T(8,128)(2,1)} %bitcast.116), custom_call_target="tpu_custom_call" | custom-call | flops 9663676416 | bytes 9437184 | tf_op jit(solution)/shard_map/expert_forward/pallas_call | solution.py:660
  255.3 16.2 %all-to-all-done.1 = bf16[8,128,768]{2,1,0:T(8,128)(2,1)} async-done(((bf16[8,128,768]{2,1,0:T(8,128)(2,1)}), bf16[8,128,768]{2,1,0:T(8,128)(2,1)}, u32[]{:S(2)}, u32[]{:S(2)}) %all-to-all-start.1) | async-done | bytes 1572896 | tf_op jit(solution)/shard_map/all_to_all | solution.py:1162
  278.5 22.6 %expert_back_in.1 = (bf16[1024,768]{1,0:T(8,128)(2,1)S(1)}, bf16[1024,2048]{1,0:T(8,128)(2,1)S(1)}, bf16[1024,2048]{1,0:T(8,128)(2,1)}, bf16[1024,2048]{1,0:T(8,128)(2,1)}) custom-call(f32[1024,2048]{1,0:T(8,128)} %get-tuple-element.150.gate_ref, f32[1024,2048]{1,0:T(8,128)} %get-tuple-element.151.up_ref, bf16[1024,768]{1,0:T(8,128)(2,1)} %bitcast.24.g_ref.gl_ref, ...), custom_call_target="tpu_custom_call" | custom-call | flops 9663676416 | bytes 18874368 | tf_op jit(solution)/shard_map/expert_back_in/pallas_call | solution.py:710
  304.3 8.1 %all-to-all-done.2 = bf16[8,128,768]{2,1,0:T(8,128)(2,1)} async-done(((bf16[8,128,768]{2,1,0:T(8,128)(2,1)}), bf16[8,128,768]{2,1,0:T(8,128)(2,1)}, u32[]{:S(2)}, u32[]{:S(2)}) %all-to-all-start.2) | async-done | bytes 1572896 | tf_op jit(solution)/shard_map/all_to_all | solution.py:1162
  317.3 10.7 %mixture.1 = (bf16[512,768]{1,0:T(8,128)(2,1)S(1)}, f32[512,768]{1,0:T(8,128)S(1)}, f32[512,128]{1,0:T(8,128)S(1)}, f32[768,128]{1,0:T(8,128)S(1)}) custom-call(f32[512,768]{1,0:T(8,128)S(1)} %copy-done.5, bf16[512,768]{1,0:T(8,128)(2,1)S(1)} %bitcast.78, f32[512,128]{1,0:T(8,128)S(1)} %copy-done.35, s32[512,2]{1,0:T(8,128)S(1)} %bitcast.82, ...), custom_call_target="tpu_custom_call" | custom-call | flops 1610612736 | bytes 4718592 | tf_op jit(solution)/shard_map/mixture/pallas_call | solution.py:827
  330.7 16.4 %expert_weight_grads.1 = bf16[4,3,192,2048]{3,2,1,0:T(8,128)(2,1)} custom-call(bf16[1024,768]{1,0:T(8,128)(2,1)} %bitcast.18.x_ref, bf16[1024,768]{1,0:T(8,128)(2,1)} %bitcast.24.g_ref.gl_ref, bf16[1024,2048]{1,0:T(8,128)(2,1)S(1)} %copy-done.63, bf16[1024,2048]{1,0:T(8,128)(2,1)} %get-tuple-element.219.dg_ref, bf16[1024,2048]{1,0:T(8,128)(2,1)} %get-tuple-element.220.du_ref), custom_call_target="tpu_custom_call" | custom-call | flops 9663676416 | bytes 18874368 | tf_op jit(solution)/shard_map/expert_weight_grads/pallas_call | solution.py:740
  351.6 36.5 %all-to-all-done.3 = bf16[8,128,768]{2,1,0:T(8,128)(2,1)} async-done(((bf16[8,128,768]{2,1,0:T(8,128)(2,1)}), bf16[8,128,768]{2,1,0:T(8,128)(2,1)}, u32[]{:S(2)}, u32[]{:S(2)}) %all-to-all-start.3) | async-done | bytes 1572896 | tf_op jit(solution)/shard_map/all_to_all | solution.py:1162
  394.5 5.7 norm_two_back.1
  411.5 6.6 %attend_back_remote.4 = (f32[768,512]{1,0:T(8,128)S(1)}, bf16[256,768]{1,0:T(8,128)(2,1)S(1)}, bf16[256,768]{1,0:T(8,128)(2,1)S(1)}, f32[48,512]{1,0:T(8,128)S(1)}) custom-call(s32[12]{0:T(128)S(1)} %concatenate.51.sc_ref, bf16[768,512]{1,0:T(8,128)(2,1)S(1)} %copy-done.49, bf16[512,768]{1,0:T(8,128)(2,1)S(1)} %copy-done.42, ...), custom_call_target="tpu_custom_call" | custom-call | flops 4026531840 | bytes 7864320 | tf_op jit(solution)/shard_map/attend_back_remote/pallas_call | solution.py:510
  422.1 10.0 %attend_back_remote.5 = (f32[768,512]{1,0:T(8,128)S(1)}, bf16[256,1536]{1,0:T(8,128)(2,1)S(1)}, bf16[256,1536]{1,0:T(8,128)(2,1)S(1)}) custom-call(s32[12]{0:T(128)S(1)} %concatenate.51.sc_ref, bf16[768,512]{1,0:T(8,128)(2,1)S(1)} %copy-done.49, bf16[512,768]{1,0:T(8,128)(2,1)S(1)} %copy-done.42, bf16[768,512]{1,0:T(8,128)(2,1)S(1)} %copy-done.59, ...), custom_call_target="tpu_custom_call" | custom-call | flops 8053063680 | bytes 9437184 | tf_op jit(solution)/shard_map/attend_back_remote/pallas_call | solution.py:510
  436.3 10.1 %attend_back_remote.6 = (f32[768,512]{1,0:T(8,128)S(1)}, bf16[256,1536]{1,0:T(8,128)(2,1)S(1)}, bf16[256,1536]{1,0:T(8,128)(2,1)S(1)}) custom-call(s32[12]{0:T(128)S(1)} %concatenate.51.sc_ref, bf16[768,512]{1,0:T(8,128)(2,1)S(1)} %copy-done.49, bf16[512,768]{1,0:T(8,128)(2,1)S(1)} %copy-done.42, bf16[768,512]{1,0:T(8,128)(2,1)S(1)} %copy-done.59, ...), custom_call_target="tpu_custom_call" | custom-call | flops 8053063680 | bytes 9437184 | tf_op jit(solution)/shard_map/attend_back_remote/pallas_call | solution.py:510
  446.5 4.9 collective-permute-done.11.gr_ref
  457.6 10.1 %attend_back_remote.7 = (f32[768,512]{1,0:T(8,128)S(1)}, bf16[256,1536]{1,0:T(8,128)(2,1)S(1)}, bf16[256,1536]{1,0:T(8,128)(2,1)S(1)}) custom-call(s32[12]{0:T(128)S(1)} %concatenate.51.sc_ref, bf16[768,512]{1,0:T(8,128)(2,1)S(1)} %copy-done.50, bf16[512,768]{1,0:T(8,128)(2,1)S(1)} %copy-done.43, bf16[768,512]{1,0:T(8,128)(2,1)S(1)} %copy-done.59, ...), custom_call_target="tpu_custom_call" | custom-call | flops 8053063680 | bytes 9437184 | tf_op jit(solution)/shard_map/attend_back_remote/pallas_call | solution.py:510
  476.1 10.3 %attend_back_local.1 = (f32[512,768]{1,0:T(8,128)S(1)}, f32[256,1536]{1,0:T(8,128)S(1)}, f32[256,1536]{1,0:T(8,128)S(1)}) custom-call(s32[12]{0:T(128)S(1)} %concatenate.51.sc_ref, bf16[768,512]{1,0:T(8,128)(2,1)S(1)} %copy-done.50, bf16[512,768]{1,0:T(8,128)(2,1)S(1)} %copy-done.43, bf16[768,512]{1,0:T(8,128)(2,1)S(1)} %copy-done.59, ...), custom_call_target="tpu_custom_call" | custom-call | flops 4026531840 | bytes 6291456 | tf_op jit(solution)/shard_map/attend_back_local/pallas_call | solution.py:481
  487.6 5.3 q_back.1
  499.0 16.4 %collective-permute-done.17.refs_0_ = bf16[256,1536]{1,0:T(8,128)(2,1)} collective-permute-done((bf16[256,1536]{1,0:T(8,128)(2,1)}, bf16[256,1536]{1,0:T(8,128)(2,1)}, u32[]{:S(2)}, u32[]{:S(2)}) %collective-permute-start.17) | collective-permute-done | bytes 786464 | tf_op jit(solution)/shard_map/ppermute | solution.py:1070
  521.8 10.6 %kv_back.1 = (f32[512,768]{1,0:T(8,128)S(1)}, bf16[2,192,1536]{2,1,0:T(8,128)(2,1)S(1)}, f32[2,192,1536]{2,1,0:T(8,128)S(1)}) custom-call(s32[12]{0:T(128)S(1)} %concatenate.51.sc_ref, bf16[512,768]{1,0:T(8,128)(2,1)S(1)} %bitcast.76, bf16[768,512]{1,0:T(8,128)(2,1)S(1)} %turn.1.nt_ref, f32[512,768]{1,0:T(8,128)S(1)} %copy-done.20, ...), custom_call_target="tpu_custom_call" | custom-call | flops 2415919104 | bytes 9437184 | tf_op jit(solution)/shard_map/kv_back/pallas_call | solution.py:1021
  536.8 5.3 collective-permute-done.21
  557.2 6.4 %collective-permute-done.20 = bf16[192,1536]{1,0:T(8,128)(2,1)S(1)} collective-permute-done((bf16[192,1536]{1,0:T(8,128)(2,1)}, bf16[192,1536]{1,0:T(8,128)(2,1)S(1)}, u32[]{:S(2)}, u32[]{:S(2)}) %collective-permute-start.20) | collective-permute-done | bytes 589856 | tf_op jit(solution)/shard_map/ppermute | solution.py:1086
  564.6 5.6 all-to-all-start.5
  575.7 9.2 %all-to-all-done.5 = bf16[8,24,1536]{2,1,0:T(8,128)(2,1)S(1)} async-done(((bf16[8,24,1536]{2,1,0:T(8,128)(2,1)}), bf16[8,24,1536]{2,1,0:T(8,128)(2,1)S(1)}, u32[]{:S(2)}, u32[]{:S(2)}) %all-to-all-start.5) | async-done | bytes 589856 | tf_op jit(solution)/shard_map/all_to_all | solution.py:1092
  (308 shorter events, 174.8 us)
Async XLA Ops:
  7.2 72.7 %all-gather.4.cloned.1.call-start = ((), (), s32[]{:S(2)}) async-start(), calls=%async_computation.7 | async-start | bytes 5068800 | tf_op jit(solution)/shard_map/all_gather | solution.py:1128
  12.7 222.8 %all-gather.6.cloned.1.call-start = ((), (), s32[]{:S(2)}) async-start(), calls=%async_computation.9 | async-start | bytes 11796480 | tf_op jit(solution)/shard_map/all_gather | solution.py:1192
  94.2 20.0 %collective-permute-start.1 = (bf16[256,1536]{1,0:T(8,128)(2,1)}, bf16[256,1536]{1,0:T(8,128)(2,1)}, u32[]{:S(2)}, u32[]{:S(2)}) collective-permute-start(bf16[256,1536]{1,0:T(8,128)(2,1)} %get-tuple-element.126.kv_ref), channel_id=1, source_target_pairs={{0,1},{2,0},{4,2},{6,4},{7,6},{5,7},{3,5},{1,3},{8,9},{10,8},{12,1... | collective-permute-start | bytes 2359304 | tf_op jit(solution)/shard_map/ppermute | solution.py:1070
  95.7 19.7 %collective-permute-start = (bf16[256,1536]{1,0:T(8,128)(2,1)}, bf16[256,1536]{1,0:T(8,128)(2,1)}, u32[]{:S(2)}, u32[]{:S(2)}) collective-permute-start(bf16[256,1536]{1,0:T(8,128)(2,1)} %get-tuple-element.126.kv_ref), channel_id=1, source_target_pairs={{0,2},{2,4},{4,6},{6,7},{7,5},{5,3},{3,1},{1,0},{8,10},{10,12},{12... | collective-permute-start | bytes 2359304 | tf_op jit(solution)/shard_map/ppermute | solution.py:1070
  115.4 18.9 %collective-permute-start.2 = (bf16[256,1536]{1,0:T(8,128)(2,1)}, bf16[256,1536]{1,0:T(8,128)(2,1)}, u32[]{:S(2)}, u32[]{:S(2)}) collective-permute-start(bf16[256,1536]{1,0:T(8,128)(2,1)} %collective-permute-done.refs_0_.refs_1_), channel_id=1, source_target_pairs={{0,2},{2,4},{4,6},{6,7},{7,5},{5,3},{3,1},{1,0},{8,10},{10,12},{12... | collective-permute-start | bytes 2359304 | tf_op jit(solution)/shard_map/ppermute | solution.py:1070
  116.0 18.6 %collective-permute-start.3 = (bf16[256,1536]{1,0:T(8,128)(2,1)}, bf16[256,1536]{1,0:T(8,128)(2,1)}, u32[]{:S(2)}, u32[]{:S(2)}) collective-permute-start(bf16[256,1536]{1,0:T(8,128)(2,1)} %collective-permute-done.1.refs_1_.refs_0_), channel_id=1, source_target_pairs={{0,1},{2,0},{4,2},{6,4},{7,6},{5,7},{3,5},{1,3},{8,9},{10,8},{12,1... | collective-permute-start | bytes 2359304 | tf_op jit(solution)/shard_map/ppermute | solution.py:1070
  134.6 17.6 %collective-permute-start.4 = (bf16[256,1536]{1,0:T(8,128)(2,1)}, bf16[256,1536]{1,0:T(8,128)(2,1)S(1)}, u32[]{:S(2)}, u32[]{:S(2)}) collective-permute-start(bf16[256,1536]{1,0:T(8,128)(2,1)} %collective-permute-done.2.refs_0_.refs_1_), channel_id=1, source_target_pairs={{0,2},{2,4},{4,6},{6,7},{7,5},{5,3},{3,1},{1,0},{8,10},{10,12},{12... | collective-permute-start | bytes 2359304 | tf_op jit(solution)/shard_map/ppermute | solution.py:1070
  136.0 17.5 %collective-permute-start.5 = (bf16[256,1536]{1,0:T(8,128)(2,1)}, bf16[256,1536]{1,0:T(8,128)(2,1)}, u32[]{:S(2)}, u32[]{:S(2)}) collective-permute-start(bf16[256,1536]{1,0:T(8,128)(2,1)} %collective-permute-done.3.refs_1_.refs_0_), channel_id=1, source_target_pairs={{0,1},{2,0},{4,2},{6,4},{7,6},{5,7},{3,5},{1,3},{8,9},{10,8},{12,1... | collective-permute-start | bytes 2359304 | tf_op jit(solution)/shard_map/ppermute | solution.py:1070
  156.0 18.4 %collective-permute-start.7 = (bf16[256,768]{1,0:T(8,128)(2,1)}, bf16[256,768]{1,0:T(8,128)(2,1)}, u32[]{:S(2)}, u32[]{:S(2)}) collective-permute-start(bf16[256,768]{1,0:T(8,128)(2,1)} %slice.71), channel_id=1, source_target_pairs={{0,1},{2,0},{4,2},{6,4},{7,6},{5,7},{3,5},{1,3},{8,9},{10,8},{12,1... | collective-permute-start | bytes 1179656 | tf_op jit(solution)/shard_map/ppermute | solution.py:1070
  156.6 17.7 %collective-permute-start.6 = (bf16[256,768]{1,0:T(8,128)(2,1)}, bf16[256,768]{1,0:T(8,128)(2,1)}, u32[]{:S(2)}, u32[]{:S(2)}) collective-permute-start(bf16[256,768]{1,0:T(8,128)(2,1)} %slice.70), channel_id=1, source_target_pairs={{0,2},{2,4},{4,6},{6,7},{7,5},{5,3},{3,1},{1,0},{8,10},{10,12},{12... | collective-permute-start | bytes 1179656 | tf_op jit(solution)/shard_map/ppermute | solution.py:1070
  191.5 39.7 %all-to-all-start = ((bf16[8,128,768]{2,1,0:T(8,128)(2,1)}), bf16[8,128,768]{2,1,0:T(8,128)(2,1)}, u32[]{:S(2)}, u32[]{:S(2)}) async-start(bf16[8,128,768]{2,1,0:T(8,128)(2,1)} %bitcast.90), calls=%async_computation | async-start | bytes 3145728 | tf_op jit(solution)/shard_map/all_to_all | solution.py:1162
  231.2 40.3 %all-to-all-start.1 = ((bf16[8,128,768]{2,1,0:T(8,128)(2,1)}), bf16[8,128,768]{2,1,0:T(8,128)(2,1)}, u32[]{:S(2)}, u32[]{:S(2)}) async-start(bf16[8,128,768]{2,1,0:T(8,128)(2,1)} %bitcast.89), calls=%async_computation.1 | async-start | bytes 3145728 | tf_op jit(solution)/shard_map/all_to_all | solution.py:1162
  271.5 40.8 %all-to-all-start.2 = ((bf16[8,128,768]{2,1,0:T(8,128)(2,1)}), bf16[8,128,768]{2,1,0:T(8,128)(2,1)}, u32[]{:S(2)}, u32[]{:S(2)}) async-start(bf16[8,128,768]{2,1,0:T(8,128)(2,1)} %bitcast.88), calls=%async_computation.2 | async-start | bytes 3145728 | tf_op jit(solution)/shard_map/all_to_all | solution.py:1162
  276.0 277.1 %reduce-scatter.2.cloned.1.call-start = ((), (), s32[]{:S(2)}) async-start(), calls=%async_computation.8 | async-start | bytes 11796480 | tf_op jit(solution)/shard_map/reduce_scatter | solution.py:1230
  347.1 40.9 %all-to-all-start.3 = ((bf16[8,128,768]{2,1,0:T(8,128)(2,1)}), bf16[8,128,768]{2,1,0:T(8,128)(2,1)}, u32[]{:S(2)}, u32[]{:S(2)}) async-start(bf16[8,128,768]{2,1,0:T(8,128)(2,1)} %bitcast.86), calls=%async_computation.3 | async-start | bytes 3145728 | tf_op jit(solution)/shard_map/all_to_all | solution.py:1162
  418.1 14.1 %collective-permute-start.8 = (bf16[256,768]{1,0:T(8,128)(2,1)S(1)}, bf16[256,768]{1,0:T(8,128)(2,1)S(1)}, u32[]{:S(2)}, u32[]{:S(2)}) collective-permute-start(bf16[256,768]{1,0:T(8,128)(2,1)S(1)} %get-tuple-element.164), channel_id=1, source_target_pairs={{0,2},{2,4},{4,6},{6,7},{7,5},{5,3},{3,1},{1,0},{8,10},{10,12},{12... | collective-permute-start | bytes 1179656 | tf_op jit(solution)/shard_map/ppermute | solution.py:1070
  418.1 14.0 %collective-permute-start.9 = (bf16[256,768]{1,0:T(8,128)(2,1)S(1)}, bf16[256,768]{1,0:T(8,128)(2,1)S(1)}, u32[]{:S(2)}, u32[]{:S(2)}) collective-permute-start(bf16[256,768]{1,0:T(8,128)(2,1)S(1)} %get-tuple-element.165), channel_id=1, source_target_pairs={{0,1},{2,0},{4,2},{6,4},{7,6},{5,7},{3,5},{1,3},{8,9},{10,8},{12,1... | collective-permute-start | bytes 1179656 | tf_op jit(solution)/shard_map/ppermute | solution.py:1070
  420.9 11.2 %collective-permute-start.10 = (bf16[2,192,896]{2,1,0:T(8,128)(2,1)S(1)}, bf16[2,192,896]{2,1,0:T(8,128)(2,1)S(1)}, u32[]{:S(2)}, u32[]{:S(2)}) collective-permute-start(bf16[2,192,896]{2,1,0:T(8,128)(2,1)S(1)} %fusion.4), channel_id=1, source_target_pairs={{0,8},{8,0},{16,24},{24,16},{1,9},{9,1},{17,25},{25,17},{2,10},{10... | collective-permute-start | bytes 2064392 | tf_op jit(solution)/shard_map/ppermute | solution.py:1078
  432.4 18.9 %collective-permute-start.11 = (bf16[256,1536]{1,0:T(8,128)(2,1)S(1)}, bf16[256,1536]{1,0:T(8,128)(2,1)S(1)}, u32[]{:S(2)}, u32[]{:S(2)}) collective-permute-start(bf16[256,1536]{1,0:T(8,128)(2,1)S(1)} %get-tuple-element.177), channel_id=1, source_target_pairs={{0,2},{2,4},{4,6},{6,7},{7,5},{5,3},{3,1},{1,0},{8,10},{10,12},{12... | collective-permute-start | bytes 2359304 | tf_op jit(solution)/shard_map/ppermute | solution.py:1070
  432.6 20.5 %collective-permute-start.12 = (bf16[256,1536]{1,0:T(8,128)(2,1)S(1)}, bf16[256,1536]{1,0:T(8,128)(2,1)S(1)}, u32[]{:S(2)}, u32[]{:S(2)}) collective-permute-start(bf16[256,1536]{1,0:T(8,128)(2,1)S(1)} %get-tuple-element.178), channel_id=1, source_target_pairs={{0,1},{2,0},{4,2},{6,4},{7,6},{5,7},{3,5},{1,3},{8,9},{10,8},{12,1... | collective-permute-start | bytes 2359304 | tf_op jit(solution)/shard_map/ppermute | solution.py:1070
  435.7 10.7 %collective-permute-start.13 = (bf16[192,896]{1,0:T(8,128)(2,1)S(1)}, bf16[192,896]{1,0:T(8,128)(2,1)S(1)}, u32[]{:S(2)}, u32[]{:S(2)}) collective-permute-start(bf16[192,896]{1,0:T(8,128)(2,1)S(1)} %fusion.6), channel_id=1, source_target_pairs={{0,16},{16,0},{8,24},{24,8},{1,17},{17,1},{9,25},{25,9},{2,18},{18... | collective-permute-start | bytes 1032200 | tf_op jit(solution)/shard_map/ppermute | solution.py:1086
  453.1 34.5 %slice-start.2 = ((s8[4915200]{0:T(1024)(128)(4,1)}), s8[4194304]{0:T(1024)(128)(4,1)S(1)}, s32[]{:S(2)}) async-start(s8[4915200]{0:T(1024)(128)(4,1)} %bitcast.72), calls=%async_computation.12 | async-start | bytes 8388608
  453.6 18.8 %collective-permute-start.14 = (bf16[256,1536]{1,0:T(8,128)(2,1)S(1)}, bf16[256,1536]{1,0:T(8,128)(2,1)S(1)}, u32[]{:S(2)}, u32[]{:S(2)}) collective-permute-start(bf16[256,1536]{1,0:T(8,128)(2,1)S(1)} %get-tuple-element.188), channel_id=1, source_target_pairs={{0,2},{2,4},{4,6},{6,7},{7,5},{5,3},{3,1},{1,0},{8,10},{10,12},{12... | collective-permute-start | bytes 2359304 | tf_op jit(solution)/shard_map/ppermute | solution.py:1070
  456.9 17.9 %collective-permute-start.15 = (bf16[256,1536]{1,0:T(8,128)(2,1)S(1)}, bf16[256,1536]{1,0:T(8,128)(2,1)S(1)}, u32[]{:S(2)}, u32[]{:S(2)}) collective-permute-start(bf16[256,1536]{1,0:T(8,128)(2,1)S(1)} %get-tuple-element.189), channel_id=1, source_target_pairs={{0,1},{2,0},{4,2},{6,4},{7,6},{5,7},{3,5},{1,3},{8,9},{10,8},{12,1... | collective-permute-start | bytes 2359304 | tf_op jit(solution)/shard_map/ppermute | solution.py:1070
  495.1 2.1 collective-permute-start.16
  495.1 20.3 %collective-permute-start.17 = (bf16[256,1536]{1,0:T(8,128)(2,1)}, bf16[256,1536]{1,0:T(8,128)(2,1)}, u32[]{:S(2)}, u32[]{:S(2)}) collective-permute-start(bf16[256,1536]{1,0:T(8,128)(2,1)} %get-tuple-element.210), channel_id=1, source_target_pairs={{0,2},{2,4},{4,6},{6,7},{7,5},{5,3},{3,1},{1,0},{8,10},{10,12},{12... | collective-permute-start | bytes 2359304 | tf_op jit(solution)/shard_map/ppermute | solution.py:1070
  496.6 20.0 %collective-permute-start.18 = (bf16[256,1536]{1,0:T(8,128)(2,1)}, bf16[256,1536]{1,0:T(8,128)(2,1)}, u32[]{:S(2)}, u32[]{:S(2)}) collective-permute-start(bf16[256,1536]{1,0:T(8,128)(2,1)} %get-tuple-element.211), channel_id=1, source_target_pairs={{0,1},{2,0},{4,2},{6,4},{7,6},{5,7},{3,5},{1,3},{8,9},{10,8},{12,1... | collective-permute-start | bytes 2359304 | tf_op jit(solution)/shard_map/ppermute | solution.py:1070
  532.4 2.9 collective-permute-start.19
  532.6 9.5 %collective-permute-start.21 = (bf16[192,768]{1,0:T(8,128)(2,1)S(1)}, bf16[192,768]{1,0:T(8,128)(2,1)S(1)}, u32[]{:S(2)}, u32[]{:S(2)}) collective-permute-start(bf16[192,768]{1,0:T(8,128)(2,1)S(1)} %fusion.7), channel_id=1, source_target_pairs={{0,16},{16,0},{8,24},{24,8},{1,17},{17,1},{9,25},{25,9},{2,18},{18... | collective-permute-start | bytes 884744 | tf_op jit(solution)/shard_map/ppermute | solution.py:1086
  543.1 21.5 %all-to-all-start.4 = ((bf16[8,24,1664]{2,1,0:T(8,128)(2,1)}), bf16[8,24,1664]{2,1,0:T(8,128)(2,1)}, u32[]{:S(2)}, u32[]{:S(2)}) async-start(bf16[8,24,1664]{2,1,0:T(8,128)(2,1)} %fusion.1), calls=%async_computation.5 | async-start | bytes 1277952 | tf_op jit(solution)/shard_map/all_to_all | solution.py:1092
  548.5 15.1 %collective-permute-start.20 = (bf16[192,1536]{1,0:T(8,128)(2,1)}, bf16[192,1536]{1,0:T(8,128)(2,1)S(1)}, u32[]{:S(2)}, u32[]{:S(2)}) collective-permute-start(bf16[192,1536]{1,0:T(8,128)(2,1)} %fusion.5), channel_id=1, source_target_pairs={{0,16},{16,0},{8,24},{24,8},{1,17},{17,1},{9,25},{25,9},{2,18},{18... | collective-permute-start | bytes 1769480 | tf_op jit(solution)/shard_map/ppermute | solution.py:1086
  564.6 20.3 %all-to-all-start.5 = ((bf16[8,24,1536]{2,1,0:T(8,128)(2,1)}), bf16[8,24,1536]{2,1,0:T(8,128)(2,1)S(1)}, u32[]{:S(2)}, u32[]{:S(2)}) async-start(bf16[8,24,1536]{2,1,0:T(8,128)(2,1)} %bitcast.50), calls=%async_computation.6 | async-start | bytes 1179648 | tf_op jit(solution)/shard_map/all_to_all | solution.py:1092
  (85 other events, 424.2 us)
Sparse Core Ops, SparseCore 0:
  12.8 67.0 all-gather.3
  81.5 62.5 all-gather.5
  347.2 76.0 reduce-scatter.1

commit v5 on v4

--- a/solution.py
+++ b/solution.py
@@ -24,7 +24,7 @@
 BF16 = jnp.bfloat16
 ALL_AXES = ("dp", "expert")
 VMEM_SMALL = 24 * 1024 * 1024
-VMEM_LARGE = 44 * 1024 * 1024
+VMEM_LARGE = 60 * 1024 * 1024
 
 
 def dot(a, b):
@@ -40,7 +40,7 @@
     return hi, (v - hi.astype(F32)).astype(BF16)
 
 
-def params(cost=None, limit=VMEM_SMALL):
+def params(cost=None, limit=VMEM_LARGE):
     return dict(
         compiler_params=pltpu.CompilerParams(vmem_limit_bytes=limit),
         cost_estimate=None if cost is None else pl.CostEstimate(
@@ -564,14 +564,6 @@
     xs_ref[...] = dot(pick.astype(BF16), n_ref[...]).astype(BF16)
 
 
-def out_w_spec():
-    return spec((D, D), lambda *_: (0, 3))
-
-
-def small_w_spec():
-    return spec((D, LANES), lambda *_: (0, 4 * D // LANES))
-
-
 def grad_rows_body(g_ref, pr_ref, tr_ref, gs_ref, mg_ref):
     t = g_ref.shape[0]
     step = pl.program_id(0)
@@ -603,14 +595,14 @@
     )(g, pr, tr)
 
 
-def route_call(x, att, pack, gain, res, rt, tr, slots):
+def route_call(x, att, ow, sw, gain, res, rt, tr, slots):
     t = x.shape[0]
     part = min(slots, 256)
     return pl.pallas_call(
         route_body,
         grid=(slots // part,),
         in_specs=[
-            whole((t, D)), whole((t, D)), out_w_spec(), small_w_spec(), whole((1, D)),
+            whole((t, D)), whole((t, D)), whole((D, D)), whole((D, LANES)), whole((1, D)),
             whole((t, LANES)), whole((t, 2)), whole((2, t)),
         ],
         out_specs=[
@@ -622,8 +614,8 @@
             shape((slots, D), BF16),
         ],
         name="route_dispatch",
-        **params((2 * t * D * D + 2 * slots * t * D, 8 * t * D)),
-    )(x, att, pack, pack, gain, res, rt, tr)
+        **params((2 * t * D * D + 2 * slots * t * D, 8 * t * D), VMEM_SMALL),
+    )(x, att, ow, sw, gain, res, rt, tr)
 
 
 def expert_fwd_body(x_ref, w_ref, o_ref, gate_ref, up_ref, acc_ref):
@@ -665,7 +657,7 @@
         out_shape=[shape((rows, D), BF16)] + [shape((rows, wide), F32)] * 2,
         scratch_shapes=[pltpu.VMEM((rows, D), F32)],
         name="expert_forward",
-        **params((6 * rows * D * wide, 6 * D * wide), VMEM_LARGE),
+        **params((6 * rows * D * wide, 6 * D * wide)),
     )(xr, w)
 
 
@@ -715,7 +707,7 @@
         out_shape=[shape((rows, D), BF16)] + [shape((rows, wide), BF16)] * 3,
         scratch_shapes=[pltpu.VMEM((rows, D), F32)],
         name="expert_back_in",
-        **params((6 * rows * D * wide, 12 * D * wide), VMEM_LARGE),
+        **params((6 * rows * D * wide, 12 * D * wide)),
     )(gate, up, gr, w)
 
 
@@ -745,7 +737,7 @@
         out_shape=shape(dims, BF16),
         scratch_shapes=[pltpu.VMEM((D, rows), BF16), pltpu.VMEM((D, rows), BF16)],
         name="expert_weight_grads",
-        **params((6 * rows * D * wide, 12 * D * wide), VMEM_LARGE),
+        **params((6 * rows * D * wide, 12 * D * wide)),
     )(xr, low, act, d_gate, d_up)
 
 
@@ -817,7 +809,7 @@
         gs_ref[...] += gs
 
 
-def mix_call(hidden, g, pr, rt, tc, ret, low, pack, rows):
+def mix_call(hidden, g, pr, rt, tc, ret, low, sw, rows):
     t = hidden.shape[0]
     half = min(t, LANES)
     slots = ret.shape[0]
@@ -828,7 +820,7 @@
         mix_body,
         grid=(t // half,),
         in_specs=[
-            tile, tile, lane_tile, pair, pair, whole((slots, D)), tile, small_w_spec(),
+            tile, tile, lane_tile, pair, pair, whole((slots, D)), tile, whole((D, LANES)),
             whole((8, D)),
         ],
         out_specs=[tile, tile, lane_tile, whole((D, LANES))],
@@ -837,7 +829,7 @@
         ],
         name="mixture",
         **params((4 * t * slots * D, 12 * t * D)),
-    )(hidden, g, pr, rt, tc, ret, low, pack, rows)
+    )(hidden, g, pr, rt, tc, ret, low, sw, rows)
 
 
 def norm_back_body(
@@ -873,7 +865,7 @@
         gg_ref[...] += jnp.broadcast_to(gain, gg_ref.shape)
 
 
-def norm_back_call(hidden, g, gn, tc, ret, rows, pack, att):
+def norm_back_call(hidden, g, gn, tc, ret, rows, ow, att):
     t = hidden.shape[0]
     half = t // 2 if (t // 2) % LANES == 0 else t
     slots = ret.shape[0]
@@ -883,7 +875,7 @@
         grid=(t // half,),
         in_specs=[
             tile, tile, tile, spec((half, 2), lambda i: (i, 0)), whole((slots, D)), whole((8, D)),
-            out_w_spec(), tile,
+            whole((D, D)), tile,
         ],
         out_specs=[tile, tile, spec((D, half), lambda i: (0, i)), whole((D, D)), whole((8, D))],
         out_shape=[
@@ -891,8 +883,8 @@
             shape((8, D), F32),
         ],
         name="norm_two_back",
-        **params((2 * t * slots * D + 4 * t * D * D, 16 * t * D)),
-    )(hidden, g, gn, tc, ret, rows, pack, att)
+        **params((2 * t * slots * D + 4 * t * D * D, 16 * t * D), VMEM_SMALL),
+    )(hidden, g, gn, tc, ret, rows, ow, att)
 
 
 def turn_body(x_ref, o_ref):
@@ -1171,8 +1163,8 @@
 
     x = to_rows(hidden_in)
     g = to_rows(cotangent)
-    small_w = pack[:, 4 * D :]
-    small_rows = jnp.transpose(small_w[:, 16:24]).astype(F32)
+    out_w, small_w = pack[:, 3 * D : 4 * D], pack[:, 4 * D :]
+    small_rows = jnp.transpose(pack[:, 4 * D + 16 : 4 * D + 24]).astype(F32)
     gain_one = small_rows[2:3]
     rows_two = jnp.concatenate([small_rows[0:2], small_rows[3:4], small_rows[3:8]], axis=0)
     gain_two = small_rows[3:4]
@@ -1201,7 +1193,9 @@
                 st, acc = fwd_local(sc, q_t, kv_prompt, kv_own)
             else:
                 st, acc = fwd_remote(sc, q_t, (right[i], left[i]), (8 - i, i), st, acc)
-            right[i + 1], left[i + 1], st = tie(right[i + 1], left[i + 1], st)
+            right[i + 1], left[i + 1], st, out_w, small_w = tie(
+                right[i + 1], left[i + 1], st, out_w, small_w
+            )
         far = [along_ring(right[3][:, :D], 1), along_ring(left[3][:, D:], -1)]
         st, acc = fwd_remote(sc, q_t, (right[3], left[3]), (5, 3), st, acc)
         st, att_t, att = fwd_remote(sc, q_t, far, (4,), st, acc, halves=True, final=True)
@@ -1211,7 +1205,7 @@
 
     res = jnp.pad(to_rows(gate_residual), ((0, 0), (0, LANES - EXPERTS - 4)))
     hidden, low_two, pr, x_send = route_call(
-        x, att, pack, gain_two, res, picked, target_rows, slots
+        x, att, out_w, small_w, gain_two, res, picked, target_rows, slots
     )
     x_got = exchange(to_owners(x_send))
     g_send = grad_rows_call(g, pr, target_rows, slots)
@@ -1223,7 +1217,7 @@
     grad_in, act, d_gate, d_up = expert_in(gate_pre, up_pre, g_got, weights)
     in_back = from_owners(grad_in)
     output, gn, grad_logits, grad_small = mix_call(
-        hidden, g, pr, picked, target_cols, out_back, low_two, pack, rows_two
+        hidden, g, pr, picked, target_cols, out_back, low_two, small_w, rows_two
     )
     act, gn = tie(act, gn)
     grad_w = expert_weights(x_got, g_got, act, d_gate, d_up, weights.shape)
@@ -1233,7 +1227,7 @@
     per = gate_weight.shape[0]
     grad_expert = [grad_expert[i * per : (i + 1) * per].astype(F32) for i in range(3)]
     gh, d_att, d_att_t, grad_ow, gg_two = norm_back_call(
-        hidden, g, gn, target_cols, in_back, rows_two, pack, att
+        hidden, g, gn, target_cols, in_back, rows_two, out_w, att
     )
 
     early = jnp.concatenate(

time: 603 us -> 592 us (0.982)
  local copies, waits for them, and re-layouts: 91.5 us -> 48.9 us
  Pallas kernels: 198 us -> 229 us
  other arithmetic: 17.1 us -> 23.4 us
    unnamed x179 -> x85, local copies, waits for them, and re-layouts: 65.8 us -> 23 us
    pallas_call x3, Pallas kernels: 2.02 us -> 8.42 us  [ring_add(): pl.pallas_call(functools.partial(ring_add_body, half), grid=(2,), in_spec...]
  transfers between devices with their start and end apart: 31 -> 31, of which waited for: 23 -> 23; matrix products, arithmetic and copies ran while one was open for 7% -> 8% of each run, Pallas kernels for 29% -> 34%
where the time goes in v5:
time: 592 us; the launch traced here: 582 us
  Pallas kernels  229 us (39%)
  waiting for transfers between devices  217 us (37%)
  starting transfers between devices  49.3 us (8%)
  local copies, waits for them, and re-layouts  48.9 us (8%)
  other arithmetic  23.4 us (4%)
  between operations  14.5 us (2%)
    all_to_all x4, waiting for transfers between devices, exchange(): lax.all_to_all(rows, 'expert', split_axis=0, concat_axis=0, tiled=True)  93.1 us
    all_gather x1, waiting for transfers between devices, per_device(): lax.all_gather(jnp.concatenate([qkv_weight, out_weight, small], axis=1),...  58.7 us
    ppermute x16, waiting for transfers between devices, along_ring(): return lax.ppermute(array, 'expert', pairs)  43.3 us
    pallas_call x4, Pallas kernels, bwd_remote(): pl.pallas_call(functools.partial(bwd_remote_body, tuple(offsets), len(kvs...  40.9 us
    pallas_call x4, Pallas kernels, fwd_remote(): pl.pallas_call(functools.partial(fwd_remote_body, tuple(offsets), len(kvs...  38.2 us
    pallas_call x1, Pallas kernels, expert_in(): pl.pallas_call(expert_in_body, grid=(wide // part,), in_specs=[tile, tile...  23.7 us
    unnamed x85, local copies, waits for them, and re-layouts  23 us
    pallas_call x1, Pallas kernels, expert_fwd(): pl.pallas_call(expert_fwd_body, grid=(wide // part,), in_specs=[whole((ro...  19.1 us
  transfers between devices with their start and end apart: 31, of which 23 were waited for; matrix products, arithmetic and copies ran while one was open for 8% of the time, Pallas kernels for 34%

profile of v5, /device:TPU:0, one launch (start us, length us, event | category | flops | bytes accessed | tf_op | source)
XLA Modules:
  0.0 582.2 jit_solution(6919510512564486127)
XLA Ops:
  21.2 58.7 %all-gather.4.cloned.1.call-done.wq_ref.wk_ref.wv_ref.w_ref = bf16[768,3200]{1,0:T(8,128)(2,1)} async-done(((bf16[24,3200]{1,0:T(8,128)(2,1)}), bf16[768,3200]{1,0:T(8,128)(2,1)}) %all-gather.4.cloned.1.call-update) | async-done | bytes 4915216 | tf_op jit(solution)/shard_map/all_gather | solution.py:1120
  82.0 9.0 %qkv_rope.1 = (bf16[512,768]{1,0:T(8,128)(2,1)}, bf16[512,768]{1,0:T(8,128)(2,1)}, bf16[768,512]{1,0:T(8,128)(2,1)}, bf16[256,1536]{1,0:T(8,128)(2,1)}, bf16[256,1536]{1,0:T(8,128)(2,1)}) custom-call(bf16[512,768]{1,0:T(8,128)(2,1)} %bitcast.70, f32[1,768]{1,0:T(1,128)} %copy.137.gain_ref, ...), custom_call_target="tpu_custom_call" | custom-call | flops 1811939328 | bytes 3538944 | tf_op jit(solution)/shard_map/qkv_rope/pallas_call | solution.py:100
  97.9 10.0 %attend_local.1 = (f32[48,512]{1,0:T(8,128)}, f32[768,512]{1,0:T(8,128)}) custom-call(s32[12]{0:T(128)} %concatenate.51.sc_ref, bf16[768,512]{1,0:T(8,128)(2,1)} %get-tuple-element.130.qt_ref, bf16[256,1536]{1,0:T(8,128)(2,1)} %get-tuple-element.132.kv_ref, bf16[256,1536]{1,0:T(8,128)(2,1)} %get-tuple-element.133.kvo_ref), custom_call_target="tpu_custom_call" | custom-call | flops 1610612736 | bytes 1572864 | tf_op jit(solution)/shard_map/attend_local/pallas_call | solution.py:262
  114.1 10.2 %attend_remote.4 = (f32[48,512]{1,0:T(8,128)}, f32[768,512]{1,0:T(8,128)}) custom-call(s32[12]{0:T(128)} %concatenate.51.sc_ref, bf16[768,512]{1,0:T(8,128)(2,1)} %get-tuple-element.130.qt_ref, bf16[256,1536]{1,0:T(8,128)(2,1)} %copy-done.37, bf16[256,1536]{1,0:T(8,128)(2,1)} %collective-permute-done.1.refs_1_.refs_0_, ...), custom_call_target="tpu_custom_call" | custom-call | flops 3221225472 | bytes 4718592 | tf_op jit(solution)/shard_map/attend_remote/pallas_call | solution.py:286
  124.3 6.5 %collective-permute-done.2.refs_0_.refs_1_ = bf16[256,1536]{1,0:T(8,128)(2,1)} collective-permute-done((bf16[256,1536]{1,0:T(8,128)(2,1)S(1)}, bf16[256,1536]{1,0:T(8,128)(2,1)}, u32[]{:S(2)}, u32[]{:S(2)}) %collective-permute-start.2) | collective-permute-done | bytes 786464 | tf_op jit(solution)/shard_map/ppermute | solution.py:1062
  134.4 10.2 %attend_remote.5 = (f32[48,512]{1,0:T(8,128)}, f32[768,512]{1,0:T(8,128)}) custom-call(s32[12]{0:T(128)} %concatenate.51.sc_ref, bf16[768,512]{1,0:T(8,128)(2,1)} %get-tuple-element.130.qt_ref, bf16[256,1536]{1,0:T(8,128)(2,1)} %collective-permute-done.2.refs_0_.refs_1_, bf16[256,1536]{1,0:T(8,128)(2,1)} %collective-permute-done.3.refs_1_.refs_0_, ...), custom_call_target="tpu_custom_call" | custom-call | flops 3221225472 | bytes 4718592 | tf_op jit(solution)/shard_map/attend_remote/pallas_call | solution.py:286
  155.7 10.2 %attend_remote.6 = (f32[48,512]{1,0:T(8,128)}, f32[768,512]{1,0:T(8,128)}) custom-call(s32[12]{0:T(128)} %concatenate.51.sc_ref, bf16[768,512]{1,0:T(8,128)(2,1)} %get-tuple-element.130.qt_ref, bf16[256,1536]{1,0:T(8,128)(2,1)} %collective-permute-done.4.refs_0_.refs_1_, bf16[256,1536]{1,0:T(8,128)(2,1)} %collective-permute-done.5.refs_1_.refs_0_, ...), custom_call_target="tpu_custom_call" | custom-call | flops 3221225472 | bytes 4718592 | tf_op jit(solution)/shard_map/attend_remote/pallas_call | solution.py:286
  165.9 7.6 %attend_remote.7 = (f32[48,512]{1,0:T(8,128)}, f32[768,512]{1,0:T(8,128)}, bf16[512,768]{1,0:T(8,128)(2,1)}) custom-call(s32[12]{0:T(128)} %concatenate.51.sc_ref, bf16[768,512]{1,0:T(8,128)(2,1)} %get-tuple-element.130.qt_ref, bf16[256,768]{1,0:T(8,128)(2,1)} %collective-permute-done.6.refs_0_, bf16[256,768]{1,0:T(8,128)(2,1)} %collective-permute-done.7.refs_1_, ...), custom_call_target="tpu_custom_call" | custom-call | flops 1610612736 | bytes 3932160 | tf_op jit(solution)/shard_map/attend_remote/pallas_call | solution.py:286
  174.6 5.7 route_dispatch.1
  184.3 6.5 %all-to-all-start = ((bf16[8,128,768]{2,1,0:T(8,128)(2,1)}), bf16[8,128,768]{2,1,0:T(8,128)(2,1)}, u32[]{:S(2)}, u32[]{:S(2)}) async-start(bf16[8,128,768]{2,1,0:T(8,128)(2,1)} %bitcast.83), calls=%async_computation | async-start | bytes 3145728 | tf_op jit(solution)/shard_map/all_to_all | solution.py:1154
  191.8 4.8 grad_rows.1
  196.6 28.0 %all-to-all-done = bf16[8,128,768]{2,1,0:T(8,128)(2,1)} async-done(((bf16[8,128,768]{2,1,0:T(8,128)(2,1)}), bf16[8,128,768]{2,1,0:T(8,128)(2,1)}, u32[]{:S(2)}, u32[]{:S(2)}) %all-to-all-start) | async-done | bytes 1572896 | tf_op jit(solution)/shard_map/all_to_all | solution.py:1154
  228.9 19.1 %expert_forward.1 = (bf16[1024,768]{1,0:T(8,128)(2,1)}, f32[1024,2048]{1,0:T(8,128)}, f32[1024,2048]{1,0:T(8,128)}) custom-call(bf16[1024,768]{1,0:T(8,128)(2,1)} %bitcast.18.x_ref, bf16[4,3,192,2048]{3,2,1,0:T(8,128)(2,1)} %bitcast.113), custom_call_target="tpu_custom_call" | custom-call | flops 9663676416 | bytes 9437184 | tf_op jit(solution)/shard_map/expert_forward/pallas_call | solution.py:652
  248.0 16.9 %all-to-all-done.1 = bf16[8,128,768]{2,1,0:T(8,128)(2,1)} async-done(((bf16[8,128,768]{2,1,0:T(8,128)(2,1)}), bf16[8,128,768]{2,1,0:T(8,128)(2,1)}, u32[]{:S(2)}, u32[]{:S(2)}) %all-to-all-start.1) | async-done | bytes 1572896 | tf_op jit(solution)/shard_map/all_to_all | solution.py:1154
  270.8 23.7 %expert_back_in.1 = (bf16[1024,768]{1,0:T(8,128)(2,1)}, bf16[1024,2048]{1,0:T(8,128)(2,1)}, bf16[1024,2048]{1,0:T(8,128)(2,1)}, bf16[1024,2048]{1,0:T(8,128)(2,1)}) custom-call(f32[1024,2048]{1,0:T(8,128)} %get-tuple-element.162.gate_ref, f32[1024,2048]{1,0:T(8,128)} %get-tuple-element.163.up_ref, bf16[1024,768]{1,0:T(8,128)(2,1)} %bitcast.24.g_ref.gl_ref, ...), custom_call_target="tpu_custom_call" | custom-call | flops 9663676416 | bytes 18874368 | tf_op jit(solution)/shard_map/expert_back_in/pallas_call | solution.py:702
  294.5 11.1 %all-to-all-done.2 = bf16[8,128,768]{2,1,0:T(8,128)(2,1)} async-done(((bf16[8,128,768]{2,1,0:T(8,128)(2,1)}), bf16[8,128,768]{2,1,0:T(8,128)(2,1)}, u32[]{:S(2)}, u32[]{:S(2)}) %all-to-all-start.2) | async-done | bytes 1572896 | tf_op jit(solution)/shard_map/all_to_all | solution.py:1154
  305.6 12.3 %mixture.1 = (bf16[512,768]{1,0:T(8,128)(2,1)}, f32[512,768]{1,0:T(8,128)}, f32[512,128]{1,0:T(8,128)}, f32[768,128]{1,0:T(8,128)}) custom-call(f32[512,768]{1,0:T(8,128)} %copy-done.8, bf16[512,768]{1,0:T(8,128)(2,1)} %bitcast.75, f32[512,128]{1,0:T(8,128)} %copy-done.19, s32[512,2]{1,0:T(8,128)} %bitcast.81, s32[512,2]{1,0:T(8,128)} %bitcast.77, ...), custom_call_target="tpu_custom_call" | custom-call | flops 1610612736 | bytes 4718592 | tf_op jit(solution)/shard_map/mixture/pallas_call | solution.py:819
  317.9 17.3 %expert_weight_grads.1 = bf16[4,3,192,2048]{3,2,1,0:T(8,128)(2,1)} custom-call(bf16[1024,768]{1,0:T(8,128)(2,1)} %bitcast.18.x_ref, bf16[1024,768]{1,0:T(8,128)(2,1)} %bitcast.24.g_ref.gl_ref, bf16[1024,2048]{1,0:T(8,128)(2,1)} %get-tuple-element.230.act_ref, bf16[1024,2048]{1,0:T(8,128)(2,1)} %get-tuple-element.231.dg_ref, ...), custom_call_target="tpu_custom_call" | custom-call | flops 9663676416 | bytes 18874368 | tf_op jit(solution)/shard_map/expert_weight_grads/pallas_call | solution.py:732
  339.1 37.1 %all-to-all-done.3 = bf16[8,128,768]{2,1,0:T(8,128)(2,1)S(1)} async-done(((bf16[8,128,768]{2,1,0:T(8,128)(2,1)}), bf16[8,128,768]{2,1,0:T(8,128)(2,1)S(1)}, u32[]{:S(2)}, u32[]{:S(2)}) %all-to-all-start.3) | async-done | bytes 1572896 | tf_op jit(solution)/shard_map/all_to_all | solution.py:1154
  381.9 4.6 norm_two_back.1
  393.4 8.4 %attend_back_remote.4 = (f32[768,512]{1,0:T(8,128)}, bf16[256,768]{1,0:T(8,128)(2,1)}, bf16[256,768]{1,0:T(8,128)(2,1)}, f32[48,512]{1,0:T(8,128)}) custom-call(s32[12]{0:T(128)} %concatenate.51.sc_ref, bf16[768,512]{1,0:T(8,128)(2,1)} %get-tuple-element.130.qt_ref, bf16[512,768]{1,0:T(8,128)(2,1)} %get-tuple-element.131.q_ref, bf16[768,512]{1,0:T(8,128)(2,1)} %copy-done.17, ...), custom_call_target="tpu_custom_call" | custom-call | flops 4026531840 | bytes 7864320 | tf_op jit(solution)/shard_map/attend_back_remote/pallas_call | solution.py:510
  403.9 10.9 %attend_back_remote.5 = (f32[768,512]{1,0:T(8,128)}, bf16[256,1536]{1,0:T(8,128)(2,1)}, bf16[256,1536]{1,0:T(8,128)(2,1)}) custom-call(s32[12]{0:T(128)} %concatenate.51.sc_ref, bf16[768,512]{1,0:T(8,128)(2,1)} %get-tuple-element.130.qt_ref, bf16[512,768]{1,0:T(8,128)(2,1)} %get-tuple-element.131.q_ref, bf16[768,512]{1,0:T(8,128)(2,1)} %copy-done.17, ...), custom_call_target="tpu_custom_call" | custom-call | flops 8053063680 | bytes 9437184 | tf_op jit(solution)/shard_map/attend_back_remote/pallas_call | solution.py:510
  421.8 10.9 %attend_back_remote.6 = (f32[768,512]{1,0:T(8,128)}, bf16[256,1536]{1,0:T(8,128)(2,1)}, bf16[256,1536]{1,0:T(8,128)(2,1)}) custom-call(s32[12]{0:T(128)} %concatenate.51.sc_ref, bf16[768,512]{1,0:T(8,128)(2,1)} %get-tuple-element.130.qt_ref, bf16[512,768]{1,0:T(8,128)(2,1)} %get-tuple-element.131.q_ref, bf16[768,512]{1,0:T(8,128)(2,1)} %copy-done.17, ...), custom_call_target="tpu_custom_call" | custom-call | flops 8053063680 | bytes 9437184 | tf_op jit(solution)/shard_map/attend_back_remote/pallas_call | solution.py:510
  432.7 4.7 collective-permute-done.11.gr_ref
  448.4 10.9 %attend_back_remote.7 = (f32[768,512]{1,0:T(8,128)}, bf16[256,1536]{1,0:T(8,128)(2,1)}, bf16[256,1536]{1,0:T(8,128)(2,1)}) custom-call(s32[12]{0:T(128)} %concatenate.51.sc_ref, bf16[768,512]{1,0:T(8,128)(2,1)} %get-tuple-element.130.qt_ref, bf16[512,768]{1,0:T(8,128)(2,1)} %get-tuple-element.131.q_ref, bf16[768,512]{1,0:T(8,128)(2,1)} %copy-done.17, ...), custom_call_target="tpu_custom_call" | custom-call | flops 8053063680 | bytes 9437184 | tf_op jit(solution)/shard_map/attend_back_remote/pallas_call | solution.py:510
  467.6 11.0 %attend_back_local.1 = (f32[512,768]{1,0:T(8,128)}, f32[256,1536]{1,0:T(8,128)}, f32[256,1536]{1,0:T(8,128)}) custom-call(s32[12]{0:T(128)} %concatenate.51.sc_ref, bf16[768,512]{1,0:T(8,128)(2,1)} %get-tuple-element.130.qt_ref, bf16[512,768]{1,0:T(8,128)(2,1)} %get-tuple-element.131.q_ref, bf16[768,512]{1,0:T(8,128)(2,1)} %copy-done.17, ...), custom_call_target="tpu_custom_call" | custom-call | flops 4026531840 | bytes 6291456 | tf_op jit(solution)/shard_map/attend_back_local/pallas_call | solution.py:481
  478.5 7.5 %q_back.1 = (f32[512,768]{1,0:T(8,128)}, bf16[2,192,768]{2,1,0:T(8,128)(2,1)}, f32[2,192,768]{2,1,0:T(8,128)}) custom-call(s32[12]{0:T(128)} %concatenate.51.sc_ref, bf16[768,512]{1,0:T(8,128)(2,1)} %turn.1.nt_ref, f32[512,768]{1,0:T(8,128)} %get-tuple-element.215.dq_ref, f32[512,128]{1,0:T(8,128)} %pad_maximum_fusion.1.c_ref, ...), custom_call_target="tpu_custom_call" | custom-call | flops 1207959552 | bytes 4718592 | tf_op jit(solution)/shard_map/q_back/pallas_call | solution.py:962
  491.5 14.7 %collective-permute-done.17.refs_0_ = bf16[256,1536]{1,0:T(8,128)(2,1)S(1)} collective-permute-done((bf16[256,1536]{1,0:T(8,128)(2,1)}, bf16[256,1536]{1,0:T(8,128)(2,1)S(1)}, u32[]{:S(2)}, u32[]{:S(2)}) %collective-permute-start.17) | collective-permute-done | bytes 786464 | tf_op jit(solution)/shard_map/ppermute | solution.py:1062
  508.3 13.5 %kv_back.1 = (f32[512,768]{1,0:T(8,128)}, bf16[2,192,1536]{2,1,0:T(8,128)(2,1)}, f32[2,192,1536]{2,1,0:T(8,128)}) custom-call(s32[12]{0:T(128)} %concatenate.51.sc_ref, bf16[512,768]{1,0:T(8,128)(2,1)} %bitcast.71, bf16[768,512]{1,0:T(8,128)(2,1)} %turn.1.nt_ref, f32[512,768]{1,0:T(8,128)} %get-tuple-element.216.gnq_ref, f32[512,768]{1,0:T(8,128)} %copy-done.6, ...), custom_call_target="tpu_custom_call" | custom-call | flops 2415919104 | bytes 9437184 | tf_op jit(solution)/shard_map/kv_back/pallas_call | solution.py:1013
  547.3 5.3 collective-permute-done.20
  553.7 5.5 all-to-all-start.5
  564.6 9.2 %all-to-all-done.5 = bf16[8,24,1536]{2,1,0:T(8,128)(2,1)S(1)} async-done(((bf16[8,24,1536]{2,1,0:T(8,128)(2,1)}), bf16[8,24,1536]{2,1,0:T(8,128)(2,1)S(1)}, u32[]{:S(2)}, u32[]{:S(2)}) %all-to-all-start.5) | async-done | bytes 589856 | tf_op jit(solution)/shard_map/all_to_all | solution.py:1084
  (214 shorter events, 145.7 us)
Async XLA Ops:
  7.2 72.7 %all-gather.4.cloned.1.call-start = ((), (), s32[]{:S(2)}) async-start(), calls=%async_computation.7 | async-start | bytes 5068800 | tf_op jit(solution)/shard_map/all_gather | solution.py:1120
  12.7 216.2 %all-gather.6.cloned.1.call-start = ((), (), s32[]{:S(2)}) async-start(), calls=%async_computation.9 | async-start | bytes 11796480 | tf_op jit(solution)/shard_map/all_gather | solution.py:1184
  91.0 20.0 %collective-permute-start = (bf16[256,1536]{1,0:T(8,128)(2,1)}, bf16[256,1536]{1,0:T(8,128)(2,1)S(1)}, u32[]{:S(2)}, u32[]{:S(2)}) collective-permute-start(bf16[256,1536]{1,0:T(8,128)(2,1)} %get-tuple-element.132.kv_ref), channel_id=1, source_target_pairs={{0,2},{2,4},{4,6},{6,7},{7,5},{5,3},{3,1},{1,0},{8,10},{10,12},{12... | collective-permute-start | bytes 2359304 | tf_op jit(solution)/shard_map/ppermute | solution.py:1062
  92.3 19.8 %collective-permute-start.1 = (bf16[256,1536]{1,0:T(8,128)(2,1)}, bf16[256,1536]{1,0:T(8,128)(2,1)}, u32[]{:S(2)}, u32[]{:S(2)}) collective-permute-start(bf16[256,1536]{1,0:T(8,128)(2,1)} %get-tuple-element.132.kv_ref), channel_id=1, source_target_pairs={{0,1},{2,0},{4,2},{6,4},{7,6},{5,7},{3,5},{1,3},{8,9},{10,8},{12,1... | collective-permute-start | bytes 2359304 | tf_op jit(solution)/shard_map/ppermute | solution.py:1062
  97.9 75.5 %copy-start.13 = (bf16[768,128]{1,0:T(8,128)(2,1)}, bf16[768,128]{1,0:T(8,128)(2,1)S(1)}, u32[]{:S(2)}) copy-start(bf16[768,128]{1,0:T(8,128)(2,1)S(1)} %slice.96.sw_ref) | copy-start | bytes 589828
  112.1 18.7 %collective-permute-start.2 = (bf16[256,1536]{1,0:T(8,128)(2,1)S(1)}, bf16[256,1536]{1,0:T(8,128)(2,1)}, u32[]{:S(2)}, u32[]{:S(2)}) collective-permute-start(bf16[256,1536]{1,0:T(8,128)(2,1)S(1)} %collective-permute-done.refs_0_.refs_1_), channel_id=1, source_target_pairs={{0,2},{2,4},{4,6},{6,7},{7,5},{5,3},{3,1},{1,0},{8,10},{10,12},{12... | collective-permute-start | bytes 2359304 | tf_op jit(solution)/shard_map/ppermute | solution.py:1062
  112.8 18.6 %collective-permute-start.3 = (bf16[256,1536]{1,0:T(8,128)(2,1)}, bf16[256,1536]{1,0:T(8,128)(2,1)}, u32[]{:S(2)}, u32[]{:S(2)}) collective-permute-start(bf16[256,1536]{1,0:T(8,128)(2,1)} %collective-permute-done.1.refs_1_.refs_0_), channel_id=1, source_target_pairs={{0,1},{2,0},{4,2},{6,4},{7,6},{5,7},{3,5},{1,3},{8,9},{10,8},{12,1... | collective-permute-start | bytes 2359304 | tf_op jit(solution)/shard_map/ppermute | solution.py:1062
  131.4 17.7 %collective-permute-start.4 = (bf16[256,1536]{1,0:T(8,128)(2,1)}, bf16[256,1536]{1,0:T(8,128)(2,1)}, u32[]{:S(2)}, u32[]{:S(2)}) collective-permute-start(bf16[256,1536]{1,0:T(8,128)(2,1)} %collective-permute-done.2.refs_0_.refs_1_), channel_id=1, source_target_pairs={{0,2},{2,4},{4,6},{6,7},{7,5},{5,3},{3,1},{1,0},{8,10},{10,12},{12... | collective-permute-start | bytes 2359304 | tf_op jit(solution)/shard_map/ppermute | solution.py:1062
  132.0 17.5 %collective-permute-start.5 = (bf16[256,1536]{1,0:T(8,128)(2,1)}, bf16[256,1536]{1,0:T(8,128)(2,1)}, u32[]{:S(2)}, u32[]{:S(2)}) collective-permute-start(bf16[256,1536]{1,0:T(8,128)(2,1)} %collective-permute-done.3.refs_1_.refs_0_), channel_id=1, source_target_pairs={{0,1},{2,0},{4,2},{6,4},{7,6},{5,7},{3,5},{1,3},{8,9},{10,8},{12,1... | collective-permute-start | bytes 2359304 | tf_op jit(solution)/shard_map/ppermute | solution.py:1062
  151.2 14.6 %collective-permute-start.6 = (bf16[256,768]{1,0:T(8,128)(2,1)}, bf16[256,768]{1,0:T(8,128)(2,1)}, u32[]{:S(2)}, u32[]{:S(2)}) collective-permute-start(bf16[256,768]{1,0:T(8,128)(2,1)} %slice.76), channel_id=1, source_target_pairs={{0,2},{2,4},{4,6},{6,7},{7,5},{5,3},{3,1},{1,0},{8,10},{10,12},{12... | collective-permute-start | bytes 1179656 | tf_op jit(solution)/shard_map/ppermute | solution.py:1062
  154.4 11.5 %collective-permute-start.7 = (bf16[256,768]{1,0:T(8,128)(2,1)}, bf16[256,768]{1,0:T(8,128)(2,1)}, u32[]{:S(2)}, u32[]{:S(2)}) collective-permute-start(bf16[256,768]{1,0:T(8,128)(2,1)} %slice.77), channel_id=1, source_target_pairs={{0,1},{2,0},{4,2},{6,4},{7,6},{5,7},{3,5},{1,3},{8,9},{10,8},{12,1... | collective-permute-start | bytes 1179656 | tf_op jit(solution)/shard_map/ppermute | solution.py:1062
  184.3 40.3 %all-to-all-start = ((bf16[8,128,768]{2,1,0:T(8,128)(2,1)}), bf16[8,128,768]{2,1,0:T(8,128)(2,1)}, u32[]{:S(2)}, u32[]{:S(2)}) async-start(bf16[8,128,768]{2,1,0:T(8,128)(2,1)} %bitcast.83), calls=%async_computation | async-start | bytes 3145728 | tf_op jit(solution)/shard_map/all_to_all | solution.py:1154
  224.6 40.3 %all-to-all-start.1 = ((bf16[8,128,768]{2,1,0:T(8,128)(2,1)}), bf16[8,128,768]{2,1,0:T(8,128)(2,1)}, u32[]{:S(2)}, u32[]{:S(2)}) async-start(bf16[8,128,768]{2,1,0:T(8,128)(2,1)} %bitcast.92), calls=%async_computation.1 | async-start | bytes 3145728 | tf_op jit(solution)/shard_map/all_to_all | solution.py:1154
  264.9 40.7 %all-to-all-start.2 = ((bf16[8,128,768]{2,1,0:T(8,128)(2,1)}), bf16[8,128,768]{2,1,0:T(8,128)(2,1)}, u32[]{:S(2)}, u32[]{:S(2)}) async-start(bf16[8,128,768]{2,1,0:T(8,128)(2,1)} %bitcast.91), calls=%async_computation.2 | async-start | bytes 3145728 | tf_op jit(solution)/shard_map/all_to_all | solution.py:1154
  269.2 274.2 %reduce-scatter.2.cloned.1.call-start = ((), (), s32[]{:S(2)}) async-start(), calls=%async_computation.8 | async-start | bytes 11796480 | tf_op jit(solution)/shard_map/reduce_scatter | solution.py:1224
  335.2 41.0 %all-to-all-start.3 = ((bf16[8,128,768]{2,1,0:T(8,128)(2,1)}), bf16[8,128,768]{2,1,0:T(8,128)(2,1)S(1)}, u32[]{:S(2)}, u32[]{:S(2)}) async-start(bf16[8,128,768]{2,1,0:T(8,128)(2,1)} %bitcast.89), calls=%async_computation.3 | async-start | bytes 3145728 | tf_op jit(solution)/shard_map/all_to_all | solution.py:1154
  393.3 21.6 %collective-permute-start.10 = (bf16[2,192,896]{2,1,0:T(8,128)(2,1)S(1)}, bf16[2,192,896]{2,1,0:T(8,128)(2,1)S(1)}, u32[]{:S(2)}, u32[]{:S(2)}) collective-permute-start(bf16[2,192,896]{2,1,0:T(8,128)(2,1)S(1)} %fusion.4), channel_id=1, source_target_pairs={{0,8},{8,0},{16,24},{24,16},{1,9},{9,1},{17,25},{25,17},{2,10},{10... | collective-permute-start | bytes 2064392 | tf_op jit(solution)/shard_map/ppermute | solution.py:1070
  401.7 13.1 %collective-permute-start.8 = (bf16[256,768]{1,0:T(8,128)(2,1)}, bf16[256,768]{1,0:T(8,128)(2,1)}, u32[]{:S(2)}, u32[]{:S(2)}) collective-permute-start(bf16[256,768]{1,0:T(8,128)(2,1)} %get-tuple-element.176), channel_id=1, source_target_pairs={{0,2},{2,4},{4,6},{6,7},{7,5},{5,3},{3,1},{1,0},{8,10},{10,12},{12... | collective-permute-start | bytes 1179656 | tf_op jit(solution)/shard_map/ppermute | solution.py:1062
  401.8 13.0 %collective-permute-start.9 = (bf16[256,768]{1,0:T(8,128)(2,1)}, bf16[256,768]{1,0:T(8,128)(2,1)}, u32[]{:S(2)}, u32[]{:S(2)}) collective-permute-start(bf16[256,768]{1,0:T(8,128)(2,1)} %get-tuple-element.177), channel_id=1, source_target_pairs={{0,1},{2,0},{4,2},{6,4},{7,6},{5,7},{3,5},{1,3},{8,9},{10,8},{12,1... | collective-permute-start | bytes 1179656 | tf_op jit(solution)/shard_map/ppermute | solution.py:1062
  417.6 19.7 %collective-permute-start.11 = (bf16[256,1536]{1,0:T(8,128)(2,1)}, bf16[256,1536]{1,0:T(8,128)(2,1)}, u32[]{:S(2)}, u32[]{:S(2)}) collective-permute-start(bf16[256,1536]{1,0:T(8,128)(2,1)} %get-tuple-element.189), channel_id=1, source_target_pairs={{0,2},{2,4},{4,6},{6,7},{7,5},{5,3},{3,1},{1,0},{8,10},{10,12},{12... | collective-permute-start | bytes 2359304 | tf_op jit(solution)/shard_map/ppermute | solution.py:1062
  418.8 20.5 %collective-permute-start.12 = (bf16[256,1536]{1,0:T(8,128)(2,1)}, bf16[256,1536]{1,0:T(8,128)(2,1)}, u32[]{:S(2)}, u32[]{:S(2)}) collective-permute-start(bf16[256,1536]{1,0:T(8,128)(2,1)} %get-tuple-element.190), channel_id=1, source_target_pairs={{0,1},{2,0},{4,2},{6,4},{7,6},{5,7},{3,5},{1,3},{8,9},{10,8},{12,1... | collective-permute-start | bytes 2359304 | tf_op jit(solution)/shard_map/ppermute | solution.py:1062
  420.9 11.7 %collective-permute-start.13 = (bf16[192,896]{1,0:T(8,128)(2,1)S(1)}, bf16[192,896]{1,0:T(8,128)(2,1)S(1)}, u32[]{:S(2)}, u32[]{:S(2)}) collective-permute-start(bf16[192,896]{1,0:T(8,128)(2,1)S(1)} %fusion.6), channel_id=1, source_target_pairs={{0,16},{16,0},{8,24},{24,8},{1,17},{17,1},{9,25},{25,9},{2,18},{18... | collective-permute-start | bytes 1032200 | tf_op jit(solution)/shard_map/ppermute | solution.py:1078
  442.2 19.5 %collective-permute-start.14 = (bf16[256,1536]{1,0:T(8,128)(2,1)}, bf16[256,1536]{1,0:T(8,128)(2,1)S(1)}, u32[]{:S(2)}, u32[]{:S(2)}) collective-permute-start(bf16[256,1536]{1,0:T(8,128)(2,1)} %get-tuple-element.200), channel_id=1, source_target_pairs={{0,2},{2,4},{4,6},{6,7},{7,5},{5,3},{3,1},{1,0},{8,10},{10,12},{12... | collective-permute-start | bytes 2359304 | tf_op jit(solution)/shard_map/ppermute | solution.py:1062
  445.4 18.4 %collective-permute-start.15 = (bf16[256,1536]{1,0:T(8,128)(2,1)}, bf16[256,1536]{1,0:T(8,128)(2,1)S(1)}, u32[]{:S(2)}, u32[]{:S(2)}) collective-permute-start(bf16[256,1536]{1,0:T(8,128)(2,1)} %get-tuple-element.201), channel_id=1, source_target_pairs={{0,1},{2,0},{4,2},{6,4},{7,6},{5,7},{3,5},{1,3},{8,9},{10,8},{12,1... | collective-permute-start | bytes 2359304 | tf_op jit(solution)/shard_map/ppermute | solution.py:1062
  486.0 2.2 collective-permute-start.16
  486.0 20.2 %collective-permute-start.17 = (bf16[256,1536]{1,0:T(8,128)(2,1)}, bf16[256,1536]{1,0:T(8,128)(2,1)S(1)}, u32[]{:S(2)}, u32[]{:S(2)}) collective-permute-start(bf16[256,1536]{1,0:T(8,128)(2,1)} %get-tuple-element.222), channel_id=1, source_target_pairs={{0,2},{2,4},{4,6},{6,7},{7,5},{5,3},{3,1},{1,0},{8,10},{10,12},{12... | collective-permute-start | bytes 2359304 | tf_op jit(solution)/shard_map/ppermute | solution.py:1062
  487.6 19.8 %collective-permute-start.18 = (bf16[256,1536]{1,0:T(8,128)(2,1)}, bf16[256,1536]{1,0:T(8,128)(2,1)S(1)}, u32[]{:S(2)}, u32[]{:S(2)}) collective-permute-start(bf16[256,1536]{1,0:T(8,128)(2,1)} %get-tuple-element.223), channel_id=1, source_target_pairs={{0,1},{2,0},{4,2},{6,4},{7,6},{5,7},{3,5},{1,3},{8,9},{10,8},{12,1... | collective-permute-start | bytes 2359304 | tf_op jit(solution)/shard_map/ppermute | solution.py:1062
  521.8 3.1 collective-permute-start.19
  522.0 9.5 %collective-permute-start.21 = (bf16[192,768]{1,0:T(8,128)(2,1)S(1)}, bf16[192,768]{1,0:T(8,128)(2,1)S(1)}, u32[]{:S(2)}, u32[]{:S(2)}) collective-permute-start(bf16[192,768]{1,0:T(8,128)(2,1)S(1)} %fusion.7), channel_id=1, source_target_pairs={{0,16},{16,0},{8,24},{24,8},{1,17},{17,1},{9,25},{25,9},{2,18},{18... | collective-permute-start | bytes 884744 | tf_op jit(solution)/shard_map/ppermute | solution.py:1078
  532.5 21.2 %all-to-all-start.4 = ((bf16[8,24,1664]{2,1,0:T(8,128)(2,1)}), bf16[8,24,1664]{2,1,0:T(8,128)(2,1)}, u32[]{:S(2)}, u32[]{:S(2)}) async-start(bf16[8,24,1664]{2,1,0:T(8,128)(2,1)} %fusion.1), calls=%async_computation.5 | async-start | bytes 1277952 | tf_op jit(solution)/shard_map/all_to_all | solution.py:1084
  537.6 15.1 %collective-permute-start.20 = (bf16[192,1536]{1,0:T(8,128)(2,1)}, bf16[192,1536]{1,0:T(8,128)(2,1)S(1)}, u32[]{:S(2)}, u32[]{:S(2)}) collective-permute-start(bf16[192,1536]{1,0:T(8,128)(2,1)} %fusion.5), channel_id=1, source_target_pairs={{0,16},{16,0},{8,24},{24,8},{1,17},{17,1},{9,25},{25,9},{2,18},{18... | collective-permute-start | bytes 1769480 | tf_op jit(solution)/shard_map/ppermute | solution.py:1078
  553.7 20.2 %all-to-all-start.5 = ((bf16[8,24,1536]{2,1,0:T(8,128)(2,1)}), bf16[8,24,1536]{2,1,0:T(8,128)(2,1)S(1)}, u32[]{:S(2)}, u32[]{:S(2)}) async-start(bf16[8,24,1536]{2,1,0:T(8,128)(2,1)} %bitcast.50), calls=%async_computation.6 | async-start | bytes 1179648 | tf_op jit(solution)/shard_map/all_to_all | solution.py:1084
  (38 other events, 253.4 us)
Sparse Core Ops, SparseCore 0:
  12.8 67.0 all-gather.3
  81.5 62.5 all-gather.5
  335.4 76.0 reduce-scatter.1

commit v6 on v4

--- a/solution.py
+++ b/solution.py
@@ -23,8 +23,7 @@
 F32 = jnp.float32
 BF16 = jnp.bfloat16
 ALL_AXES = ("dp", "expert")
-VMEM_SMALL = 24 * 1024 * 1024
-VMEM_LARGE = 44 * 1024 * 1024
+VMEM_LIMIT = 60 * 1024 * 1024
 
 
 def dot(a, b):
@@ -40,7 +39,7 @@
     return hi, (v - hi.astype(F32)).astype(BF16)
 
 
-def params(cost=None, limit=VMEM_SMALL):
+def params(cost=None, limit=VMEM_LIMIT):
     return dict(
         compiler_params=pltpu.CompilerParams(vmem_limit_bytes=limit),
         cost_estimate=None if cost is None else pl.CostEstimate(
@@ -665,7 +664,7 @@
         out_shape=[shape((rows, D), BF16)] + [shape((rows, wide), F32)] * 2,
         scratch_shapes=[pltpu.VMEM((rows, D), F32)],
         name="expert_forward",
-        **params((6 * rows * D * wide, 6 * D * wide), VMEM_LARGE),
+        **params((6 * rows * D * wide, 6 * D * wide)),
     )(xr, w)
 
 
@@ -715,7 +714,7 @@
         out_shape=[shape((rows, D), BF16)] + [shape((rows, wide), BF16)] * 3,
         scratch_shapes=[pltpu.VMEM((rows, D), F32)],
         name="expert_back_in",
-        **params((6 * rows * D * wide, 12 * D * wide), VMEM_LARGE),
+        **params((6 * rows * D * wide, 12 * D * wide)),
     )(gate, up, gr, w)
 
 
@@ -745,7 +744,7 @@
         out_shape=shape(dims, BF16),
         scratch_shapes=[pltpu.VMEM((D, rows), BF16), pltpu.VMEM((D, rows), BF16)],
         name="expert_weight_grads",
-        **params((6 * rows * D * wide, 12 * D * wide), VMEM_LARGE),
+        **params((6 * rows * D * wide, 12 * D * wide)),
     )(xr, low, act, d_gate, d_up)
 
 
@@ -1236,18 +1235,18 @@
         hidden, g, gn, target_cols, in_back, rows_two, pack, att
     )
 
-    early = jnp.concatenate(
-        [grad_ow, grad_small[:, :19], jnp.transpose(gg_two[0:1]), jnp.zeros((D, LANES - 20), F32)],
-        axis=1,
-    )
+    def early_rows(grad_ow, grad_small, gg_two):
+        return jnp.concatenate(
+            [
+                grad_ow, grad_small[:, :19], jnp.transpose(gg_two[0:1]),
+                jnp.zeros((D, LANES - 20), F32),
+            ],
+            axis=1,
+        )
+
+    early = (grad_ow, grad_small, gg_two)
     back = (sc, q_t, q, d_att_t, d_att)
     if ring:
-        parts = early.reshape(2, 2, D // 4, D + LANES)
-        core = lax.axis_index("dp") % 2
-        early_keep = lax.dynamic_index_in_dim(parts, core, 1, keepdims=False)
-        early_got = swap_core(
-            lax.dynamic_index_in_dim(parts, 1 - core, 1, keepdims=False).astype(BF16)
-        )
         dq_t, send_r, send_l, st = bwd_remote(
             *back, st, att_t, far, (4,), halves=True, first=True, dtype=BF16
         )
@@ -1256,12 +1255,24 @@
             dq_t, part_r, part_l = bwd_remote(
                 *back, st, dq_t, (left[i], right[i]), (i, 8 - i), dtype=BF16
             )
-            got_r, got_l, part_r, part_l, dq_t, early_got = tie(
-                got_r, got_l, part_r, part_l, dq_t, early_got
+            got_r, got_l, part_r, part_l, dq_t, early = tie(
+                got_r, got_l, part_r, part_l, dq_t, early
             )
             send_r, send_l = ring_add(part_r, got_r, part_l, got_l)
             if i == 3:
-                early_keep, early_got = add_and_cross(early_keep, early_got)
+                send_r, early = tie(send_r, early)
+                parts = early_rows(*early).reshape(2, 2, D // 4, D + LANES)
+                core = lax.axis_index("dp") % 2
+                early_keep = lax.dynamic_index_in_dim(parts, core, 1, keepdims=False)
+                early_send = lax.dynamic_index_in_dim(parts, 1 - core, 1, keepdims=False)
+                dq_t, early_send = tie(dq_t, early_send.astype(BF16))
+                early = swap_core(early_send)
+            elif i == 2:
+                send_r, early = tie(send_r, early)
+                early_keep, early_got = add_and_cross(early_keep, early)
+                dq_t, early_keep = tie(dq_t, early_keep)
+                early = early_got
+        early_got = early
         send_r, send_l, dq_t = tie(send_r, send_l, dq_t)
         got_r = along_ring(send_r, 1)
         got_l = along_ring(send_l, -1)
@@ -1273,7 +1284,7 @@
         )
         dq, dkv_own, dkv_cont = bwd_local(*back, st, dq_t, kv_prompt, kv_own)
         got = (lax.psum_scatter(dkv_all, "expert", scatter_dimension=0, tiled=True),)
-        early = scatter_all(early)
+        early = scatter_all(early_rows(*early))
     if per_cont > 1:
         dkv_cont = lax.psum_scatter(
             dkv_cont, "expert", scatter_dimension=0, tiled=True, axis_index_groups=cont_groups
@@ -1281,14 +1292,13 @@
     gn_q, *grad_q = q_back_call(sc, low_one_t, dq, cosine, sine, pack, ring)
     if ring:
         got_q = swap_core(grad_q[0])
-        keep_q, got_q = add_and_cross(grad_q[1], got_q)
-        keep_q, *got = tie(keep_q, *got)
     grad_input, *grad_kv = kv_back_call(
         sc, x, low_one_t, gn_q, gh, gain_one, cosine, sine, pack, dkv_own, dkv_cont, got, ring
     )
     output, grad_input = from_rows(output), from_rows(grad_input)
     if ring:
         got_kv = swap_core(grad_kv[0])
+        keep_q, got_q = add_and_cross(grad_q[1], got_q)
         keep_kv, got_kv = add_and_cross(grad_kv[1], got_kv)
         keep_kv, got_q, early_got = tie(keep_kv, got_q, early_got)
         got_q = add_and_scatter(

time: 603 us -> 575 us (0.954)
  local copies, waits for them, and re-layouts: 91.5 us -> 38.6 us
  Pallas kernels: 198 us -> 237 us
  waiting for transfers between devices: 222 us -> 207 us
    unnamed x179 -> x71, local copies, waits for them, and re-layouts: 65.8 us -> 14 us
    ppermute x16, waiting for transfers between devices: 47.9 us -> 29.3 us  [along_ring(): return lax.ppermute(array, 'expert', pairs)]
    pallas_call x3, Pallas kernels: 2.02 us -> 8.24 us  [ring_add(): pl.pallas_call(functools.partial(ring_add_body, half), grid=(2,), in_spec...]
  transfers between devices with their start and end apart: 31 -> 31, of which waited for: 23 -> 20; matrix products, arithmetic and copies ran while one was open for 7% -> 8% of each run, Pallas kernels for 29% -> 37%
where the time goes in v6:
time: 575 us; the launch traced here: 566 us
  Pallas kernels  237 us (41%)
  waiting for transfers between devices  207 us (36%)
  starting transfers between devices  47.8 us (8%)
  local copies, waits for them, and re-layouts  38.6 us (7%)
  other arithmetic  20.2 us (4%)
  between operations  14.5 us (3%)
    all_to_all x4, waiting for transfers between devices, exchange(): lax.all_to_all(rows, 'expert', split_axis=0, concat_axis=0, tiled=True)  94.6 us
    all_gather x1, waiting for transfers between devices, per_device(): lax.all_gather(jnp.concatenate([qkv_weight, out_weight, small], axis=1),...  58.7 us
    pallas_call x4, Pallas kernels, bwd_remote(): pl.pallas_call(functools.partial(bwd_remote_body, tuple(offsets), len(kvs...  41 us
    pallas_call x4, Pallas kernels, fwd_remote(): pl.pallas_call(functools.partial(fwd_remote_body, tuple(offsets), len(kvs...  38.1 us
    ppermute x16, waiting for transfers between devices, along_ring(): return lax.ppermute(array, 'expert', pairs)  29.3 us
    pallas_call x1, Pallas kernels, expert_in(): pl.pallas_call(expert_in_body, grid=(wide // part,), in_specs=[tile, tile...  23.7 us
    pallas_call x1, Pallas kernels, expert_fwd(): pl.pallas_call(expert_fwd_body, grid=(wide // part,), in_specs=[whole((ro...  19.1 us
    ppermute x16, starting transfers between devices, along_ring(): return lax.ppermute(array, 'expert', pairs)  18.5 us
  transfers between devices with their start and end apart: 31, of which 20 were waited for; matrix products, arithmetic and copies ran while one was open for 8% of the time, Pallas kernels for 37%

profile of v6, /device:TPU:0, one launch (start us, length us, event | category | flops | bytes accessed | tf_op | source)
XLA Modules:
  0.0 565.6 jit_solution(3680523082470518016)
XLA Ops:
  21.2 58.7 %all-gather.4.cloned.1.call-done.wq_ref.wk_ref.wv_ref.ow_ref.sw_ref.w_ref = bf16[768,3200]{1,0:T(8,128)(2,1)} async-done(((bf16[24,3200]{1,0:T(8,128)(2,1)}), bf16[768,3200]{1,0:T(8,128)(2,1)}) %all-gather.4.cloned.1.call-update) | async-done | bytes 4915216 | tf_op jit(solution)/shard_map/all_gather | solution.py:1127
  82.0 9.0 %qkv_rope.1 = (bf16[512,768]{1,0:T(8,128)(2,1)}, bf16[512,768]{1,0:T(8,128)(2,1)}, bf16[768,512]{1,0:T(8,128)(2,1)}, bf16[256,1536]{1,0:T(8,128)(2,1)}, bf16[256,1536]{1,0:T(8,128)(2,1)}) custom-call(bf16[512,768]{1,0:T(8,128)(2,1)} %bitcast.70, f32[1,768]{1,0:T(1,128)} %copy.137.gain_ref, ...), custom_call_target="tpu_custom_call" | custom-call | flops 1811939328 | bytes 3538944 | tf_op jit(solution)/shard_map/qkv_rope/pallas_call | solution.py:99
  95.6 9.9 %attend_local.1 = (f32[48,512]{1,0:T(8,128)}, f32[768,512]{1,0:T(8,128)}) custom-call(s32[12]{0:T(128)} %concatenate.51.sc_ref, bf16[768,512]{1,0:T(8,128)(2,1)} %get-tuple-element.133.qt_ref, bf16[256,1536]{1,0:T(8,128)(2,1)} %get-tuple-element.135.kv_ref, bf16[256,1536]{1,0:T(8,128)(2,1)} %get-tuple-element.136.kvo_ref), custom_call_target="tpu_custom_call" | custom-call | flops 1610612736 | bytes 1572864 | tf_op jit(solution)/shard_map/attend_local/pallas_call | solution.py:261
  105.5 5.4 collective-permute-done.1.refs_1_.refs_0_
  114.1 10.2 %attend_remote.4 = (f32[48,512]{1,0:T(8,128)}, f32[768,512]{1,0:T(8,128)}) custom-call(s32[12]{0:T(128)} %concatenate.51.sc_ref, bf16[768,512]{1,0:T(8,128)(2,1)} %get-tuple-element.133.qt_ref, bf16[256,1536]{1,0:T(8,128)(2,1)} %copy-done.29, bf16[256,1536]{1,0:T(8,128)(2,1)} %copy-done.28, f32[48,512]{1,0:T(8,128)} %get-tuple-element.140.refs_2_, ...), custom_call_target="tpu_custom_call" | custom-call | flops 3221225472 | bytes 4718592 | tf_op jit(solution)/shard_map/attend_remote/pallas_call | solution.py:285
  124.3 6.6 %collective-permute-done.2.refs_0_.refs_1_ = bf16[256,1536]{1,0:T(8,128)(2,1)} collective-permute-done((bf16[256,1536]{1,0:T(8,128)(2,1)S(1)}, bf16[256,1536]{1,0:T(8,128)(2,1)}, u32[]{:S(2)}, u32[]{:S(2)}) %collective-permute-start.2) | collective-permute-done | bytes 786464 | tf_op jit(solution)/shard_map/ppermute | solution.py:1069
  134.2 10.2 %attend_remote.5 = (f32[48,512]{1,0:T(8,128)}, f32[768,512]{1,0:T(8,128)}) custom-call(s32[12]{0:T(128)} %concatenate.51.sc_ref, bf16[768,512]{1,0:T(8,128)(2,1)} %get-tuple-element.133.qt_ref, bf16[256,1536]{1,0:T(8,128)(2,1)} %collective-permute-done.2.refs_0_.refs_1_, bf16[256,1536]{1,0:T(8,128)(2,1)} %collective-permute-done.3.refs_1_.refs_0_, ...), custom_call_target="tpu_custom_call" | custom-call | flops 3221225472 | bytes 4718592 | tf_op jit(solution)/shard_map/attend_remote/pallas_call | solution.py:285
  156.6 10.2 %attend_remote.6 = (f32[48,512]{1,0:T(8,128)}, f32[768,512]{1,0:T(8,128)}) custom-call(s32[12]{0:T(128)} %concatenate.51.sc_ref, bf16[768,512]{1,0:T(8,128)(2,1)} %get-tuple-element.133.qt_ref, bf16[256,1536]{1,0:T(8,128)(2,1)} %copy-done.22, bf16[256,1536]{1,0:T(8,128)(2,1)} %copy-done.23, f32[48,512]{1,0:T(8,128)} %get-tuple-element.150.refs_2_, ...), custom_call_target="tpu_custom_call" | custom-call | flops 3221225472 | bytes 4718592 | tf_op jit(solution)/shard_map/attend_remote/pallas_call | solution.py:285
  166.8 7.5 %attend_remote.7 = (f32[48,512]{1,0:T(8,128)}, f32[768,512]{1,0:T(8,128)}, bf16[512,768]{1,0:T(8,128)(2,1)}) custom-call(s32[12]{0:T(128)} %concatenate.51.sc_ref, bf16[768,512]{1,0:T(8,128)(2,1)} %get-tuple-element.133.qt_ref, bf16[256,768]{1,0:T(8,128)(2,1)} %collective-permute-done.6.refs_0_, bf16[256,768]{1,0:T(8,128)(2,1)} %collective-permute-done.7.refs_1_, ...), custom_call_target="tpu_custom_call" | custom-call | flops 1610612736 | bytes 3932160 | tf_op jit(solution)/shard_map/attend_remote/pallas_call | solution.py:285
  174.3 9.4 %route_dispatch.1 = (f32[512,768]{1,0:T(8,128)}, bf16[512,768]{1,0:T(8,128)(2,1)}, f32[512,128]{1,0:T(8,128)}, bf16[1024,768]{1,0:T(8,128)(2,1)}) custom-call(bf16[512,768]{1,0:T(8,128)(2,1)} %bitcast.71, bf16[512,768]{1,0:T(8,128)(2,1)} %get-tuple-element.154.att_ref, ...), custom_call_target="tpu_custom_call" | custom-call | flops 1409286144 | bytes 3145728 | tf_op jit(solution)/shard_map/route_dispatch/pallas_call | solution.py:608
  183.7 5.8 %all-to-all-start = ((bf16[8,128,768]{2,1,0:T(8,128)(2,1)}), bf16[8,128,768]{2,1,0:T(8,128)(2,1)S(1)}, u32[]{:S(2)}, u32[]{:S(2)}) async-start(bf16[8,128,768]{2,1,0:T(8,128)(2,1)} %bitcast.96), calls=%async_computation | async-start | bytes 3145728 | tf_op jit(solution)/shard_map/all_to_all | solution.py:1161
  195.3 28.0 %all-to-all-done = bf16[8,128,768]{2,1,0:T(8,128)(2,1)S(1)} async-done(((bf16[8,128,768]{2,1,0:T(8,128)(2,1)}), bf16[8,128,768]{2,1,0:T(8,128)(2,1)S(1)}, u32[]{:S(2)}, u32[]{:S(2)}) %all-to-all-start) | async-done | bytes 1572896 | tf_op jit(solution)/shard_map/all_to_all | solution.py:1161
  228.1 19.1 %expert_forward.1 = (bf16[1024,768]{1,0:T(8,128)(2,1)}, f32[1024,2048]{1,0:T(8,128)}, f32[1024,2048]{1,0:T(8,128)}) custom-call(bf16[1024,768]{1,0:T(8,128)(2,1)} %bitcast.89, bf16[4,3,192,2048]{3,2,1,0:T(8,128)(2,1)} %bitcast.117), custom_call_target="tpu_custom_call" | custom-call | flops 9663676416 | bytes 9437184 | tf_op jit(solution)/shard_map/expert_forward/pallas_call | solution.py:659
  247.2 17.4 %all-to-all-done.1 = bf16[8,128,768]{2,1,0:T(8,128)(2,1)S(1)} async-done(((bf16[8,128,768]{2,1,0:T(8,128)(2,1)}), bf16[8,128,768]{2,1,0:T(8,128)(2,1)S(1)}, u32[]{:S(2)}, u32[]{:S(2)}) %all-to-all-start.1) | async-done | bytes 1572896 | tf_op jit(solution)/shard_map/all_to_all | solution.py:1161
  270.8 23.7 %expert_back_in.1 = (bf16[1024,768]{1,0:T(8,128)(2,1)}, bf16[1024,2048]{1,0:T(8,128)(2,1)}, bf16[1024,2048]{1,0:T(8,128)(2,1)}, bf16[1024,2048]{1,0:T(8,128)(2,1)}) custom-call(f32[1024,2048]{1,0:T(8,128)} %get-tuple-element.159.gate_ref, f32[1024,2048]{1,0:T(8,128)} %get-tuple-element.160.up_ref, bf16[1024,768]{1,0:T(8,128)(2,1)} %bitcast.92, ...), custom_call_target="tpu_custom_call" | custom-call | flops 9663676416 | bytes 18874368 | tf_op jit(solution)/shard_map/expert_back_in/pallas_call | solution.py:709
  294.5 12.1 %all-to-all-done.2 = bf16[8,128,768]{2,1,0:T(8,128)(2,1)S(1)} async-done(((bf16[8,128,768]{2,1,0:T(8,128)(2,1)}), bf16[8,128,768]{2,1,0:T(8,128)(2,1)S(1)}, u32[]{:S(2)}, u32[]{:S(2)}) %all-to-all-start.2) | async-done | bytes 1572896 | tf_op jit(solution)/shard_map/all_to_all | solution.py:1161
  307.7 12.3 %mixture.1 = (bf16[512,768]{1,0:T(8,128)(2,1)}, f32[512,768]{1,0:T(8,128)}, f32[512,128]{1,0:T(8,128)}, f32[768,128]{1,0:T(8,128)}) custom-call(f32[512,768]{1,0:T(8,128)} %get-tuple-element.155.h_ref, bf16[512,768]{1,0:T(8,128)(2,1)} %bitcast.76, f32[512,128]{1,0:T(8,128)} %get-tuple-element.157.pr_ref, s32[512,2]{1,0:T(8,128)} %bitcast.80, ...), custom_call_target="tpu_custom_call" | custom-call | flops 1610612736 | bytes 4718592 | tf_op jit(solution)/shard_map/mixture/pallas_call | solution.py:826
  320.1 17.3 %expert_weight_grads.1 = bf16[4,3,192,2048]{3,2,1,0:T(8,128)(2,1)} custom-call(bf16[1024,768]{1,0:T(8,128)(2,1)} %bitcast.90, bf16[1024,768]{1,0:T(8,128)(2,1)} %bitcast.93, bf16[1024,2048]{1,0:T(8,128)(2,1)} %get-tuple-element.234.act_ref, bf16[1024,2048]{1,0:T(8,128)(2,1)} %get-tuple-element.235.dg_ref, bf16[1024,2048]{1,0:T(8,128)(2,1)} %get-tuple-element.236.du_ref), custom_call_target="tpu_custom_call" | custom-call | flops 9663676416 | bytes 18874368 | tf_op jit(solution)/shard_map/expert_weight_grads/pallas_call | solution.py:739
  341.1 37.1 %all-to-all-done.3 = bf16[8,128,768]{2,1,0:T(8,128)(2,1)S(1)} async-done(((bf16[8,128,768]{2,1,0:T(8,128)(2,1)}), bf16[8,128,768]{2,1,0:T(8,128)(2,1)S(1)}, u32[]{:S(2)}, u32[]{:S(2)}) %all-to-all-start.3) | async-done | bytes 1572896 | tf_op jit(solution)/shard_map/all_to_all | solution.py:1161
  379.3 8.9 %norm_two_back.1 = (f32[512,768]{1,0:T(8,128)}, bf16[512,768]{1,0:T(8,128)(2,1)}, bf16[768,512]{1,0:T(8,128)(2,1)}, f32[768,768]{1,0:T(8,128)}, f32[8,768]{1,0:T(8,128)}) custom-call(f32[512,768]{1,0:T(8,128)} %get-tuple-element.155.h_ref, bf16[512,768]{1,0:T(8,128)(2,1)} %bitcast.77, f32[512,768]{1,0:T(8,128)} %get-tuple-element.166.gn_ref, ...), custom_call_target="tpu_custom_call" | custom-call | flops 2013265920 | bytes 6291456 | tf_op jit(solution)/shard_map/norm_two_back/pallas_call | solution.py:880
  388.2 8.4 %attend_back_remote.4 = (f32[768,512]{1,0:T(8,128)}, bf16[256,768]{1,0:T(8,128)(2,1)}, bf16[256,768]{1,0:T(8,128)(2,1)}, f32[48,512]{1,0:T(8,128)}) custom-call(s32[12]{0:T(128)} %concatenate.51.sc_ref, bf16[768,512]{1,0:T(8,128)(2,1)} %get-tuple-element.133.qt_ref, bf16[512,768]{1,0:T(8,128)(2,1)} %get-tuple-element.134.q_ref, ...), custom_call_target="tpu_custom_call" | custom-call | flops 4026531840 | bytes 7864320 | tf_op jit(solution)/shard_map/attend_back_remote/pallas_call | solution.py:509
  399.1 10.9 %attend_back_remote.5 = (f32[768,512]{1,0:T(8,128)}, bf16[256,1536]{1,0:T(8,128)(2,1)}, bf16[256,1536]{1,0:T(8,128)(2,1)}) custom-call(s32[12]{0:T(128)} %concatenate.51.sc_ref, bf16[768,512]{1,0:T(8,128)(2,1)} %get-tuple-element.133.qt_ref, bf16[512,768]{1,0:T(8,128)(2,1)} %get-tuple-element.134.q_ref, bf16[768,512]{1,0:T(8,128)(2,1)} %get-tuple-element.168.dot_ref, ...), custom_call_target="tpu_custom_call" | custom-call | flops 8053063680 | bytes 9437184 | tf_op jit(solution)/shard_map/attend_back_remote/pallas_call | solution.py:509
  419.7 10.9 %attend_back_remote.6 = (f32[768,512]{1,0:T(8,128)}, bf16[256,1536]{1,0:T(8,128)(2,1)}, bf16[256,1536]{1,0:T(8,128)(2,1)}) custom-call(s32[12]{0:T(128)} %concatenate.51.sc_ref, bf16[768,512]{1,0:T(8,128)(2,1)} %get-tuple-element.133.qt_ref, bf16[512,768]{1,0:T(8,128)(2,1)} %get-tuple-element.134.q_ref, bf16[768,512]{1,0:T(8,128)(2,1)} %get-tuple-element.168.dot_ref, ...), custom_call_target="tpu_custom_call" | custom-call | flops 8053063680 | bytes 9437184 | tf_op jit(solution)/shard_map/attend_back_remote/pallas_call | solution.py:509
  444.5 10.9 %attend_back_remote.7 = (f32[768,512]{1,0:T(8,128)}, bf16[256,1536]{1,0:T(8,128)(2,1)}, bf16[256,1536]{1,0:T(8,128)(2,1)}) custom-call(s32[12]{0:T(128)} %concatenate.51.sc_ref, bf16[768,512]{1,0:T(8,128)(2,1)} %get-tuple-element.133.qt_ref, bf16[512,768]{1,0:T(8,128)(2,1)} %get-tuple-element.134.q_ref, bf16[768,512]{1,0:T(8,128)(2,1)} %get-tuple-element.168.dot_ref, ...), custom_call_target="tpu_custom_call" | custom-call | flops 8053063680 | bytes 9437184 | tf_op jit(solution)/shard_map/attend_back_remote/pallas_call | solution.py:509
  468.5 11.0 %attend_back_local.1 = (f32[512,768]{1,0:T(8,128)}, f32[256,1536]{1,0:T(8,128)}, f32[256,1536]{1,0:T(8,128)}) custom-call(s32[12]{0:T(128)} %concatenate.51.sc_ref, bf16[768,512]{1,0:T(8,128)(2,1)} %get-tuple-element.133.qt_ref, bf16[512,768]{1,0:T(8,128)(2,1)} %get-tuple-element.134.q_ref, bf16[768,512]{1,0:T(8,128)(2,1)} %get-tuple-element.168.dot_ref, ...), custom_call_target="tpu_custom_call" | custom-call | flops 4026531840 | bytes 6291456 | tf_op jit(solution)/shard_map/attend_back_local/pallas_call | solution.py:480
  479.5 7.5 %q_back.1 = (f32[512,768]{1,0:T(8,128)}, bf16[2,192,768]{2,1,0:T(8,128)(2,1)}, f32[2,192,768]{2,1,0:T(8,128)}) custom-call(s32[12]{0:T(128)} %concatenate.51.sc_ref, bf16[768,512]{1,0:T(8,128)(2,1)} %turn.1.nt_ref, f32[512,768]{1,0:T(8,128)} %get-tuple-element.223.dq_ref, f32[512,128]{1,0:T(8,128)} %pad_maximum_fusion.1.c_ref, ...), custom_call_target="tpu_custom_call" | custom-call | flops 1207959552 | bytes 4718592 | tf_op jit(solution)/shard_map/q_back/pallas_call | solution.py:969
  488.3 13.6 %kv_back.1 = (f32[512,768]{1,0:T(8,128)}, bf16[2,192,1536]{2,1,0:T(8,128)(2,1)}, f32[2,192,1536]{2,1,0:T(8,128)}) custom-call(s32[12]{0:T(128)} %concatenate.51.sc_ref, bf16[512,768]{1,0:T(8,128)(2,1)} %bitcast.72, bf16[768,512]{1,0:T(8,128)(2,1)} %turn.1.nt_ref, f32[512,768]{1,0:T(8,128)} %get-tuple-element.224.gnq_ref, ...), custom_call_target="tpu_custom_call" | custom-call | flops 2415919104 | bytes 9437184 | tf_op jit(solution)/shard_map/kv_back/pallas_call | solution.py:1020
  507.9 7.2 %collective-permute-done.21 = bf16[192,768]{1,0:T(8,128)(2,1)S(1)} collective-permute-done((bf16[192,768]{1,0:T(8,128)(2,1)S(1)}, bf16[192,768]{1,0:T(8,128)(2,1)S(1)}, u32[]{:S(2)}, u32[]{:S(2)}) %collective-permute-start.21) | collective-permute-done | bytes 294944 | tf_op jit(solution)/shard_map/ppermute | solution.py:1085
  516.0 5.1 all-to-all-start.4
  531.6 4.9 collective-permute-done.19
  537.7 5.5 all-to-all-start.5
  548.6 8.7 %all-to-all-done.5 = bf16[8,24,1536]{2,1,0:T(8,128)(2,1)S(1)} async-done(((bf16[8,24,1536]{2,1,0:T(8,128)(2,1)}), bf16[8,24,1536]{2,1,0:T(8,128)(2,1)S(1)}, u32[]{:S(2)}, u32[]{:S(2)}) %all-to-all-start.5) | async-done | bytes 589856 | tf_op jit(solution)/shard_map/all_to_all | solution.py:1091
  (198 shorter events, 127.9 us)
Async XLA Ops:
  7.2 72.7 %all-gather.4.cloned.1.call-start = ((), (), s32[]{:S(2)}) async-start(), calls=%async_computation.7 | async-start | bytes 5068800 | tf_op jit(solution)/shard_map/all_gather | solution.py:1127
  12.7 215.4 %all-gather.6.cloned.1.call-start = ((), (), s32[]{:S(2)}) async-start(), calls=%async_computation.9 | async-start | bytes 11796480 | tf_op jit(solution)/shard_map/all_gather | solution.py:1191
  91.0 20.0 %collective-permute-start.1 = (bf16[256,1536]{1,0:T(8,128)(2,1)}, bf16[256,1536]{1,0:T(8,128)(2,1)S(1)}, u32[]{:S(2)}, u32[]{:S(2)}) collective-permute-start(bf16[256,1536]{1,0:T(8,128)(2,1)} %get-tuple-element.135.kv_ref), channel_id=1, source_target_pairs={{0,1},{2,0},{4,2},{6,4},{7,6},{5,7},{3,5},{1,3},{8,9},{10,8},{12,1... | collective-permute-start | bytes 2359304 | tf_op jit(solution)/shard_map/ppermute | solution.py:1069
  92.4 19.7 %collective-permute-start = (bf16[256,1536]{1,0:T(8,128)(2,1)}, bf16[256,1536]{1,0:T(8,128)(2,1)S(1)}, u32[]{:S(2)}, u32[]{:S(2)}) collective-permute-start(bf16[256,1536]{1,0:T(8,128)(2,1)} %get-tuple-element.135.kv_ref), channel_id=1, source_target_pairs={{0,2},{2,4},{4,6},{6,7},{7,5},{5,3},{3,1},{1,0},{8,10},{10,12},{12... | collective-permute-start | bytes 2359304 | tf_op jit(solution)/shard_map/ppermute | solution.py:1069
  112.1 18.8 %collective-permute-start.2 = (bf16[256,1536]{1,0:T(8,128)(2,1)S(1)}, bf16[256,1536]{1,0:T(8,128)(2,1)}, u32[]{:S(2)}, u32[]{:S(2)}) collective-permute-start(bf16[256,1536]{1,0:T(8,128)(2,1)S(1)} %collective-permute-done.refs_0_.refs_1_), channel_id=1, source_target_pairs={{0,2},{2,4},{4,6},{6,7},{7,5},{5,3},{3,1},{1,0},{8,10},{10,12},{12... | collective-permute-start | bytes 2359304 | tf_op jit(solution)/shard_map/ppermute | solution.py:1069
  112.7 18.5 %collective-permute-start.3 = (bf16[256,1536]{1,0:T(8,128)(2,1)S(1)}, bf16[256,1536]{1,0:T(8,128)(2,1)}, u32[]{:S(2)}, u32[]{:S(2)}) collective-permute-start(bf16[256,1536]{1,0:T(8,128)(2,1)S(1)} %collective-permute-done.1.refs_1_.refs_0_), channel_id=1, source_target_pairs={{0,1},{2,0},{4,2},{6,4},{7,6},{5,7},{3,5},{1,3},{8,9},{10,8},{12,1... | collective-permute-start | bytes 2359304 | tf_op jit(solution)/shard_map/ppermute | solution.py:1069
  131.2 17.8 %collective-permute-start.4 = (bf16[256,1536]{1,0:T(8,128)(2,1)}, bf16[256,1536]{1,0:T(8,128)(2,1)S(1)}, u32[]{:S(2)}, u32[]{:S(2)}) collective-permute-start(bf16[256,1536]{1,0:T(8,128)(2,1)} %collective-permute-done.2.refs_0_.refs_1_), channel_id=1, source_target_pairs={{0,2},{2,4},{4,6},{6,7},{7,5},{5,3},{3,1},{1,0},{8,10},{10,12},{12... | collective-permute-start | bytes 2359304 | tf_op jit(solution)/shard_map/ppermute | solution.py:1069
  132.5 17.5 %collective-permute-start.5 = (bf16[256,1536]{1,0:T(8,128)(2,1)}, bf16[256,1536]{1,0:T(8,128)(2,1)S(1)}, u32[]{:S(2)}, u32[]{:S(2)}) collective-permute-start(bf16[256,1536]{1,0:T(8,128)(2,1)} %collective-permute-done.3.refs_1_.refs_0_), channel_id=1, source_target_pairs={{0,1},{2,0},{4,2},{6,4},{7,6},{5,7},{3,5},{1,3},{8,9},{10,8},{12,1... | collective-permute-start | bytes 2359304 | tf_op jit(solution)/shard_map/ppermute | solution.py:1069
  152.0 14.8 %collective-permute-start.7 = (bf16[256,768]{1,0:T(8,128)(2,1)S(1)}, bf16[256,768]{1,0:T(8,128)(2,1)}, u32[]{:S(2)}, u32[]{:S(2)}) collective-permute-start(bf16[256,768]{1,0:T(8,128)(2,1)S(1)} %slice.71), channel_id=1, source_target_pairs={{0,1},{2,0},{4,2},{6,4},{7,6},{5,7},{3,5},{1,3},{8,9},{10,8},{12,1... | collective-permute-start | bytes 1179656 | tf_op jit(solution)/shard_map/ppermute | solution.py:1069
  152.7 14.1 %collective-permute-start.6 = (bf16[256,768]{1,0:T(8,128)(2,1)S(1)}, bf16[256,768]{1,0:T(8,128)(2,1)}, u32[]{:S(2)}, u32[]{:S(2)}) collective-permute-start(bf16[256,768]{1,0:T(8,128)(2,1)S(1)} %slice.70), channel_id=1, source_target_pairs={{0,2},{2,4},{4,6},{6,7},{7,5},{5,3},{3,1},{1,0},{8,10},{10,12},{12... | collective-permute-start | bytes 1179656 | tf_op jit(solution)/shard_map/ppermute | solution.py:1069
  183.7 39.6 %all-to-all-start = ((bf16[8,128,768]{2,1,0:T(8,128)(2,1)}), bf16[8,128,768]{2,1,0:T(8,128)(2,1)S(1)}, u32[]{:S(2)}, u32[]{:S(2)}) async-start(bf16[8,128,768]{2,1,0:T(8,128)(2,1)} %bitcast.96), calls=%async_computation | async-start | bytes 3145728 | tf_op jit(solution)/shard_map/all_to_all | solution.py:1161
  224.5 40.1 %all-to-all-start.1 = ((bf16[8,128,768]{2,1,0:T(8,128)(2,1)}), bf16[8,128,768]{2,1,0:T(8,128)(2,1)S(1)}, u32[]{:S(2)}, u32[]{:S(2)}) async-start(bf16[8,128,768]{2,1,0:T(8,128)(2,1)} %bitcast.95), calls=%async_computation.1 | async-start | bytes 3145728 | tf_op jit(solution)/shard_map/all_to_all | solution.py:1161
  265.8 40.8 %all-to-all-start.2 = ((bf16[8,128,768]{2,1,0:T(8,128)(2,1)}), bf16[8,128,768]{2,1,0:T(8,128)(2,1)S(1)}, u32[]{:S(2)}, u32[]{:S(2)}) async-start(bf16[8,128,768]{2,1,0:T(8,128)(2,1)} %bitcast.94), calls=%async_computation.2 | async-start | bytes 3145728 | tf_op jit(solution)/shard_map/all_to_all | solution.py:1161
  269.4 258.2 %reduce-scatter.2.cloned.1.call-start = ((), (), s32[]{:S(2)}) async-start(), calls=%async_computation.8 | async-start | bytes 11796480 | tf_op jit(solution)/shard_map/reduce_scatter | solution.py:1229
  337.4 40.8 %all-to-all-start.3 = ((bf16[8,128,768]{2,1,0:T(8,128)(2,1)}), bf16[8,128,768]{2,1,0:T(8,128)(2,1)S(1)}, u32[]{:S(2)}, u32[]{:S(2)}) async-start(bf16[8,128,768]{2,1,0:T(8,128)(2,1)} %bitcast.28), calls=%async_computation.3 | async-start | bytes 3145728 | tf_op jit(solution)/shard_map/all_to_all | solution.py:1161
  396.7 13.3 %collective-permute-start.8 = (bf16[256,768]{1,0:T(8,128)(2,1)}, bf16[256,768]{1,0:T(8,128)(2,1)S(1)}, u32[]{:S(2)}, u32[]{:S(2)}) collective-permute-start(bf16[256,768]{1,0:T(8,128)(2,1)} %get-tuple-element.173), channel_id=1, source_target_pairs={{0,2},{2,4},{4,6},{6,7},{7,5},{5,3},{3,1},{1,0},{8,10},{10,12},{12... | collective-permute-start | bytes 1179656 | tf_op jit(solution)/shard_map/ppermute | solution.py:1069
  396.8 13.3 %collective-permute-start.9 = (bf16[256,768]{1,0:T(8,128)(2,1)}, bf16[256,768]{1,0:T(8,128)(2,1)S(1)}, u32[]{:S(2)}, u32[]{:S(2)}) collective-permute-start(bf16[256,768]{1,0:T(8,128)(2,1)} %get-tuple-element.174), channel_id=1, source_target_pairs={{0,1},{2,0},{4,2},{6,4},{7,6},{5,7},{3,5},{1,3},{8,9},{10,8},{12,1... | collective-permute-start | bytes 1179656 | tf_op jit(solution)/shard_map/ppermute | solution.py:1069
  414.5 18.1 %collective-permute-start.10 = (bf16[256,1536]{1,0:T(8,128)(2,1)}, bf16[256,1536]{1,0:T(8,128)(2,1)S(1)}, u32[]{:S(2)}, u32[]{:S(2)}) collective-permute-start(bf16[256,1536]{1,0:T(8,128)(2,1)} %get-tuple-element.190), channel_id=1, source_target_pairs={{0,2},{2,4},{4,6},{6,7},{7,5},{5,3},{3,1},{1,0},{8,10},{10,12},{12... | collective-permute-start | bytes 2359304 | tf_op jit(solution)/shard_map/ppermute | solution.py:1069
  415.2 20.7 %collective-permute-start.11 = (bf16[256,1536]{1,0:T(8,128)(2,1)}, bf16[256,1536]{1,0:T(8,128)(2,1)}, u32[]{:S(2)}, u32[]{:S(2)}) collective-permute-start(bf16[256,1536]{1,0:T(8,128)(2,1)} %get-tuple-element.191), channel_id=1, source_target_pairs={{0,1},{2,0},{4,2},{6,4},{7,6},{5,7},{3,5},{1,3},{8,9},{10,8},{12,1... | collective-permute-start | bytes 2359304 | tf_op jit(solution)/shard_map/ppermute | solution.py:1069
  419.7 10.9 %collective-permute-start.12 = (bf16[2,192,896]{2,1,0:T(8,128)(2,1)}, bf16[2,192,896]{2,1,0:T(8,128)(2,1)}, u32[]{:S(2)}, u32[]{:S(2)}) collective-permute-start(bf16[2,192,896]{2,1,0:T(8,128)(2,1)} %fusion.4), channel_id=1, source_target_pairs={{0,8},{8,0},{16,24},{24,16},{1,9},{9,1},{17,25},{25,17},{2,10},{10... | collective-permute-start | bytes 2064392 | tf_op jit(solution)/shard_map/ppermute | solution.py:1077
  438.7 19.2 %collective-permute-start.13 = (bf16[256,1536]{1,0:T(8,128)(2,1)}, bf16[256,1536]{1,0:T(8,128)(2,1)S(1)}, u32[]{:S(2)}, u32[]{:S(2)}) collective-permute-start(bf16[256,1536]{1,0:T(8,128)(2,1)} %get-tuple-element.207), channel_id=1, source_target_pairs={{0,2},{2,4},{4,6},{6,7},{7,5},{5,3},{3,1},{1,0},{8,10},{10,12},{12... | collective-permute-start | bytes 2359304 | tf_op jit(solution)/shard_map/ppermute | solution.py:1069
  441.9 18.3 %collective-permute-start.14 = (bf16[256,1536]{1,0:T(8,128)(2,1)}, bf16[256,1536]{1,0:T(8,128)(2,1)}, u32[]{:S(2)}, u32[]{:S(2)}) collective-permute-start(bf16[256,1536]{1,0:T(8,128)(2,1)} %get-tuple-element.208), channel_id=1, source_target_pairs={{0,1},{2,0},{4,2},{6,4},{7,6},{5,7},{3,5},{1,3},{8,9},{10,8},{12,1... | collective-permute-start | bytes 2359304 | tf_op jit(solution)/shard_map/ppermute | solution.py:1069
  444.1 11.3 %collective-permute-start.15 = (bf16[192,896]{1,0:T(8,128)(2,1)S(1)}, bf16[192,896]{1,0:T(8,128)(2,1)S(1)}, u32[]{:S(2)}, u32[]{:S(2)}) collective-permute-start(bf16[192,896]{1,0:T(8,128)(2,1)S(1)} %fusion.6), channel_id=1, source_target_pairs={{0,16},{16,0},{8,24},{24,8},{1,17},{17,1},{9,25},{25,9},{2,18},{18... | collective-permute-start | bytes 1032200 | tf_op jit(solution)/shard_map/ppermute | solution.py:1085
  455.4 24.1 %copy-start.19 = (bf16[192,896]{1,0:T(8,128)(2,1)}, bf16[192,896]{1,0:T(8,128)(2,1)S(1)}, u32[]{:S(2)}) copy-start(bf16[192,896]{1,0:T(8,128)(2,1)S(1)} %collective-permute-done.15) | copy-start | bytes 1032196
  463.0 24.1 %collective-permute-start.16 = (bf16[256,1536]{1,0:T(8,128)(2,1)}, bf16[256,1536]{1,0:T(8,128)(2,1)S(1)}, u32[]{:S(2)}, u32[]{:S(2)}) collective-permute-start(bf16[256,1536]{1,0:T(8,128)(2,1)} %get-tuple-element.228), channel_id=1, source_target_pairs={{0,2},{2,4},{4,6},{6,7},{7,5},{5,3},{3,1},{1,0},{8,10},{10,12},{12... | collective-permute-start | bytes 2359304 | tf_op jit(solution)/shard_map/ppermute | solution.py:1069
  465.3 21.7 %collective-permute-start.17 = (bf16[256,1536]{1,0:T(8,128)(2,1)}, bf16[256,1536]{1,0:T(8,128)(2,1)S(1)}, u32[]{:S(2)}, u32[]{:S(2)}) collective-permute-start(bf16[256,1536]{1,0:T(8,128)(2,1)} %get-tuple-element.229), channel_id=1, source_target_pairs={{0,1},{2,0},{4,2},{6,4},{7,6},{5,7},{3,5},{1,3},{8,9},{10,8},{12,1... | collective-permute-start | bytes 2359304 | tf_op jit(solution)/shard_map/ppermute | solution.py:1069
  501.8 4.6 collective-permute-start.18
  501.9 3.9 collective-permute-start.20
  506.0 9.1 %collective-permute-start.21 = (bf16[192,768]{1,0:T(8,128)(2,1)S(1)}, bf16[192,768]{1,0:T(8,128)(2,1)S(1)}, u32[]{:S(2)}, u32[]{:S(2)}) collective-permute-start(bf16[192,768]{1,0:T(8,128)(2,1)S(1)} %fusion.7), channel_id=1, source_target_pairs={{0,16},{16,0},{8,24},{24,8},{1,17},{17,1},{9,25},{25,9},{2,18},{18... | collective-permute-start | bytes 884744 | tf_op jit(solution)/shard_map/ppermute | solution.py:1085
  516.0 21.6 %all-to-all-start.4 = ((bf16[8,24,1664]{2,1,0:T(8,128)(2,1)}), bf16[8,24,1664]{2,1,0:T(8,128)(2,1)}, u32[]{:S(2)}, u32[]{:S(2)}) async-start(bf16[8,24,1664]{2,1,0:T(8,128)(2,1)} %fusion.1), calls=%async_computation.5 | async-start | bytes 1277952 | tf_op jit(solution)/shard_map/all_to_all | solution.py:1091
  522.0 14.4 %collective-permute-start.19 = (bf16[192,1536]{1,0:T(8,128)(2,1)}, bf16[192,1536]{1,0:T(8,128)(2,1)S(1)}, u32[]{:S(2)}, u32[]{:S(2)}) collective-permute-start(bf16[192,1536]{1,0:T(8,128)(2,1)} %fusion.5), channel_id=1, source_target_pairs={{0,16},{16,0},{8,24},{24,8},{1,17},{17,1},{9,25},{25,9},{2,18},{18... | collective-permute-start | bytes 1769480 | tf_op jit(solution)/shard_map/ppermute | solution.py:1085
  537.7 19.6 %all-to-all-start.5 = ((bf16[8,24,1536]{2,1,0:T(8,128)(2,1)}), bf16[8,24,1536]{2,1,0:T(8,128)(2,1)S(1)}, u32[]{:S(2)}, u32[]{:S(2)}) async-start(bf16[8,24,1536]{2,1,0:T(8,128)(2,1)} %bitcast.50), calls=%async_computation.6 | async-start | bytes 1179648 | tf_op jit(solution)/shard_map/all_to_all | solution.py:1091
  (31 other events, 195.6 us)
Sparse Core Ops, SparseCore 0:
  12.8 67.0 all-gather.3
  81.5 62.5 all-gather.5
  337.5 76.0 reduce-scatter.1
